TPU v7x, 512 devices: a whole 4x4x16 slice. The times are simulated.
512 devices in a mesh: lon: 32 (over z, core), lat: 16 (over y, x).
Axes of the slice: x: 4, y: 4, z: 16, core: 2. Of those that a mesh axis runs over, the one named last changes fastest.
Arguments:
- land_sea: int32 [2048, 7168], P('lat', 'lon'), may hold values from 0 to 1, as said below
- obs_cell: int32 [16, 32, 2048], P('lat', 'lon'), may hold values from 0 to 28671
- obs_value: float32 [16, 32, 2048], P('lat', 'lon'), may hold values from -12 to 12
- obs_weight: float32 [16, 32, 2048], P('lat', 'lon'), may hold values from 0.5 to 4
- intersection: int32 [16, 32], P('lat', 'lon'), may hold values from 1 to 16, as said below
- factors: float32 [160, 16, 16, 8192], P('lat', None, None, 'lon'), may hold values from -1 to 1, as said below
- coarse_inverse: float32 [8192, 8192], P(('lon', 'lat')), may hold values from -1 to 1, as said below
Outputs:
- solution: float32 [2048, 7168], P('lat', 'lon')
- residual: float32 [2048, 7168], P('lat', 'lon')
- preconditioned: float32 [2048, 7168], P('lat', 'lon')
Inputs may be any that keep to these rules, and one draw needn't show every extreme that they name: `land_sea`: 1 marks ocean and 0 land; the first and last rows of the grid are land. Some tile has intersection 16. `factors`: each block is lower triangular (zero where the third index exceeds the second) with a positive diagonal. `coarse_inverse`: symmetric and positive definite.
All inputs are finite; a program needn't handle non-finite values.
Results may differ from a plain program's by a relative error of at most 0.00012.
Values sent between devices are 32-bit elements; how exact they have to be, the bound alone decides.
No kernel may reach another device: no remote copies, remote signals or barrier semaphores. Data moves between devices by JAX's collectives and lax.ppermute only.
A program may use at most 64 MiB of HBM per device.

v0:
```python
import jax
import jax.numpy as jnp
from jax import lax
from jax.sharding import PartitionSpec as P

HW = 16
SUB = 4


DAMPING = 0.02


def with_halo(x, sides, width):
    for axis, dim in sides:
        size, length = (lax.axis_size(axis), x.shape[dim])
        up = [(i, (i + 1) % size) for i in range(size)]
        down = [(j, i) for i, j in up]
        last = lax.slice_in_dim(x, length - width, length, axis=dim)
        initial = lax.slice_in_dim(x, 0, width, axis=dim)
        before = lax.ppermute(last, axis, up)
        after = lax.ppermute(initial, axis, down)
        x = jnp.concatenate([before, x, after], axis=dim)
    return x


def with_faces(field):
    return with_halo(field, (("lon", 1), ("lat", 0)), 1)


def with_margin(field):
    return with_halo(field, (("lon", 1), ("lat", 0)), HW)


def fold_rows(back):
    length = back.shape[0] - 4 * HW
    inner = back[2 * HW : 2 * HW + length]
    head = jnp.pad(back[:HW], ((0, length - HW), (0, 0)))
    tail = jnp.pad(back[length + 3 * HW :], ((length - HW, 0), (0, 0)))
    return inner + head + tail


def fold_cols(back):
    length = back.shape[1] - 4 * HW
    inner = back[:, 2 * HW : 2 * HW + length]
    head = jnp.pad(back[:, :HW], ((0, 0), (0, length - HW)))
    tail = jnp.pad(back[:, length + 3 * HW :], ((0, 0), (length - HW, 0)))
    return inner + head + tail


def body(land_sea, obs_cell, obs_value, obs_weight, intersection, factors, coarse_inverse):
    ocean_mask = land_sea.astype(jnp.float32)
    tile_rows, tile_cols = land_sea.shape
    cells = obs_cell[0, 0]
    obs_diag = jax.ops.segment_sum(
        obs_weight[0, 0], cells, num_segments=tile_rows * tile_cols
    ).reshape(tile_rows, tile_cols)
    obs_load = jax.ops.segment_sum(
        obs_weight[0, 0] * obs_value[0, 0], cells, num_segments=tile_rows * tile_cols
    ).reshape(tile_rows, tile_cols)
    rhs = ocean_mask * obs_load
    ocean_pad = with_faces(ocean_mask)
    east = ocean_mask * ocean_pad[1:-1, 2:]
    west = ocean_mask * ocean_pad[1:-1, :-2]
    north = ocean_mask * ocean_pad[:-2, 1:-1]
    south = ocean_mask * ocean_pad[2:, 1:-1]
    total_conduct = east + west + north + south
    mask_wide = with_margin(ocean_mask)
    lat_index = lax.axis_index("lat")
    lat_count = lax.axis_size("lat")
    row_pos = jnp.arange(tile_rows + 2 * HW, dtype=jnp.int32)
    col_pos = jnp.arange(tile_cols + 2 * HW, dtype=jnp.int32)
    reach = intersection[0, 0]
    global_row = lat_index * tile_rows + row_pos - HW
    row_ok = (
        (row_pos >= HW - reach)
        & (row_pos < HW + tile_rows + reach)
        & (global_row >= 0)
        & (global_row < lat_count * tile_rows)
    )
    col_ok = (col_pos >= HW - reach) & (col_pos < HW + tile_cols + reach)
    weights = mask_wide * row_ok[:, None].astype(jnp.float32) * col_ok[None, :].astype(jnp.float32)
    block_count, block_size = (factors.shape[0], factors.shape[1])
    coarse_rows = coarse_inverse.shape[0]
    residual = rhs
    wide = with_margin(residual)
    source = (weights * wide).reshape(block_count, block_size, wide.shape[1])
    forward = jnp.einsum("kabx,kbx->kax", factors, source, precision=lax.Precision.HIGHEST)
    solved = jnp.einsum("kabx,kax->kbx", factors, forward, precision=lax.Precision.HIGHEST)
    contrib = weights * solved.reshape(wide.shape)
    back = with_halo(contrib, (("lon", 1), ("lat", 0)), HW)
    local = fold_cols(fold_rows(back))
    sums = jnp.sum(
        (ocean_mask * residual).reshape(SUB, tile_rows // SUB, SUB, tile_cols // SUB), axis=(1, 3)
    ).reshape(coarse_rows)
    answer = jnp.dot(
        coarse_inverse,
        lax.all_gather(sums, ("lon", "lat"), axis=0, tiled=True),
        precision=lax.Precision.HIGHEST,
        preferred_element_type=jnp.float32,
    )
    spread = jnp.broadcast_to(
        answer.reshape(SUB, 1, SUB, 1), (SUB, tile_rows // SUB, SUB, tile_cols // SUB)
    )
    precond = local + ocean_mask * spread.reshape(tile_rows, tile_cols)
    affinity = lax.psum(jnp.sum(residual * precond), ("lon", "lat"))
    padded = with_faces(precond)
    beside = (
        east * padded[1:-1, 2:]
        + west * padded[1:-1, :-2]
        + north * padded[:-2, 1:-1]
        + south * padded[2:, 1:-1]
    )
    coupling = total_conduct * precond - beside
    image = ocean_mask * ((obs_diag + DAMPING) * precond + coupling) + (1.0 - ocean_mask) * precond
    alpha = affinity / lax.psum(jnp.sum(precond * image), ("lon", "lat"))
    solution = alpha * precond
    residual = residual - alpha * image
    return (solution, residual, precond)


def solution(mesh):
    in_specs = (
        P("lat", "lon"),
        P("lat", "lon", None),
        P("lat", "lon", None),
        P("lat", "lon", None),
        P("lat", "lon"),
        P("lat", None, None, "lon"),
        P(("lon", "lat"), None),
    )
    out_specs = (P("lat", "lon"), P("lat", "lon"), P("lat", "lon"))
    return jax.shard_map(body, mesh=mesh, in_specs=in_specs, out_specs=out_specs, check_vma=False)
```

profile of v0, /device:TPU:1, one launch (start us, length us, event | category | flops | bytes accessed | tf_op | source)
XLA Modules:
  0.0 320.2 jit_solution(18353582769522902506)
XLA Ops:
  0.7 0.9 mul.100
  1.5 11.5 %scatter_custom_fusion = f32[28672]{0:T(1024)S(1)} fusion(s32[2048]{0:T(1024)} %bitcast.32, f32[2048]{0:T(1024)S(1)} %mul.100, f32[]{:T(128)} %constant.13.clone.1), kind=kCustom, calls=%fused_computation.56 | custom fusion | flops 2048 | bytes 115200 | tf_op jit(solution)/shard_map/scatter-add | solution.py:57
  13.2 1.0 copy.15
  14.2 0.7 convert_multiply_fusion
  14.9 0.7 fusion.39
  15.6 3.0 collective-permute-start.4
  18.6 3.8 %collective-permute-start.5 = (f32[128,16]{1,0:T(8,128)}, f32[128,16]{1,0:T(8,128)}, u32[]{:S(2)}, u32[]{:S(2)}) collective-permute-start(f32[128,16]{1,0:T(8,128)} %get-tuple-element.35), channel_id=1, source_target_pairs={{16,0},{32,16},{48,32},{64,48},{80,64},{96,80},{112,96},{128,112},... | collective-permute-start | bytes 24584 | tf_op jit(solution)/shard_map/ppermute | solution.py:21
  22.4 0.7 fusion.38
  23.2 3.6 %collective-permute-start.1 = (f32[128,16]{1,0:T(8,128)}, f32[128,16]{1,0:T(8,128)}, u32[]{:S(2)}, u32[]{:S(2)}) collective-permute-start(f32[128,16]{1,0:T(8,128)} %get-tuple-element.33), channel_id=1, source_target_pairs={{16,0},{32,16},{48,32},{64,48},{80,64},{96,80},{112,96},{128,112},... | collective-permute-start | bytes 24584 | tf_op jit(solution)/shard_map/ppermute | solution.py:21
  26.7 0.7 fusion.36
  27.5 3.0 collective-permute-start.12
  31.1 0.6 and_convert_fusion.1
  31.7 1.8 reshape.75
  33.5 1.1 reduce_sum.27
  34.6 0.6 reshape.96
  35.2 0.6 broadcast.83
  35.8 1.4 dynamic-update-slice
  37.2 101.8 %all-reduce.3 = f32[8192]{0:T(1024)} all-reduce(f32[8192]{0:T(1024)} %dynamic-update-slice), channel_id=1, replica_groups=mesh['lon'=32,'lat'=16] {'lon','lat'}, use_global_device_ids=true, to_apply=%add.3 | all-reduce | flops 8192 | bytes 65536
  139.1 2.5 collective-permute-start.13
  141.6 0.8 pad_maximum_fusion.23
  142.4 1.9 collective-permute-start.6
  144.3 6.7 %collective-permute-start.7 = (f32[16,256]{1,0:T(8,128)S(1)}, f32[16,256]{1,0:T(8,128)S(1)}, u32[]{:S(2)}, u32[]{:S(2)}) collective-permute-start(f32[16,256]{1,0:T(8,128)S(1)} %get-tuple-element.25), channel_id=1, source_target_pairs={{1,0},{2,1},{3,2},{4,3},{5,4},{6,5},{7,6},{8,7},{9,8},{10,9},{11,1... | collective-permute-start | bytes 49160 | tf_op jit(solution)/shard_map/ppermute | solution.py:21
  151.0 0.8 pad_maximum_fusion.26
  151.9 1.9 collective-permute-start.2
  153.8 6.7 %collective-permute-start.3 = (f32[16,256]{1,0:T(8,128)S(1)}, f32[16,256]{1,0:T(8,128)S(1)}, u32[]{:S(2)}, u32[]{:S(2)}) collective-permute-start(f32[16,256]{1,0:T(8,128)S(1)} %get-tuple-element.23), channel_id=1, source_target_pairs={{1,0},{2,1},{3,2},{4,3},{5,4},{6,5},{7,6},{8,7},{9,8},{10,9},{11,1... | collective-permute-start | bytes 49160 | tf_op jit(solution)/shard_map/ppermute | solution.py:21
  160.5 1.0 pad_maximum_fusion.2
  161.5 1.0 pad_maximum_fusion.1
  162.6 0.7 multiply_reduce_fusion.1
  163.3 0.5 multiply_reduce_fusion
  163.9 1.0 bitcast_multiply_fusion
  165.0 1.5 collective-permute-start.8
  166.5 0.7 convolution_bitcast_fusion
  168.0 2.4 collective-permute-done.9
  170.5 1.9 collective-permute-start.10
  172.4 7.2 %collective-permute-start.11 = (f32[16,288]{1,0:T(8,128)S(1)}, f32[16,288]{1,0:T(8,128)S(1)}, u32[]{:S(2)}, u32[]{:S(2)}) collective-permute-start(f32[16,288]{1,0:T(8,128)S(1)} %get-tuple-element.17), channel_id=1, source_target_pairs={{1,0},{2,1},{3,2},{4,3},{5,4},{6,5},{7,6},{8,7},{9,8},{10,9},{11,1... | collective-permute-start | bytes 55304 | tf_op jit(solution)/shard_map/ppermute | solution.py:21
  179.8 0.8 collective-permute-done.11
  181.4 1.3 collective-permute-start.17
  182.7 0.8 pad_maximum_fusion.32
  183.5 1.9 collective-permute-start.14
  185.4 7.4 %collective-permute-start.15 = (f32[1,226]{1,0:T(1,128)S(1)}, f32[1,226]{1,0:T(1,128)S(1)}, u32[]{:S(2)}, u32[]{:S(2)}) collective-permute-start(f32[1,226]{1,0:T(1,128)S(1)} %get-tuple-element.19), channel_id=1, source_target_pairs={{1,0},{2,1},{3,2},{4,3},{5,4},{6,5},{7,6},{8,7},{9,8},{10,9},{11,1... | collective-permute-start | bytes 2720 | tf_op jit(solution)/shard_map/ppermute | solution.py:21
  193.0 1.9 collective-permute-start.18
  194.9 6.7 %collective-permute-start.19 = (f32[1,226]{1,0:T(1,128)S(1)}, f32[1,226]{1,0:T(1,128)S(1)}, u32[]{:S(2)}, u32[]{:S(2)}) collective-permute-start(f32[1,226]{1,0:T(1,128)S(1)} %get-tuple-element.21), channel_id=1, source_target_pairs={{1,0},{2,1},{3,2},{4,3},{5,4},{6,5},{7,6},{8,7},{9,8},{10,9},{11,1... | collective-permute-start | bytes 2720 | tf_op jit(solution)/shard_map/ppermute | solution.py:21
  201.6 11.4 %scatter_custom_fusion.1 = f32[28672]{0:T(1024)S(1)} fusion(s32[2048]{0:T(1024)} %bitcast.33, f32[2048]{0:T(1024)} %bitcast.31, f32[]{:T(128)} %constant.35.clone.1), kind=kCustom, calls=%fused_computation.54 | custom fusion | flops 2048 | bytes 115200 | tf_op jit(solution)/shard_map/scatter-add | solution.py:54
  213.1 0.7 copy.18
  213.9 2.0 multiply_reduce_fusion.2
  215.9 101.4 %all-reduce.4 = (f32[]{:T(128)}, f32[]{:T(128)}) all-reduce(f32[]{:T(128)} %get-tuple-element.10, f32[]{:T(128)} %get-tuple-element.9), channel_id=1, replica_groups=mesh['lon'=32,'lat'=16] {'lon','lat'}, use_global_device_ids=true, to_apply=%region_3.4 | all-reduce | flops 2 | bytes 16 | tf_op jit(solution)/shard_map/psum | solution.py:105
  318.7 0.7 copy.16
  319.4 0.7 copy.17
  (49 shorter events, 2.3 us)
Async XLA Ops:
  0.6 165.9 %copy-start = (f32[16,8192]{1,0:T(8,128)S(1)}, f32[16,8192]{1,0:T(8,128)}, u32[]{:S(2)}) copy-start(f32[16,8192]{1,0:T(8,128)} %param.13) | copy-start | bytes 1572868
  0.6 162.0 %copy-start.1 = (f32[10,16,16,256]{3,2,1,0:T(8,128)S(1)}, f32[10,16,16,256]{3,2,1,0:T(8,128)}, u32[]{:S(2)}) copy-start(f32[10,16,16,256]{3,2,1,0:T(8,128)} %param.12) | copy-start | bytes 7864324
  15.6 123.5 %collective-permute-start.4 = (f32[128,16]{1,0:T(8,128)}, f32[128,16]{1,0:T(8,128)}, u32[]{:S(2)}, u32[]{:S(2)}) collective-permute-start(f32[128,16]{1,0:T(8,128)} %get-tuple-element.34), channel_id=1, source_target_pairs={{0,16},{16,32},{32,48},{48,64},{64,80},{80,96},{96,112},{112,128},... | collective-permute-start | bytes 24584 | tf_op jit(solution)/shard_map/ppermute | solution.py:20
  18.6 123.0 %collective-permute-start.5 = (f32[128,16]{1,0:T(8,128)}, f32[128,16]{1,0:T(8,128)}, u32[]{:S(2)}, u32[]{:S(2)}) collective-permute-start(f32[128,16]{1,0:T(8,128)} %get-tuple-element.35), channel_id=1, source_target_pairs={{16,0},{32,16},{48,32},{64,48},{80,64},{96,80},{112,96},{128,112},... | collective-permute-start | bytes 24584 | tf_op jit(solution)/shard_map/ppermute | solution.py:21
  23.1 121.2 %collective-permute-start = (f32[128,16]{1,0:T(8,128)}, f32[128,16]{1,0:T(8,128)}, u32[]{:S(2)}, u32[]{:S(2)}) collective-permute-start(f32[128,16]{1,0:T(8,128)} %get-tuple-element.32), channel_id=1, source_target_pairs={{0,16},{16,32},{32,48},{48,64},{64,80},{80,96},{96,112},{112,128},... | collective-permute-start | bytes 24584 | tf_op jit(solution)/shard_map/ppermute | solution.py:20
  23.2 127.9 %collective-permute-start.1 = (f32[128,16]{1,0:T(8,128)}, f32[128,16]{1,0:T(8,128)}, u32[]{:S(2)}, u32[]{:S(2)}) collective-permute-start(f32[128,16]{1,0:T(8,128)} %get-tuple-element.33), channel_id=1, source_target_pairs={{16,0},{32,16},{48,32},{64,48},{80,64},{96,80},{112,96},{128,112},... | collective-permute-start | bytes 24584 | tf_op jit(solution)/shard_map/ppermute | solution.py:21
  27.5 155.3 %collective-permute-start.12 = (f32[128,1]{1,0:T(8,128)}, f32[128,1]{1,0:T(8,128)}, u32[]{:S(2)}, u32[]{:S(2)}) collective-permute-start(f32[128,1]{1,0:T(8,128)} %get-tuple-element.29), channel_id=1, source_target_pairs={{16,0},{32,16},{48,32},{64,48},{80,64},{96,80},{112,96},{128,112},... | collective-permute-start | bytes 1544 | tf_op jit(solution)/shard_map/ppermute | solution.py:21
  139.1 43.6 %collective-permute-start.13 = (f32[128,1]{1,0:T(8,128)}, f32[128,1]{1,0:T(8,128)}, u32[]{:S(2)}, u32[]{:S(2)}) collective-permute-start(f32[128,1]{1,0:T(8,128)} %get-tuple-element.28), channel_id=1, source_target_pairs={{0,16},{16,32},{32,48},{48,64},{64,80},{80,96},{96,112},{112,128},... | collective-permute-start | bytes 1544 | tf_op jit(solution)/shard_map/ppermute | solution.py:20
  142.4 11.4 %collective-permute-start.6 = (f32[16,256]{1,0:T(8,128)S(1)}, f32[16,256]{1,0:T(8,128)S(1)}, u32[]{:S(2)}, u32[]{:S(2)}) collective-permute-start(f32[16,256]{1,0:T(8,128)S(1)} %get-tuple-element.24), channel_id=1, source_target_pairs={{0,1},{1,2},{2,3},{3,4},{4,5},{5,6},{6,7},{7,8},{8,9},{9,10},{10,1... | collective-permute-start | bytes 49160 | tf_op jit(solution)/shard_map/ppermute | solution.py:20
  144.3 16.2 %collective-permute-start.7 = (f32[16,256]{1,0:T(8,128)S(1)}, f32[16,256]{1,0:T(8,128)S(1)}, u32[]{:S(2)}, u32[]{:S(2)}) collective-permute-start(f32[16,256]{1,0:T(8,128)S(1)} %get-tuple-element.25), channel_id=1, source_target_pairs={{1,0},{2,1},{3,2},{4,3},{5,4},{6,5},{7,6},{8,7},{9,8},{10,9},{11,1... | collective-permute-start | bytes 49160 | tf_op jit(solution)/shard_map/ppermute | solution.py:21
  151.9 9.6 %collective-permute-start.2 = (f32[16,256]{1,0:T(8,128)S(1)}, f32[16,256]{1,0:T(8,128)S(1)}, u32[]{:S(2)}, u32[]{:S(2)}) collective-permute-start(f32[16,256]{1,0:T(8,128)S(1)} %get-tuple-element.22), channel_id=1, source_target_pairs={{0,1},{1,2},{2,3},{3,4},{4,5},{5,6},{6,7},{7,8},{8,9},{9,10},{10,1... | collective-permute-start | bytes 49160 | tf_op jit(solution)/shard_map/ppermute | solution.py:20
  153.8 7.7 %collective-permute-start.3 = (f32[16,256]{1,0:T(8,128)S(1)}, f32[16,256]{1,0:T(8,128)S(1)}, u32[]{:S(2)}, u32[]{:S(2)}) collective-permute-start(f32[16,256]{1,0:T(8,128)S(1)} %get-tuple-element.23), channel_id=1, source_target_pairs={{1,0},{2,1},{3,2},{4,3},{5,4},{6,5},{7,6},{8,7},{9,8},{10,9},{11,1... | collective-permute-start | bytes 49160 | tf_op jit(solution)/shard_map/ppermute | solution.py:21
  162.6 1.2 copy-start.3
  163.3 3.2 %copy-start.2 = (f32[8192]{0:T(1024)S(1)}, f32[8192]{0:T(1024)}, u32[]{:S(2)}) copy-start(f32[8192]{0:T(1024)} %all-reduce.3) | copy-start | bytes 98308
  163.3 17.4 %copy-start.4 = (pred[224]{0:T(512)(128)(4,1)S(1)}, pred[224]{0:T(512)(128)(4,1)}, u32[]{:S(2)}) copy-start(pred[224]{0:T(512)(128)(4,1)} %constant.34.clone.1) | copy-start | bytes 676
  165.0 3.0 collective-permute-start.8
  166.5 3.9 %collective-permute-start.9 = (f32[160,16]{1,0:T(8,128)S(1)}, f32[160,16]{1,0:T(8,128)S(1)}, u32[]{:S(2)}, u32[]{:S(2)}) collective-permute-start(f32[160,16]{1,0:T(8,128)S(1)} %get-tuple-element.27), channel_id=1, source_target_pairs={{16,0},{32,16},{48,32},{64,48},{80,64},{96,80},{112,96},{128,112},... | collective-permute-start | bytes 30728 | tf_op jit(solution)/shard_map/ppermute | solution.py:21
  170.5 9.3 %collective-permute-start.10 = (f32[16,288]{1,0:T(8,128)S(1)}, f32[16,288]{1,0:T(8,128)S(1)}, u32[]{:S(2)}, u32[]{:S(2)}) collective-permute-start(f32[16,288]{1,0:T(8,128)S(1)} %get-tuple-element.16), channel_id=1, source_target_pairs={{0,1},{1,2},{2,3},{3,4},{4,5},{5,6},{6,7},{7,8},{8,9},{9,10},{10,1... | collective-permute-start | bytes 55304 | tf_op jit(solution)/shard_map/ppermute | solution.py:20
  172.4 8.2 %collective-permute-start.11 = (f32[16,288]{1,0:T(8,128)S(1)}, f32[16,288]{1,0:T(8,128)S(1)}, u32[]{:S(2)}, u32[]{:S(2)}) collective-permute-start(f32[16,288]{1,0:T(8,128)S(1)} %get-tuple-element.17), channel_id=1, source_target_pairs={{1,0},{2,1},{3,2},{4,3},{5,4},{6,5},{7,6},{8,7},{9,8},{10,9},{11,1... | collective-permute-start | bytes 55304 | tf_op jit(solution)/shard_map/ppermute | solution.py:21
  181.0 11.9 %collective-permute-start.16 = (f32[128,1]{1,0:T(8,128)S(1)}, f32[128,1]{1,0:T(8,128)S(1)}, u32[]{:S(2)}, u32[]{:S(2)}) collective-permute-start(f32[128,1]{1,0:T(8,128)S(1)} %get-tuple-element.31), channel_id=1, source_target_pairs={{16,0},{32,16},{48,32},{64,48},{80,64},{96,80},{112,96},{128,112},... | collective-permute-start | bytes 1544 | tf_op jit(solution)/shard_map/ppermute | solution.py:21
  181.4 11.5 %collective-permute-start.17 = (f32[128,1]{1,0:T(8,128)S(1)}, f32[128,1]{1,0:T(8,128)S(1)}, u32[]{:S(2)}, u32[]{:S(2)}) collective-permute-start(f32[128,1]{1,0:T(8,128)S(1)} %get-tuple-element.30), channel_id=1, source_target_pairs={{0,16},{16,32},{32,48},{48,64},{64,80},{80,96},{96,112},{112,128},... | collective-permute-start | bytes 1544 | tf_op jit(solution)/shard_map/ppermute | solution.py:20
  183.5 30.3 %collective-permute-start.14 = (f32[1,226]{1,0:T(1,128)S(1)}, f32[1,226]{1,0:T(1,128)S(1)}, u32[]{:S(2)}, u32[]{:S(2)}) collective-permute-start(f32[1,226]{1,0:T(1,128)S(1)} %get-tuple-element.18), channel_id=1, source_target_pairs={{0,1},{1,2},{2,3},{3,4},{4,5},{5,6},{6,7},{7,8},{8,9},{9,10},{10,1... | collective-permute-start | bytes 2720 | tf_op jit(solution)/shard_map/ppermute | solution.py:20
  185.4 28.4 %collective-permute-start.15 = (f32[1,226]{1,0:T(1,128)S(1)}, f32[1,226]{1,0:T(1,128)S(1)}, u32[]{:S(2)}, u32[]{:S(2)}) collective-permute-start(f32[1,226]{1,0:T(1,128)S(1)} %get-tuple-element.19), channel_id=1, source_target_pairs={{1,0},{2,1},{3,2},{4,3},{5,4},{6,5},{7,6},{8,7},{9,8},{10,9},{11,1... | collective-permute-start | bytes 2720 | tf_op jit(solution)/shard_map/ppermute | solution.py:21
  193.0 20.9 %collective-permute-start.18 = (f32[1,226]{1,0:T(1,128)S(1)}, f32[1,226]{1,0:T(1,128)S(1)}, u32[]{:S(2)}, u32[]{:S(2)}) collective-permute-start(f32[1,226]{1,0:T(1,128)S(1)} %get-tuple-element.20), channel_id=1, source_target_pairs={{0,1},{1,2},{2,3},{3,4},{4,5},{5,6},{6,7},{7,8},{8,9},{9,10},{10,1... | collective-permute-start | bytes 2720 | tf_op jit(solution)/shard_map/ppermute | solution.py:20
  194.9 19.0 %collective-permute-start.19 = (f32[1,226]{1,0:T(1,128)S(1)}, f32[1,226]{1,0:T(1,128)S(1)}, u32[]{:S(2)}, u32[]{:S(2)}) collective-permute-start(f32[1,226]{1,0:T(1,128)S(1)} %get-tuple-element.21), channel_id=1, source_target_pairs={{1,0},{2,1},{3,2},{4,3},{5,4},{6,5},{7,6},{8,7},{9,8},{10,9},{11,1... | collective-permute-start | bytes 2720 | tf_op jit(solution)/shard_map/ppermute | solution.py:21
where the time goes:
time: 321 us; the launch traced here: 320 us
  blocking collectives  203 us (63%)
  starting transfers between devices  63.5 us (20%)
  other arithmetic  35.4 us (11%)
  local copies, waits for them, and re-layouts  10.7 us (3%)
  waiting for transfers between devices  3.64 us (1%)
    unnamed x1, blocking collectives  102 us
    psum x1, blocking collectives, body(): affinity = lax.psum(jnp.sum(residual * precond), ('lon', 'lat'))  101 us
    ppermute x10, starting transfers between devices, with_halo(): after = lax.ppermute(initial, axis, down)  45.5 us
    ppermute x10, starting transfers between devices, with_halo(): before = lax.ppermute(last, axis, up)  17.9 us
    scatter-add x1, other arithmetic, body(): jax.ops.segment_sum(obs_weight[0, 0] * obs_value[0, 0], cells, num_segmen...  11.5 us
    scatter-add x1, other arithmetic, body(): jax.ops.segment_sum(obs_weight[0, 0], cells, num_segments=tile_rows * til...  11.4 us
  transfers between devices with their start and end apart: 20, of which 3 were waited for; matrix products, arithmetic and copies ran while one was open for 9% of the time, Pallas kernels for 0%

commit v1 on v0

v1 whole, which is shorter than its diff:
```python
import jax
import jax.numpy as jnp
from jax import lax
from jax.experimental import pallas as pl
from jax.experimental.pallas import tpu as pltpu
from jax.sharding import PartitionSpec as P

F32 = jnp.float32
DAMPING = 0.02
ROWS, COLS, HW, EXT = 128, 224, 16, 256
BLK = 8
TRI = 192
QTR = TRI // 4
OBS = 2048

VM = pl.BlockSpec(memory_space=pltpu.VMEM)
SM = pl.BlockSpec(memory_space=pltpu.SMEM)


def iota(shape, dim):
    return lax.broadcasted_iota(jnp.int32, shape, dim)


def call(kernel, outs, ins, smem=0, scratch=(), flops=100000):
    size = sum(4 * x.size for x in ins)
    return pl.pallas_call(
        kernel,
        out_shape=[jax.ShapeDtypeStruct(s, F32) for s in outs],
        in_specs=[SM] * smem + [VM] * (len(ins) - smem),
        out_specs=[VM] * len(outs),
        scratch_shapes=list(scratch),
        cost_estimate=pl.CostEstimate(flops=flops, bytes_accessed=size, transcendentals=0),
    )(*ins)


def tri_rows(get):
    return jnp.concatenate([get(p, 8) for p in range(8)] + [get(p, 16) for p in range(8, 16)], axis=0)


def pack_kernel(reach_ref, fac_ref, east_ref, west_ref, south_ref, north_ref):
    reach = reach_ref[0, 0]
    lane = iota((TRI, 128), 1)
    row = iota((TRI, 128), 0)
    q = jnp.where(row < 64, row & 7, row & 15)
    first_rows = q >= HW - reach
    last_rows = q < reach
    east = jnp.zeros((TRI, 128), F32)
    west = jnp.zeros((TRI, 128), F32)
    for k in range(BLK):
        own = (lane >= k * 16) & (lane < k * 16 + 16)
        hi = tri_rows(lambda p, n: fac_ref[k + 1, p, 0:n, 128:256])
        lo = tri_rows(lambda p, n: fac_ref[k + 1, p, 0:n, 0:128])
        east = jnp.where(own & (lane - k * 16 < reach), pltpu.roll(hi, (k * 16 - 112) % 128, 1), east)
        west = jnp.where(own & (lane - k * 16 >= HW - reach), pltpu.roll(lo, k * 16, 1) if k else lo, west)
    east_ref[0:TRI, :] = east
    west_ref[0:TRI, :] = west
    top_lo = tri_rows(lambda p, n: fac_ref[0, p, 0:n, 0:128])
    top_hi = tri_rows(lambda p, n: fac_ref[0, p, 0:n, 128:256])
    end_lo = tri_rows(lambda p, n: fac_ref[BLK + 1, p, 0:n, 0:128])
    end_hi = tri_rows(lambda p, n: fac_ref[BLK + 1, p, 0:n, 128:256])
    top_lo = jnp.where(first_rows, top_lo, 0.0)
    top_hi = jnp.where(first_rows, top_hi, 0.0)
    end_lo = jnp.where(last_rows, end_lo, 0.0)
    end_hi = jnp.where(last_rows, end_hi, 0.0)
    east_corner = jnp.where(
        lane < 16, pltpu.roll(top_hi, 16, 1), jnp.where(lane < 32, pltpu.roll(end_hi, 32, 1), 0.0)
    )
    east_corner = jnp.where((lane & 15) < reach, east_corner, 0.0)
    west_corner = jnp.where(lane < 16, top_lo, jnp.where(lane < 32, pltpu.roll(end_lo, 16, 1), 0.0))
    west_corner = jnp.where((lane & 15) >= HW - reach, west_corner, 0.0)
    for ref, corner in ((east_ref, east_corner), (west_ref, west_corner)):
        packed = corner[0:QTR]
        for g in range(1, 4):
            packed = packed + pltpu.roll(corner[g * QTR : (g + 1) * QTR], 32 * g, 1)
        ref[TRI : TRI + QTR, :] = packed
    north_ref[:, 0:128] = jnp.where(lane >= 16, top_lo, 0.0)
    north_ref[:, 128:256] = jnp.where(lane < 112, top_hi, 0.0)
    south_ref[:, 0:128] = jnp.where(lane >= 16, end_lo, 0.0)
    south_ref[:, 128:256] = jnp.where(lane < 112, end_hi, 0.0)


def pieces(x):
    hi = x.astype(jnp.bfloat16).astype(F32)
    rest = x - hi
    mid = rest.astype(jnp.bfloat16).astype(F32)
    low = (rest - mid).astype(jnp.bfloat16).astype(F32)
    return hi, mid, low


def load_kernel(n_lat, lat_ref, cell_ref, value_ref, weight_ref, land_ref, diag_ref, rhs_ref, ocean_ref, send_ref,
                wide, left, right):
    me = lat_ref[0]
    wide[...] = jnp.zeros((ROWS, EXT), F32)
    wide[:, 0:COLS] = land_ref[...].astype(F32)
    ocean = pltpu.roll(wide[...], HW, 1)
    ocean_ref[...] = ocean
    step = 512
    for start in range(0, OBS, step):
        cut = slice(start, start + step)
        cell = cell_ref[:, cut]
        at_row = ((cell >> 5) * 9363) >> 16
        at_col = cell - at_row * COLS + HW
        weight = weight_ref[:, cut]
        parts = pieces(weight) + pieces(weight * value_ref[:, cut])
        hit = iota((ROWS, step), 0) == at_row
        for n, part in enumerate(parts):
            left[n * ROWS : (n + 1) * ROWS, cut] = jnp.where(hit, part, 0.0).astype(jnp.bfloat16)
        right[:, cut] = jnp.where(iota((EXT, step), 0) == at_col, 1.0, 0.0).astype(jnp.bfloat16)
    sums = lax.dot_general(left[...], right[...], (((1,), (1,)), ((), ())), preferred_element_type=F32)
    part = [sums[n * ROWS : (n + 1) * ROWS] for n in range(6)]
    diag_ref[...] = part[0] + (part[1] + part[2])
    rhs = ocean * (part[3] + (part[4] + part[5]))
    rhs_ref[...] = rhs
    sub = iota((16, EXT), 0)
    lane = iota((16, EXT), 1)
    pooled = jnp.zeros((16, EXT), F32)
    for s in range(4):
        band = jnp.sum(rhs[s * 32 : s * 32 + 32], axis=0, keepdims=True)
        pooled = jnp.where((sub >> 2) == s, band, pooled)
    first = HW + (sub & 3) * 56
    pooled = jnp.where((lane >= first) & (lane < first + 56), pooled, 0.0)
    coarse = jnp.sum(pooled, axis=1, keepdims=True)
    n_row = n_lat * 16 // 128
    placed = jnp.sum(jnp.where(lane == sub + 16 * me, coarse, 0.0), axis=0, keepdims=True)
    for p in range(n_lat):
        for r in range(n_row):
            send_ref[p, r : r + 1, :] = placed[:, r * 128 : (r + 1) * 128]
        face = jnp.where(p < me, ocean[0:1], ocean[ROWS - 1 : ROWS])
        send_ref[p, n_row : n_row + 1, :] = face[:, 0:128]
        send_ref[p, n_row + 1 : n_row + 2, :] = face[:, 128:256]


def merge_kernel(n_lon, n_row, from_w_ref, from_e_ref, south_ref, north_ref, got_ref, to_s_ref, to_n_ref, send_ref):
    lane = iota((QTR, 128), 1)
    for g in range(4):
        rows = slice(g * QTR, (g + 1) * QTR)
        packed_w = from_w_ref[TRI : TRI + QTR, :]
        packed_e = from_e_ref[TRI : TRI + QTR, :]
        for ref, base, shift in ((to_n_ref, north_ref, 0), (to_s_ref, south_ref, 16)):
            left = pltpu.roll(packed_w, (-32 * g - shift) % 128, 1) if g or shift else packed_w
            right = pltpu.roll(packed_e, (112 - 32 * g - shift) % 128, 1)
            ref[rows, 0:128] = jnp.where(lane < 16, left, base[rows, 0:128])
            ref[rows, 128:256] = jnp.where(lane >= 112, right, base[rows, 128:256])
    total = jnp.sum(got_ref[:, 0:n_row, :], axis=0)
    for p in range(n_lon):
        send_ref[p] = total


def apply_block(u, get):
    low = u[0:8]
    g_low = jnp.zeros_like(low)
    g_high = jnp.zeros_like(low)
    for p in range(8):
        line = get(p, 8)
        f = jnp.sum(line * low, axis=0, keepdims=True)
        g_low = g_low + line * f
    for p in range(8, 16):
        line = get(p, 16)
        f = jnp.sum(line * u, axis=0, keepdims=True)
        g = line * f
        g_low = g_low + g[0:8]
        g_high = g_high + g[8:16]
    return jnp.concatenate([g_low, g_high], axis=0)


def tri_get(ref):
    def get(p, n):
        start = p * 8 if p < 8 else 64 + (p - 8) * 16
        return ref[start : start + n, :]

    return get


def solve_kernel(n_lon, n_row, fac_ref, rhs_ref, ocean_ref, from_w_ref, from_e_ref, from_n_ref, from_s_ref,
                 inverse_ref, coarse_ref, z_ref, face_w_ref, face_e_ref, acc):
    lane = iota((16, 128), 1)
    wide_lane = iota((16, EXT), 1)
    u_w = jnp.zeros((16, 128), F32)
    u_e = jnp.zeros((16, 128), F32)
    for k in range(BLK):
        rows = slice(k * 16, k * 16 + 16)
        u = rhs_ref[rows, :]
        acc[rows, :] = apply_block(u, lambda p, n: fac_ref[k + 1, p, 0:n, :])
        own = (lane >= k * 16) & (lane < k * 16 + 16)
        u_w = jnp.where(own, pltpu.roll(u[:, 0:128], (k * 16 - 16) % 128, 1), u_w)
        u_e = jnp.where(own, pltpu.roll(u[:, 128:256], (k * 16 - 96) % 128, 1), u_e)
    g_w = apply_block(u_w, tri_get(from_w_ref))
    g_e = apply_block(u_e, tri_get(from_e_ref))
    for k in range(BLK):
        rows = slice(k * 16, k * 16 + 16)
        in_w = (lane >= 16) & (lane < 32)
        in_e = (lane >= 96) & (lane < 112)
        acc[rows, 0:128] += jnp.where(in_w, pltpu.roll(g_w, (16 - k * 16) % 128, 1), 0.0)
        acc[rows, 128:256] += jnp.where(in_e, pltpu.roll(g_e, (96 - k * 16) % 128, 1), 0.0)
    for rows, ref in ((slice(0, 16), from_n_ref), (slice(ROWS - 16, ROWS), from_s_ref)):
        u = rhs_ref[rows, :]
        u = jnp.where(
            wide_lane < 16, pltpu.roll(u, EXT - 16, 1), jnp.where(wide_lane >= 240, pltpu.roll(u, 16, 1), u)
        )
        g = apply_block(u, tri_get(ref))
        core = jnp.where((wide_lane >= 16) & (wide_lane < 240), g, 0.0)
        from_left = jnp.where((wide_lane >= 16) & (wide_lane < 32), pltpu.roll(g, 16, 1), 0.0)
        from_right = jnp.where((wide_lane >= 224) & (wide_lane < 240), pltpu.roll(g, EXT - 16, 1), 0.0)
        acc[rows, :] += core + from_left + from_right
    dot = jnp.zeros((16, 128), F32)
    for j in range(n_lon):
        for r in range(n_row):
            at = (j * n_row + r) * 128
            dot = dot + inverse_ref[:, at : at + 128] * coarse_ref[j, r : r + 1, :]
    answer = jnp.sum(dot, axis=1, keepdims=True)
    sub = iota((16, EXT), 0)
    first = HW + (sub & 3) * 56
    spread = jnp.where((wide_lane >= first) & (wide_lane < first + 56), answer, 0.0)
    for s in range(4):
        rows = slice(s * 32, s * 32 + 32)
        band = jnp.sum(jnp.where((sub >> 2) == s, spread, 0.0), axis=0, keepdims=True)
        z_ref[rows, :] = ocean_ref[rows, :] * (acc[rows, :] + band)
    z_left = jnp.transpose(z_ref[:, 0:128])
    z_right = jnp.transpose(z_ref[:, 128:256])
    o_left = jnp.transpose(ocean_ref[:, 0:128])
    o_right = jnp.transpose(ocean_ref[:, 128:256])
    face_w_ref[0:1, :] = z_left[16:17]
    face_w_ref[1:2, :] = o_left[16:17]
    face_e_ref[0:1, :] = z_right[111:112]
    face_e_ref[1:2, :] = o_right[111:112]


def image_kernel(n_lat, n_row, lat_ref, z_ref, ocean_ref, diag_ref, rhs_ref, got_ref, from_w_ref, from_e_ref,
                 image_ref, send_ref):
    me = lat_ref[0]
    lane = iota((ROWS, EXT), 1)
    row = iota((ROWS, EXT), 0)
    z = z_ref[...]
    ocean = ocean_ref[...]

    def column(ref, n):
        col = jnp.transpose(jnp.broadcast_to(ref[n : n + 1, :], (128, 128)))
        return jnp.concatenate([col, col], axis=1)

    def padded(x, n):
        return jnp.where(lane == 15, column(from_w_ref, n), jnp.where(lane == 240, column(from_e_ref, n), x))

    def sides(x):
        return pltpu.roll(x, 1, 1) + pltpu.roll(x, EXT - 1, 1)

    def line(index, inside):
        face = jnp.concatenate([got_ref[index, n_row : n_row + 1, :], got_ref[index, n_row + 1 : n_row + 2, :]], axis=1)
        return jnp.where(inside, face, 0.0)

    o_north = line(jnp.maximum(me - 1, 0), me > 0)
    o_south = line(jnp.minimum(me + 1, n_lat - 1), me < n_lat - 1)

    def rows(x, north, south):
        return jnp.where(row == 0, north, pltpu.roll(x, 1, 0)) + jnp.where(
            row == ROWS - 1, south, pltpu.roll(x, ROWS - 1, 0)
        )

    total = sides(padded(ocean, 1)) + rows(ocean, o_north, o_south)
    beside = sides(padded(z, 0)) + rows(z, 0.0, 0.0)
    image = ocean * ((diag_ref[...] + DAMPING) * z + (total * z - beside)) + (1.0 - ocean) * z
    image_ref[...] = image
    affinity = jnp.sum(jnp.sum(rhs_ref[...] * z, axis=0, keepdims=True), axis=1, keepdims=True)
    energy = jnp.sum(jnp.sum(z * image, axis=0, keepdims=True), axis=1, keepdims=True)
    small = iota((1, 128), 1)
    scalars = jnp.where(small == 0, affinity, jnp.where(small == 1, energy, 0.0))
    for p in range(n_lat):
        send_ref[p, 0:1, :] = z[0:1, 0:128]
        send_ref[p, 1:2, :] = z[0:1, 128:256]
        send_ref[p, 2:3, :] = z[ROWS - 1 : ROWS, 0:128]
        send_ref[p, 3:4, :] = z[ROWS - 1 : ROWS, 128:256]
        send_ref[p, 4:5, :] = scalars


def cross_kernel(n_lat, n_lon, got_ref, send_ref):
    cross = jnp.zeros((2, 128), F32)
    for i in range(n_lat - 1):
        cross = cross + got_ref[i, 2:4, :] * got_ref[i + 1, 0:2, :]
    cross = jnp.sum(jnp.sum(cross, axis=0, keepdims=True), axis=1, keepdims=True)
    small = iota((1, 128), 1)
    total = jnp.sum(got_ref[:, 4:5, :], axis=0) - jnp.where(small == 1, 2.0 * cross, 0.0)
    for p in range(n_lon):
        send_ref[p] = total


def final_kernel(n_lat, lat_ref, z_ref, image_ref, rhs_ref, ocean_ref, got_ref, sums_ref, sol_ref, res_ref, pre_ref):
    me = lat_ref[0]
    row = iota((ROWS, EXT), 0)
    z = z_ref[...]
    sums = jnp.sum(sums_ref[...], axis=0)
    small = iota((1, 128), 1)
    affinity = jnp.sum(jnp.where(small == 0, sums, 0.0), axis=1, keepdims=True)
    energy = jnp.sum(jnp.where(small == 1, sums, 0.0), axis=1, keepdims=True)
    alpha = affinity / energy

    def line(index, first, inside):
        face = jnp.concatenate([got_ref[index, first : first + 1, :], got_ref[index, first + 1 : first + 2, :]], axis=1)
        return jnp.where(inside, face, 0.0)

    z_north = line(jnp.maximum(me - 1, 0), 2, me > 0)
    z_south = line(jnp.minimum(me + 1, n_lat - 1), 0, me < n_lat - 1)
    edge = jnp.where(row == 0, z_north, jnp.where(row == ROWS - 1, z_south, 0.0))
    image = image_ref[...] - ocean_ref[...] * edge

    def store(ref, x):
        ref[...] = pltpu.roll(x, EXT - HW, 1)[:, 0:COLS]

    store(pre_ref, z)
    store(sol_ref, alpha * z)
    store(res_ref, rhs_ref[...] - alpha * image)


def body(land_sea, obs_cell, obs_value, obs_weight, intersection, factors, coarse_inverse):
    n_lat, n_lon = lax.axis_size("lat"), lax.axis_size("lon")
    n_row = n_lat * 16 // 128
    me = lax.axis_index("lat").astype(jnp.int32).reshape(1)
    ring = [(j, (j + 1) % n_lon) for j in range(n_lon)]
    back = [(b, a) for a, b in ring]
    line = [(i, i + 1) for i in range(n_lat - 1)]
    up = [(b, a) for a, b in line]
    tile = (ROWS, EXT)

    def k(kernel, *static):
        def run(*refs):
            kernel(*static, *refs)

        run.__name__ = kernel.__name__
        return run

    slab = (TRI + QTR, 128)
    to_e, to_w, south, north = call(
        pack_kernel, [slab, slab, (TRI, EXT), (TRI, EXT)], (intersection, factors), smem=1
    )
    from_w = lax.ppermute(to_e, "lon", ring)
    from_e = lax.ppermute(to_w, "lon", back)
    diag, rhs, ocean, send = call(
        k(load_kernel, n_lat),
        [tile, tile, tile, (n_lat, n_row + 2, 128)],
        (me, obs_cell.reshape(1, OBS), obs_value.reshape(1, OBS), obs_weight.reshape(1, OBS), land_sea),
        smem=1,
        scratch=[pltpu.VMEM(tile, F32), pltpu.VMEM((6 * ROWS, OBS), jnp.bfloat16), pltpu.VMEM((EXT, OBS), jnp.bfloat16)],
    )
    got = lax.all_to_all(send, "lat", 0, 0, tiled=True)
    to_s, to_n, send = call(
        k(merge_kernel, n_lon, n_row),
        [(TRI, EXT), (TRI, EXT), (n_lon, n_row, 128)],
        (from_w, from_e, south, north, got),
    )
    from_n = lax.ppermute(to_s, "lat", line)
    from_s = lax.ppermute(to_n, "lat", up)
    coarse = lax.all_to_all(send, "lon", 0, 0, tiled=True)
    z, face_w, face_e = call(
        k(solve_kernel, n_lon, n_row),
        [tile, (2, 128), (2, 128)],
        (factors, rhs, ocean, from_w, from_e, from_n, from_s, coarse_inverse, coarse),
        scratch=[pltpu.VMEM(tile, F32)],
    )
    z_w = lax.ppermute(face_e, "lon", ring)
    z_e = lax.ppermute(face_w, "lon", back)
    image, send = call(
        k(image_kernel, n_lat, n_row), [tile, (n_lat, 5, 128)], (me, z, ocean, diag, rhs, got, z_w, z_e), smem=1
    )
    edges = lax.all_to_all(send, "lat", 0, 0, tiled=True)
    (send,) = call(k(cross_kernel, n_lat, n_lon), [(n_lon, 1, 128)], (edges,))
    sums = lax.all_to_all(send, "lon", 0, 0, tiled=True)
    out = (ROWS, COLS)
    return tuple(
        call(k(final_kernel, n_lat), [out, out, out], (me, z, image, rhs, ocean, edges, sums), smem=1)
    )


def solution(mesh):
    in_specs = (
        P("lat", "lon"),
        P("lat", "lon", None),
        P("lat", "lon", None),
        P("lat", "lon", None),
        P("lat", "lon"),
        P("lat", None, None, "lon"),
        P(("lon", "lat"), None),
    )
    out_specs = (P("lat", "lon"), P("lat", "lon"), P("lat", "lon"))
    return jax.shard_map(body, mesh=mesh, in_specs=in_specs, out_specs=out_specs, check_vma=False)
```

time: 321 us -> 113 us (0.35)
  blocking collectives: 203 us -> 71.3 us
  starting transfers between devices: 63.5 us -> 11.5 us
  other arithmetic: 35.4 us -> 0 us
  Pallas kernels: 0 us -> 17.2 us
    unnamed x1 -> x0, blocking collectives: 102 us -> none
    psum x1 -> x0, blocking collectives: 101 us -> none  [body(): affinity = lax.psum(jnp.sum(residual * precond), ('lon', 'lat'))]
    all_to_all x0 -> x4, blocking collectives: none -> 71.3 us  [the longest x1 29.5 us: body(): coarse = lax.all_to_all(send, 'lon', 0, 0, tiled=True)]
    ppermute x20 -> x6, starting transfers between devices: 63.5 us -> 11.5 us  [the longest x1 3.83 us: body(): from_e = lax.ppermute(to_w, 'lon', back)]
    scatter-add x2 -> x0, other arithmetic: 22.9 us -> none  [the longest x1 11.5 us: body(): jax.ops.segment_sum(obs_weight[0, 0] * obs_value[0, 0], cells, num_segmen...]
    pallas_call x0 -> x7, Pallas kernels: none -> 17.2 us  [call(): pl.pallas_call(kernel, out_shape=[jax.ShapeDtypeStruct(s, F32) for s in o...]
    pallas_call x0 -> x3, local copies, waits for them, and re-layouts: none -> 4.95 us  [call(): pl.pallas_call(kernel, out_shape=[jax.ShapeDtypeStruct(s, F32) for s in o...]
  transfers between devices with their start and end apart: 20 -> 6, of which waited for: 3 -> 2; matrix products, arithmetic and copies ran while one was open for 9% -> 1% of each run, Pallas kernels for 0% -> 2%
where the time goes in v1:
time: 113 us
  blocking collectives  71.3 us (63%)
  Pallas kernels  17.2 us (15%)
  starting transfers between devices  11.5 us (10%)
  local copies, waits for them, and re-layouts  7.69 us (7%)
  waiting for transfers between devices  3.51 us (3%)
  between operations  1.37 us (1%)
    all_to_all x1, blocking collectives, body(): coarse = lax.all_to_all(send, 'lon', 0, 0, tiled=True)  29.5 us
    all_to_all x1, blocking collectives, body(): sums = lax.all_to_all(send, 'lon', 0, 0, tiled=True)  18.1 us
    pallas_call x7, Pallas kernels, call(): pl.pallas_call(kernel, out_shape=[jax.ShapeDtypeStruct(s, F32) for s in o...  17.2 us
    all_to_all x1, blocking collectives, body(): edges = lax.all_to_all(send, 'lat', 0, 0, tiled=True)  13.1 us
    all_to_all x1, blocking collectives, body(): got = lax.all_to_all(send, 'lat', 0, 0, tiled=True)  10.6 us
    pallas_call x3, local copies, waits for them, and re-layouts, call(): pl.pallas_call(kernel, out_shape=[jax.ShapeDtypeStruct(s, F32) for s in o...  4.95 us
    ppermute x1, starting transfers between devices, body(): from_e = lax.ppermute(to_w, 'lon', back)  3.83 us
    ppermute x1, starting transfers between devices, body(): from_w = lax.ppermute(to_e, 'lon', ring)  3.02 us
  transfers between devices with their start and end apart: 6, of which 2 were waited for; matrix products, arithmetic and copies ran while one was open for 1% of the time, Pallas kernels for 2%

profile of v1, /device:TPU:1, one launch (start us, length us, event | category | flops | bytes accessed | tf_op | source)
XLA Modules:
  0.0 112.6 jit_solution(12702435587036240201)
XLA Ops:
  0.6 0.0 copy-start.4
  1.3 3.1 %shard_map.95 = (f32[240,128]{1,0:T(8,128)}, f32[240,128]{1,0:T(8,128)}, f32[192,256]{1,0:T(8,128)}, f32[192,256]{1,0:T(8,128)}) custom-call(s32[1,1]{1,0:T(1,128)S(6)} %copy.14.reach_ref, f32[10,16,16,256]{3,2,1,0:T(8,128)} %refs_0_.1), custom_call_target="tpu_custom_call" | custom-call | flops 100000 | bytes 2621444 | tf_op jit(solution)/shard_map/pallas_call | solution.py:26
  4.4 3.0 %collective-permute-start = (f32[240,128]{1,0:T(8,128)}, f32[240,128]{1,0:T(8,128)S(1)}, u32[]{:S(2)}, u32[]{:S(2)}) collective-permute-start(f32[240,128]{1,0:T(8,128)} %get-tuple-element.21), channel_id=1, source_target_pairs={{0,16},{16,32},{32,48},{48,64},{64,80},{80,96},{96,112},{112,128},... | collective-permute-start | bytes 368648 | tf_op jit(solution)/shard_map/ppermute | solution.py:333
  7.4 3.8 %collective-permute-start.1 = (f32[240,128]{1,0:T(8,128)}, f32[240,128]{1,0:T(8,128)S(1)}, u32[]{:S(2)}, u32[]{:S(2)}) collective-permute-start(f32[240,128]{1,0:T(8,128)} %get-tuple-element.22), channel_id=1, source_target_pairs={{16,0},{32,16},{48,32},{64,48},{80,64},{96,80},{112,96},{128,112},... | collective-permute-start | bytes 368648 | tf_op jit(solution)/shard_map/ppermute | solution.py:334
  11.3 0.0 copy-done.4
  11.3 0.8 copy.10.refs_4_
  12.0 2.7 %shard_map.94 = (f32[128,256]{1,0:T(8,128)}, f32[128,256]{1,0:T(8,128)}, f32[128,256]{1,0:T(8,128)}, f32[16,4,128]{2,1,0:T(4,128)}) custom-call(s32[1]{0:T(128)} %bitcast.refs_0_, s32[1,2048]{1,0:T(1,128)} %bitcast.4, f32[1,2048]{1,0:T(1,128)} %bitcast.5, f32[1,2048]{1,0:T(1,128)} %bitcast.6, s32[128,224]{1,0:T(8,128)} %copy.10.refs_4_), custom_call_target="tpu_custom_call" | custom-call | flops 100000 | bytes 139268 | tf_op jit(solution)/shard_map/pallas_call | solution.py:26
  14.7 10.6 %all_to_all.20.refs_4_.refs_5_ = f32[16,4,128]{2,1,0:T(4,128)} all-to-all(f32[16,4,128]{2,1,0:T(4,128)} %get-tuple-element.25), channel_id=1, replica_groups=mesh['lon'=32,'lat'=16] {'lat'}, dimensions={0} | all-to-all | bytes 65536 | tf_op jit(solution)/shard_map/all_to_all | solution.py:342
  25.3 0.0 collective-permute-done.refs_0_.refs_3_
  25.3 0.0 copy-start
  25.3 0.0 collective-permute-done.1.refs_1_.refs_4_
  25.3 0.0 copy-start.1
  25.3 0.6 copy-done
  25.9 0.0 copy-done.1
  26.0 2.0 %shard_map.96 = (f32[192,256]{1,0:T(8,128)}, f32[192,256]{1,0:T(8,128)}, f32[32,2,128]{2,1,0:T(2,128)}) custom-call(f32[240,128]{1,0:T(8,128)} %copy-done, f32[240,128]{1,0:T(8,128)} %copy-done.1, f32[192,256]{1,0:T(8,128)} %get-tuple-element.23.refs_2_, f32[192,256]{1,0:T(8,128)} %get-tuple-element.24.refs_3_, f32[16,4,128]{2,1,0:T(4,128)} %all_to_all.20.refs_4_.refs_5_), custom_call_target="tpu_custom_call" | custom-call | flops 100000 | bytes 671744 | tf_op jit(solution)/shard_map/pallas_call | solution.py:26
  28.0 2.2 %collective-permute-start.2 = (f32[192,256]{1,0:T(8,128)}, f32[192,256]{1,0:T(8,128)S(1)}, u32[]{:S(2)}, u32[]{:S(2)}) collective-permute-start(f32[192,256]{1,0:T(8,128)} %get-tuple-element.26), channel_id=1, source_target_pairs={{0,1},{1,2},{2,3},{3,4},{4,5},{5,6},{6,7},{7,8},{8,9},{9,10},{10,1... | collective-permute-start | bytes 589832 | tf_op jit(solution)/shard_map/ppermute | solution.py:348
  30.2 1.3 %collective-permute-start.3 = (f32[192,256]{1,0:T(8,128)}, f32[192,256]{1,0:T(8,128)S(1)}, u32[]{:S(2)}, u32[]{:S(2)}) collective-permute-start(f32[192,256]{1,0:T(8,128)} %get-tuple-element.27), channel_id=1, source_target_pairs={{1,0},{2,1},{3,2},{4,3},{5,4},{6,5},{7,6},{8,7},{9,8},{10,9},{11,1... | collective-permute-start | bytes 589832 | tf_op jit(solution)/shard_map/ppermute | solution.py:349
  31.5 29.5 %all_to_all.21.refs_8_ = f32[32,2,128]{2,1,0:T(2,128)} all-to-all(f32[32,2,128]{2,1,0:T(2,128)} %get-tuple-element.28), channel_id=1, replica_groups=mesh['lon'=32,'lat'=16] {'lon'}, dimensions={0} | all-to-all | bytes 65536 | tf_op jit(solution)/shard_map/all_to_all | solution.py:350
  61.0 0.0 collective-permute-done.2.refs_5_
  61.0 0.0 copy-start.2
  61.0 0.0 collective-permute-done.3.refs_6_
  61.0 0.0 copy-start.3
  61.0 0.7 copy-done.2
  61.7 0.1 copy-done.3
  61.8 3.5 %shard_map.97 = (f32[128,256]{1,0:T(8,128)}, f32[2,128]{1,0:T(2,128)}, f32[2,128]{1,0:T(2,128)}) custom-call(f32[10,16,16,256]{3,2,1,0:T(8,128)} %refs_0_.1, f32[128,256]{1,0:T(8,128)} %get-tuple-element.19.refs_1_.refs_4_.refs_3_, f32[128,256]{1,0:T(8,128)} %get-tuple-element.20.refs_2_.refs_4_, f32[240,128]{1,0:T(8,128)} %copy-done, f32[240,128]{1,0:T(8,128)} %copy-done.1, ...), custom_call_target="tpu_custom_call" | custom-call | flops 100000 | bytes 4079616 | tf_op jit(solution)/shard_map/pallas_call | solution.py:26
  65.3 1.2 %collective-permute-start.4 = (f32[2,128]{1,0:T(2,128)}, f32[2,128]{1,0:T(2,128)S(1)}, u32[]{:S(2)}, u32[]{:S(2)}) collective-permute-start(f32[2,128]{1,0:T(2,128)} %get-tuple-element.31), channel_id=1, source_target_pairs={{0,16},{16,32},{32,48},{48,64},{64,80},{80,96},{96,112},{112,128},... | collective-permute-start | bytes 3080 | tf_op jit(solution)/shard_map/ppermute | solution.py:357
  66.5 0.0 collective-permute-start.5
  66.5 0.9 collective-permute-done.4.refs_6_
  67.4 0.0 copy-start.5
  67.4 2.6 %collective-permute-done.5.refs_7_ = f32[2,128]{1,0:T(2,128)S(1)} collective-permute-done((f32[2,128]{1,0:T(2,128)}, f32[2,128]{1,0:T(2,128)S(1)}, u32[]{:S(2)}, u32[]{:S(2)}) %collective-permute-start.5) | collective-permute-done | bytes 1056 | tf_op jit(solution)/shard_map/ppermute | solution.py:358
  70.0 0.0 copy-start.6
  70.0 0.0 copy-done.5
  70.0 0.6 copy-done.6
  70.5 2.1 %shard_map.98 = (f32[128,256]{1,0:T(8,128)}, f32[16,5,128]{2,1,0:T(8,128)}) custom-call(s32[1]{0:T(128)} %bitcast.refs_0_, f32[128,256]{1,0:T(8,128)} %get-tuple-element.29.refs_1_, f32[128,256]{1,0:T(8,128)} %get-tuple-element.20.refs_2_.refs_4_, f32[128,256]{1,0:T(8,128)} %get-tuple-element.30.refs_3_, ...), custom_call_target="tpu_custom_call" | custom-call | flops 100000 | bytes 559108 | tf_op jit(solution)/shard_map/pallas_call | solution.py:26
  72.7 13.1 %all_to_all.22.refs_0_.refs_5_ = f32[16,5,128]{2,1,0:T(8,128)} all-to-all(f32[16,5,128]{2,1,0:T(8,128)} %get-tuple-element.34), channel_id=1, replica_groups=mesh['lon'=32,'lat'=16] {'lat'}, dimensions={0} | all-to-all | bytes 81920 | tf_op jit(solution)/shard_map/all_to_all | solution.py:362
  85.8 1.6 %shard_map.99 = f32[32,1,128]{2,1,0:T(1,128)} custom-call(f32[16,5,128]{2,1,0:T(8,128)} %all_to_all.22.refs_0_.refs_5_), custom_call_target="tpu_custom_call" | custom-call | flops 100000 | bytes 40960 | tf_op jit(solution)/shard_map/pallas_call | solution.py:26
  87.4 18.1 %all_to_all.23.refs_6_ = f32[32,1,128]{2,1,0:T(1,128)} all-to-all(f32[32,1,128]{2,1,0:T(1,128)} %shard_map.99), channel_id=1, replica_groups=mesh['lon'=32,'lat'=16] {'lon'}, dimensions={0} | all-to-all | bytes 32768 | tf_op jit(solution)/shard_map/all_to_all | solution.py:364
  105.5 2.1 %shard_map.100 = (f32[128,224]{1,0:T(8,128)}, f32[128,224]{1,0:T(8,128)}, f32[128,224]{1,0:T(8,128)}) custom-call(s32[1]{0:T(128)} %bitcast.refs_0_, f32[128,256]{1,0:T(8,128)} %get-tuple-element.29.refs_1_, f32[128,256]{1,0:T(8,128)} %get-tuple-element.33.refs_2_, f32[128,256]{1,0:T(8,128)} %get-tuple-element.19.refs_1_.refs_4_.refs_3_, ...), custom_call_target="tpu_custom_call" | custom-call | flops 100000 | bytes 581636 | tf_op jit(solution)/shard_map/pallas_call | solution.py:26
  107.6 1.6 %copy.11 = f32[128,224]{0,1:T(8,128)} copy(f32[128,224]{1,0:T(8,128)} %get-tuple-element.35) | data formatting | bytes 229376 | tf_op jit(solution)/shard_map/pallas_call | solution.py:26
  109.3 1.6 %copy.12 = f32[128,224]{0,1:T(8,128)} copy(f32[128,224]{1,0:T(8,128)} %get-tuple-element.36) | data formatting | bytes 229376 | tf_op jit(solution)/shard_map/pallas_call | solution.py:26
  110.9 1.6 %copy.13 = f32[128,224]{0,1:T(8,128)} copy(f32[128,224]{1,0:T(8,128)} %get-tuple-element.37) | data formatting | bytes 229376 | tf_op jit(solution)/shard_map/pallas_call | solution.py:26
Async XLA Ops:
  0.6 10.6 %copy-start.4 = (s32[128,224]{0,1:T(8,128)S(1)}, s32[128,224]{0,1:T(8,128)}, u32[]{:S(2)}) copy-start(s32[128,224]{0,1:T(8,128)} %param.7) | copy-start | bytes 344068
  4.4 20.9 %collective-permute-start = (f32[240,128]{1,0:T(8,128)}, f32[240,128]{1,0:T(8,128)S(1)}, u32[]{:S(2)}, u32[]{:S(2)}) collective-permute-start(f32[240,128]{1,0:T(8,128)} %get-tuple-element.21), channel_id=1, source_target_pairs={{0,16},{16,32},{32,48},{48,64},{64,80},{80,96},{96,112},{112,128},... | collective-permute-start | bytes 368648 | tf_op jit(solution)/shard_map/ppermute | solution.py:333
  7.4 17.9 %collective-permute-start.1 = (f32[240,128]{1,0:T(8,128)}, f32[240,128]{1,0:T(8,128)S(1)}, u32[]{:S(2)}, u32[]{:S(2)}) collective-permute-start(f32[240,128]{1,0:T(8,128)} %get-tuple-element.22), channel_id=1, source_target_pairs={{16,0},{32,16},{48,32},{64,48},{80,64},{96,80},{112,96},{128,112},... | collective-permute-start | bytes 368648 | tf_op jit(solution)/shard_map/ppermute | solution.py:334
  25.3 0.6 copy-start
  25.3 0.7 copy-start.1
  28.0 33.0 %collective-permute-start.2 = (f32[192,256]{1,0:T(8,128)}, f32[192,256]{1,0:T(8,128)S(1)}, u32[]{:S(2)}, u32[]{:S(2)}) collective-permute-start(f32[192,256]{1,0:T(8,128)} %get-tuple-element.26), channel_id=1, source_target_pairs={{0,1},{1,2},{2,3},{3,4},{4,5},{5,6},{6,7},{7,8},{8,9},{9,10},{10,1... | collective-permute-start | bytes 589832 | tf_op jit(solution)/shard_map/ppermute | solution.py:348
  30.2 30.8 %collective-permute-start.3 = (f32[192,256]{1,0:T(8,128)}, f32[192,256]{1,0:T(8,128)S(1)}, u32[]{:S(2)}, u32[]{:S(2)}) collective-permute-start(f32[192,256]{1,0:T(8,128)} %get-tuple-element.27), channel_id=1, source_target_pairs={{1,0},{2,1},{3,2},{4,3},{5,4},{6,5},{7,6},{8,7},{9,8},{10,9},{11,1... | collective-permute-start | bytes 589832 | tf_op jit(solution)/shard_map/ppermute | solution.py:349
  61.0 0.7 copy-start.2
  61.0 0.8 copy-start.3
  65.3 2.1 %collective-permute-start.4 = (f32[2,128]{1,0:T(2,128)}, f32[2,128]{1,0:T(2,128)S(1)}, u32[]{:S(2)}, u32[]{:S(2)}) collective-permute-start(f32[2,128]{1,0:T(2,128)} %get-tuple-element.31), channel_id=1, source_target_pairs={{0,16},{16,32},{32,48},{48,64},{64,80},{80,96},{96,112},{112,128},... | collective-permute-start | bytes 3080 | tf_op jit(solution)/shard_map/ppermute | solution.py:357
  66.5 3.5 %collective-permute-start.5 = (f32[2,128]{1,0:T(2,128)}, f32[2,128]{1,0:T(2,128)S(1)}, u32[]{:S(2)}, u32[]{:S(2)}) collective-permute-start(f32[2,128]{1,0:T(2,128)} %get-tuple-element.32), channel_id=1, source_target_pairs={{16,0},{32,16},{48,32},{64,48},{80,64},{96,80},{112,96},{128,112},... | collective-permute-start | bytes 3080 | tf_op jit(solution)/shard_map/ppermute | solution.py:358
  67.4 2.6 %copy-start.5 = (f32[2,128]{1,0:T(2,128)}, f32[2,128]{1,0:T(2,128)S(1)}, u32[]{:S(2)}) copy-start(f32[2,128]{1,0:T(2,128)S(1)} %collective-permute-done.4.refs_6_) | copy-start | bytes 3076
  70.0 0.6 copy-start.6

commit v2 on v1

--- a/solution.py
+++ b/solution.py
@@ -10,7 +10,6 @@
 ROWS, COLS, HW, EXT = 128, 224, 16, 256
 BLK = 8
 TRI = 192
-QTR = TRI // 4
 OBS = 2048
 
 VM = pl.BlockSpec(memory_space=pltpu.VMEM)
@@ -21,15 +20,16 @@
     return lax.broadcasted_iota(jnp.int32, shape, dim)
 
 
-def call(kernel, outs, ins, smem=0, scratch=(), flops=100000):
+def call(kernel, outs, ins, smem=0, scratch=(), flops=100000, limit=16, hbm=0):
     size = sum(4 * x.size for x in ins)
     return pl.pallas_call(
         kernel,
         out_shape=[jax.ShapeDtypeStruct(s, F32) for s in outs],
-        in_specs=[SM] * smem + [VM] * (len(ins) - smem),
+        in_specs=[SM] * smem + [pl.BlockSpec(memory_space=pltpu.HBM)] * hbm + [VM] * (len(ins) - smem - hbm),
         out_specs=[VM] * len(outs),
         scratch_shapes=list(scratch),
         cost_estimate=pl.CostEstimate(flops=flops, bytes_accessed=size, transcendentals=0),
+        compiler_params=pltpu.CompilerParams(vmem_limit_bytes=limit << 20),
     )(*ins)
 
 
@@ -37,46 +37,22 @@
     return jnp.concatenate([get(p, 8) for p in range(8)] + [get(p, 16) for p in range(8, 16)], axis=0)
 
 
-def pack_kernel(reach_ref, fac_ref, east_ref, west_ref, south_ref, north_ref):
+def halo_kernel(reach_ref, fac_ref, south_ref, north_ref, first, last, sems):
+    copies = [
+        pltpu.make_async_copy(fac_ref.at[0], first, sems.at[0]),
+        pltpu.make_async_copy(fac_ref.at[BLK + 1], last, sems.at[1]),
+    ]
+    for copy in copies:
+        copy.start()
     reach = reach_ref[0, 0]
-    lane = iota((TRI, 128), 1)
-    row = iota((TRI, 128), 0)
+    lane = iota((TRI, EXT), 1)
+    row = iota((TRI, EXT), 0)
     q = jnp.where(row < 64, row & 7, row & 15)
-    first_rows = q >= HW - reach
-    last_rows = q < reach
-    east = jnp.zeros((TRI, 128), F32)
-    west = jnp.zeros((TRI, 128), F32)
-    for k in range(BLK):
-        own = (lane >= k * 16) & (lane < k * 16 + 16)
-        hi = tri_rows(lambda p, n: fac_ref[k + 1, p, 0:n, 128:256])
-        lo = tri_rows(lambda p, n: fac_ref[k + 1, p, 0:n, 0:128])
-        east = jnp.where(own & (lane - k * 16 < reach), pltpu.roll(hi, (k * 16 - 112) % 128, 1), east)
-        west = jnp.where(own & (lane - k * 16 >= HW - reach), pltpu.roll(lo, k * 16, 1) if k else lo, west)
-    east_ref[0:TRI, :] = east
-    west_ref[0:TRI, :] = west
-    top_lo = tri_rows(lambda p, n: fac_ref[0, p, 0:n, 0:128])
-    top_hi = tri_rows(lambda p, n: fac_ref[0, p, 0:n, 128:256])
-    end_lo = tri_rows(lambda p, n: fac_ref[BLK + 1, p, 0:n, 0:128])
-    end_hi = tri_rows(lambda p, n: fac_ref[BLK + 1, p, 0:n, 128:256])
-    top_lo = jnp.where(first_rows, top_lo, 0.0)
-    top_hi = jnp.where(first_rows, top_hi, 0.0)
-    end_lo = jnp.where(last_rows, end_lo, 0.0)
-    end_hi = jnp.where(last_rows, end_hi, 0.0)
-    east_corner = jnp.where(
-        lane < 16, pltpu.roll(top_hi, 16, 1), jnp.where(lane < 32, pltpu.roll(end_hi, 32, 1), 0.0)
-    )
-    east_corner = jnp.where((lane & 15) < reach, east_corner, 0.0)
-    west_corner = jnp.where(lane < 16, top_lo, jnp.where(lane < 32, pltpu.roll(end_lo, 16, 1), 0.0))
-    west_corner = jnp.where((lane & 15) >= HW - reach, west_corner, 0.0)
-    for ref, corner in ((east_ref, east_corner), (west_ref, west_corner)):
-        packed = corner[0:QTR]
-        for g in range(1, 4):
-            packed = packed + pltpu.roll(corner[g * QTR : (g + 1) * QTR], 32 * g, 1)
-        ref[TRI : TRI + QTR, :] = packed
-    north_ref[:, 0:128] = jnp.where(lane >= 16, top_lo, 0.0)
-    north_ref[:, 128:256] = jnp.where(lane < 112, top_hi, 0.0)
-    south_ref[:, 0:128] = jnp.where(lane >= 16, end_lo, 0.0)
-    south_ref[:, 128:256] = jnp.where(lane < 112, end_hi, 0.0)
+    inside = (lane >= HW - reach) & (lane < HW + COLS + reach)
+    copies[0].wait()
+    north_ref[...] = jnp.where(inside & (q >= HW - reach), tri_rows(lambda p, n: first[p, 0:n, :]), 0.0)
+    copies[1].wait()
+    south_ref[...] = jnp.where(inside & (q < reach), tri_rows(lambda p, n: last[p, 0:n, :]), 0.0)
 
 
 def pieces(x):
@@ -90,9 +66,10 @@
 def load_kernel(n_lat, lat_ref, cell_ref, value_ref, weight_ref, land_ref, diag_ref, rhs_ref, ocean_ref, send_ref,
                 wide, left, right):
     me = lat_ref[0]
-    wide[...] = jnp.zeros((ROWS, EXT), F32)
-    wide[:, 0:COLS] = land_ref[...].astype(F32)
-    ocean = pltpu.roll(wide[...], HW, 1)
+    wide[0:HW, :] = jnp.zeros((HW, ROWS), F32)
+    wide[HW : HW + COLS, :] = land_ref[...].astype(F32)
+    wide[HW + COLS : EXT, :] = jnp.zeros((HW, ROWS), F32)
+    ocean = jnp.transpose(wide[...])
     ocean_ref[...] = ocean
     step = 512
     for start in range(0, OBS, step):
@@ -130,17 +107,25 @@
         send_ref[p, n_row + 1 : n_row + 2, :] = face[:, 128:256]
 
 
-def merge_kernel(n_lon, n_row, from_w_ref, from_e_ref, south_ref, north_ref, got_ref, to_s_ref, to_n_ref, send_ref):
-    lane = iota((QTR, 128), 1)
-    for g in range(4):
-        rows = slice(g * QTR, (g + 1) * QTR)
-        packed_w = from_w_ref[TRI : TRI + QTR, :]
-        packed_e = from_e_ref[TRI : TRI + QTR, :]
-        for ref, base, shift in ((to_n_ref, north_ref, 0), (to_s_ref, south_ref, 16)):
-            left = pltpu.roll(packed_w, (-32 * g - shift) % 128, 1) if g or shift else packed_w
-            right = pltpu.roll(packed_e, (112 - 32 * g - shift) % 128, 1)
-            ref[rows, 0:128] = jnp.where(lane < 16, left, base[rows, 0:128])
-            ref[rows, 128:256] = jnp.where(lane >= 112, right, base[rows, 128:256])
+def side_kernel(n_lon, n_row, reach_ref, fac_ref, from_n_ref, from_s_ref, got_ref, to_e_ref, to_w_ref, send_ref):
+    reach = reach_ref[0, 0]
+    lane = iota((TRI, 128), 1)
+    east = jnp.zeros((TRI, 128), F32)
+    west = jnp.zeros((TRI, 128), F32)
+    for k in range(BLK):
+        own = (lane >= k * 16) & (lane < k * 16 + 16)
+        hi = tri_rows(lambda p, n: fac_ref[k + 1, p, 0:n, 128:256])
+        lo = tri_rows(lambda p, n: fac_ref[k + 1, p, 0:n, 0:128])
+        east = jnp.where(own & (lane - k * 16 < reach), pltpu.roll(hi, (k * 16 - 112) % 128, 1), east)
+        west = jnp.where(own & (lane - k * 16 >= HW - reach), pltpu.roll(lo, k * 16, 1) if k else lo, west)
+    to_e_ref[:, 0:128] = east
+    to_w_ref[:, 0:128] = west
+    north, south = from_n_ref[:, 128:256], from_s_ref[:, 128:256]
+    to_e_ref[:, 128:256] = jnp.where(
+        lane < 16, pltpu.roll(north, 16, 1), jnp.where(lane < 32, pltpu.roll(south, 32, 1), 0.0)
+    )
+    north, south = from_n_ref[:, 0:128], from_s_ref[:, 0:128]
+    to_w_ref[:, 128:256] = jnp.where(lane < 16, north, jnp.where(lane < 32, pltpu.roll(south, 16, 1), 0.0))
     total = jnp.sum(got_ref[:, 0:n_row, :], axis=0)
     for p in range(n_lon):
         send_ref[p] = total
@@ -184,24 +169,33 @@
         own = (lane >= k * 16) & (lane < k * 16 + 16)
         u_w = jnp.where(own, pltpu.roll(u[:, 0:128], (k * 16 - 16) % 128, 1), u_w)
         u_e = jnp.where(own, pltpu.roll(u[:, 128:256], (k * 16 - 96) % 128, 1), u_e)
+    top, end = rhs_ref[0:16, :], rhs_ref[ROWS - 16 : ROWS, :]
+
+    def corners(top, end, at):
+        return jnp.where(
+            lane < 16, pltpu.roll(top, (-at) % 128, 1), jnp.where(lane < 32, pltpu.roll(end, (16 - at) % 128, 1), 0.0)
+        )
+
+    u_w = jnp.concatenate([u_w, corners(top[:, 0:128], end[:, 0:128], 16)], axis=1)
+    u_e = jnp.concatenate([u_e, corners(top[:, 128:256], end[:, 128:256], 96)], axis=1)
     g_w = apply_block(u_w, tri_get(from_w_ref))
     g_e = apply_block(u_e, tri_get(from_e_ref))
+    in_w = (lane >= 16) & (lane < 32)
+    in_e = (lane >= 96) & (lane < 112)
     for k in range(BLK):
         rows = slice(k * 16, k * 16 + 16)
-        in_w = (lane >= 16) & (lane < 32)
-        in_e = (lane >= 96) & (lane < 112)
-        acc[rows, 0:128] += jnp.where(in_w, pltpu.roll(g_w, (16 - k * 16) % 128, 1), 0.0)
-        acc[rows, 128:256] += jnp.where(in_e, pltpu.roll(g_e, (96 - k * 16) % 128, 1), 0.0)
+        add_w = pltpu.roll(g_w[:, 0:128], (16 - k * 16) % 128, 1)
+        add_e = pltpu.roll(g_e[:, 0:128], (96 - k * 16) % 128, 1)
+        if k == 0:
+            add_w = add_w + pltpu.roll(g_w[:, 128:256], 16, 1)
+            add_e = add_e + pltpu.roll(g_e[:, 128:256], 96, 1)
+        if k == BLK - 1:
+            add_w = add_w + g_w[:, 128:256]
+            add_e = add_e + pltpu.roll(g_e[:, 128:256], 80, 1)
+        acc[rows, 0:128] += jnp.where(in_w, add_w, 0.0)
+        acc[rows, 128:256] += jnp.where(in_e, add_e, 0.0)
     for rows, ref in ((slice(0, 16), from_n_ref), (slice(ROWS - 16, ROWS), from_s_ref)):
-        u = rhs_ref[rows, :]
-        u = jnp.where(
-            wide_lane < 16, pltpu.roll(u, EXT - 16, 1), jnp.where(wide_lane >= 240, pltpu.roll(u, 16, 1), u)
-        )
-        g = apply_block(u, tri_get(ref))
-        core = jnp.where((wide_lane >= 16) & (wide_lane < 240), g, 0.0)
-        from_left = jnp.where((wide_lane >= 16) & (wide_lane < 32), pltpu.roll(g, 16, 1), 0.0)
-        from_right = jnp.where((wide_lane >= 224) & (wide_lane < 240), pltpu.roll(g, EXT - 16, 1), 0.0)
-        acc[rows, :] += core + from_left + from_right
+        acc[rows, :] += apply_block(rhs_ref[rows, :], tri_get(ref))
     dot = jnp.zeros((16, 128), F32)
     for j in range(n_lon):
         for r in range(n_row):
@@ -302,7 +296,7 @@
     image = image_ref[...] - ocean_ref[...] * edge
 
     def store(ref, x):
-        ref[...] = pltpu.roll(x, EXT - HW, 1)[:, 0:COLS]
+        ref[...] = jnp.transpose(x)[HW : HW + COLS, :]
 
     store(pre_ref, z)
     store(sol_ref, alpha * z)
@@ -326,27 +320,33 @@
         run.__name__ = kernel.__name__
         return run
 
-    slab = (TRI + QTR, 128)
-    to_e, to_w, south, north = call(
-        pack_kernel, [slab, slab, (TRI, EXT), (TRI, EXT)], (intersection, factors), smem=1
-    )
-    from_w = lax.ppermute(to_e, "lon", ring)
-    from_e = lax.ppermute(to_w, "lon", back)
+    slab = (TRI, EXT)
+    to_s, to_n = call(
+        halo_kernel,
+        [slab, slab],
+        (intersection, factors),
+        smem=1,
+        hbm=1,
+        scratch=[pltpu.VMEM((16, 16, EXT), F32), pltpu.VMEM((16, 16, EXT), F32), pltpu.SemaphoreType.DMA((2,))],
+    )
+    from_n = lax.ppermute(to_s, "lat", line)
+    from_s = lax.ppermute(to_n, "lat", up)
     diag, rhs, ocean, send = call(
         k(load_kernel, n_lat),
         [tile, tile, tile, (n_lat, n_row + 2, 128)],
-        (me, obs_cell.reshape(1, OBS), obs_value.reshape(1, OBS), obs_weight.reshape(1, OBS), land_sea),
+        (me, obs_cell.reshape(1, OBS), obs_value.reshape(1, OBS), obs_weight.reshape(1, OBS), land_sea.T),
         smem=1,
-        scratch=[pltpu.VMEM(tile, F32), pltpu.VMEM((6 * ROWS, OBS), jnp.bfloat16), pltpu.VMEM((EXT, OBS), jnp.bfloat16)],
+        scratch=[pltpu.VMEM((EXT, ROWS), F32), pltpu.VMEM((6 * ROWS, OBS), jnp.bfloat16), pltpu.VMEM((EXT, OBS), jnp.bfloat16)],
     )
     got = lax.all_to_all(send, "lat", 0, 0, tiled=True)
-    to_s, to_n, send = call(
-        k(merge_kernel, n_lon, n_row),
-        [(TRI, EXT), (TRI, EXT), (n_lon, n_row, 128)],
-        (from_w, from_e, south, north, got),
-    )
-    from_n = lax.ppermute(to_s, "lat", line)
-    from_s = lax.ppermute(to_n, "lat", up)
+    to_e, to_w, send = call(
+        k(side_kernel, n_lon, n_row),
+        [slab, slab, (n_lon, n_row, 128)],
+        (intersection, factors, from_n, from_s, got),
+        smem=1,
+    )
+    from_w = lax.ppermute(to_e, "lon", ring)
+    from_e = lax.ppermute(to_w, "lon", back)
     coarse = lax.all_to_all(send, "lon", 0, 0, tiled=True)
     z, face_w, face_e = call(
         k(solve_kernel, n_lon, n_row),
@@ -362,9 +362,9 @@
     edges = lax.all_to_all(send, "lat", 0, 0, tiled=True)
     (send,) = call(k(cross_kernel, n_lat, n_lon), [(n_lon, 1, 128)], (edges,))
     sums = lax.all_to_all(send, "lon", 0, 0, tiled=True)
-    out = (ROWS, COLS)
+    out = (COLS, ROWS)
     return tuple(
-        call(k(final_kernel, n_lat), [out, out, out], (me, z, image, rhs, ocean, edges, sums), smem=1)
+        x.T for x in call(k(final_kernel, n_lat), [out, out, out], (me, z, image, rhs, ocean, edges, sums), smem=1)
     )
 
 

time: 113 us -> 94 us (0.83)
  Pallas kernels: 17.2 us -> 4.68 us
  local copies, waits for them, and re-layouts: 7.69 us -> 4.72 us
  blocking collectives: 71.3 us -> 68.5 us
    pallas_call x7, Pallas kernels: 17.2 us -> 4.68 us  [call(): pl.pallas_call(kernel, out_shape=[jax.ShapeDtypeStruct(s, F32) for s in o...]
    pallas_call x3 -> x0, local copies, waits for them, and re-layouts: 4.95 us -> none  [call(): pl.pallas_call(kernel, out_shape=[jax.ShapeDtypeStruct(s, F32) for s in o...]
    ppermute x1, starting transfers between devices: 3.83 us -> 0.01 us  [body(): from_e = lax.ppermute(to_w, 'lon', back)]
    all_to_all x1, blocking collectives: 13.1 us -> 9.33 us  [body(): edges = lax.all_to_all(send, 'lat', 0, 0, tiled=True)]
    all_to_all x1, blocking collectives: 10.6 us -> 13.9 us  [body(): got = lax.all_to_all(send, 'lat', 0, 0, tiled=True)]
    unnamed x15 -> x14, local copies, waits for them, and re-layouts: 2.75 us -> 4.72 us
    ppermute x1, starting transfers between devices: 2.19 us -> 4.08 us  [body(): from_n = lax.ppermute(to_s, 'lat', line)]
    all_to_all x1, blocking collectives: 18.1 us -> 16.8 us  [body(): sums = lax.all_to_all(send, 'lon', 0, 0, tiled=True)]
  transfers between devices with their start and end apart: 6 -> 6, of which waited for: 2 -> 2; matrix products, arithmetic and copies ran while one was open for 1% -> 0% of each run, Pallas kernels for 2% -> 1%
where the time goes in v2:
time: 94 us; the launch traced here: 93.5 us
  blocking collectives  68.5 us (73%)
  starting transfers between devices  10.9 us (12%)
  local copies, waits for them, and re-layouts  4.72 us (5%)
  Pallas kernels  4.68 us (5%)
  waiting for transfers between devices  3.3 us (4%)
  between operations  1.37 us (1%)
    all_to_all x1, blocking collectives, body(): coarse = lax.all_to_all(send, 'lon', 0, 0, tiled=True)  28.5 us
    all_to_all x1, blocking collectives, body(): sums = lax.all_to_all(send, 'lon', 0, 0, tiled=True)  16.8 us
    all_to_all x1, blocking collectives, body(): got = lax.all_to_all(send, 'lat', 0, 0, tiled=True)  13.9 us
    all_to_all x1, blocking collectives, body(): edges = lax.all_to_all(send, 'lat', 0, 0, tiled=True)  9.33 us
    unnamed x14, local copies, waits for them, and re-layouts  4.72 us
    pallas_call x7, Pallas kernels, call(): pl.pallas_call(kernel, out_shape=[jax.ShapeDtypeStruct(s, F32) for s in o...  4.68 us
    ppermute x1, starting transfers between devices, body(): from_w = lax.ppermute(to_e, 'lon', ring)  4.2 us
    ppermute x1, starting transfers between devices, body(): from_n = lax.ppermute(to_s, 'lat', line)  4.08 us
  transfers between devices with their start and end apart: 6, of which 2 were waited for; matrix products, arithmetic and copies ran while one was open for 0% of the time, Pallas kernels for 1%

profile of v2, /device:TPU:1, one launch (start us, length us, event | category | flops | bytes accessed | tf_op | source)
XLA Modules:
  0.0 93.5 jit_solution(12995082244650943190)
XLA Ops:
  1.3 0.0 copy-start
  1.3 1.7 %copy-done = f32[10,16,16,256]{3,2,1,0:T(8,128)S(1)} copy-done((f32[10,16,16,256]{3,2,1,0:T(8,128)S(1)}, f32[10,16,16,256]{3,2,1,0:T(8,128)}, u32[]{:S(2)}) %copy-start) | copy-done | bytes 2621464
  3.0 0.0 copy-start.1
  3.0 0.0 copy-start.2
  3.0 0.8 shard_map.95
  3.9 4.1 %collective-permute-start = (f32[192,256]{1,0:T(8,128)}, f32[192,256]{1,0:T(8,128)S(1)}, u32[]{:S(2)}, u32[]{:S(2)}) collective-permute-start(f32[192,256]{1,0:T(8,128)} %get-tuple-element.22), channel_id=1, source_target_pairs={{0,1},{1,2},{2,3},{3,4},{4,5},{5,6},{6,7},{7,8},{8,9},{9,10},{10,1... | collective-permute-start | bytes 589832 | tf_op jit(solution)/shard_map/ppermute | solution.py:332
  8.0 1.3 %collective-permute-start.1 = (f32[192,256]{1,0:T(8,128)}, f32[192,256]{1,0:T(8,128)S(1)}, u32[]{:S(2)}, u32[]{:S(2)}) collective-permute-start(f32[192,256]{1,0:T(8,128)} %get-tuple-element.23), channel_id=1, source_target_pairs={{1,0},{2,1},{3,2},{4,3},{5,4},{6,5},{7,6},{8,7},{9,8},{10,9},{11,1... | collective-permute-start | bytes 589832 | tf_op jit(solution)/shard_map/ppermute | solution.py:333
  9.3 0.0 copy-start.3
  9.3 0.9 copy-done.3
  10.2 0.0 copy-start.4
  10.2 0.7 copy-done.4
  10.9 0.0 copy-start.5
  10.9 0.7 copy-done.5
  11.6 0.0 copy-start.6
  11.6 0.7 copy-done.6
  12.3 1.1 %shard_map.94 = (f32[128,256]{1,0:T(8,128)S(1)}, f32[128,256]{1,0:T(8,128)S(1)}, f32[128,256]{1,0:T(8,128)S(1)}, f32[16,4,128]{2,1,0:T(4,128)S(1)}) custom-call(s32[1]{0:T(128)} %bitcast.refs_0_, s32[1,2048]{1,0:T(1,128)S(1)} %bitcast.9, f32[1,2048]{1,0:T(1,128)S(1)} %bitcast.10, f32[1,2048]{1,0:T(1,128)S(1)} %bitcast.11, s32[224,128]{1,0:T(8,128)S(1)} %bitcast.8), custom_call_target="tpu_custom_call" | custom-call | flops 100000 | bytes 139268 | tf_op jit(solution)/shard_map/pallas_call | solution.py:25
  13.4 13.9 %all_to_all.20.refs_4_.refs_5_ = f32[16,4,128]{2,1,0:T(4,128)S(1)} all-to-all(f32[16,4,128]{2,1,0:T(4,128)S(1)} %get-tuple-element.24), channel_id=1, replica_groups=mesh['lon'=32,'lat'=16] {'lat'}, dimensions={0} | all-to-all | bytes 65536 | tf_op jit(solution)/shard_map/all_to_all | solution.py:341
  27.3 0.0 collective-permute-done.refs_2_.refs_5_
  27.3 0.0 collective-permute-done.1.refs_3_.refs_6_
  27.3 0.0 copy-done.1
  27.3 0.5 shard_map.96
  27.8 4.2 %collective-permute-start.2 = (f32[192,256]{1,0:T(8,128)S(1)}, f32[192,256]{1,0:T(8,128)S(1)}, u32[]{:S(2)}, u32[]{:S(2)}) collective-permute-start(f32[192,256]{1,0:T(8,128)S(1)} %get-tuple-element.25), channel_id=1, source_target_pairs={{0,16},{16,32},{32,48},{48,64},{64,80},{80,96},{96,112},{112,128},... | collective-permute-start | bytes 589832 | tf_op jit(solution)/shard_map/ppermute | solution.py:348
  32.0 0.0 collective-permute-start.3
  32.0 28.5 %all_to_all.21.refs_8_ = f32[32,2,128]{2,1,0:T(2,128)S(1)} all-to-all(f32[32,2,128]{2,1,0:T(2,128)S(1)} %get-tuple-element.27), channel_id=1, replica_groups=mesh['lon'=32,'lat'=16] {'lon'}, dimensions={0} | all-to-all | bytes 65536 | tf_op jit(solution)/shard_map/all_to_all | solution.py:350
  60.5 0.0 collective-permute-done.2.refs_3_
  60.5 0.0 collective-permute-done.3.refs_4_
  60.5 0.0 copy-done.2
  60.5 0.8 shard_map.97
  61.3 1.4 %collective-permute-start.4 = (f32[2,128]{1,0:T(2,128)S(1)}, f32[2,128]{1,0:T(2,128)S(1)}, u32[]{:S(2)}, u32[]{:S(2)}) collective-permute-start(f32[2,128]{1,0:T(2,128)S(1)} %get-tuple-element.30), channel_id=1, source_target_pairs={{0,16},{16,32},{32,48},{48,64},{64,80},{80,96},{96,112},{112,128},... | collective-permute-start | bytes 3080 | tf_op jit(solution)/shard_map/ppermute | solution.py:357
  62.7 0.0 collective-permute-start.5
  62.7 0.7 collective-permute-done.4.refs_6_
  63.4 2.6 %collective-permute-done.5.refs_7_ = f32[2,128]{1,0:T(2,128)S(1)} collective-permute-done((f32[2,128]{1,0:T(2,128)S(1)}, f32[2,128]{1,0:T(2,128)S(1)}, u32[]{:S(2)}, u32[]{:S(2)}) %collective-permute-start.5) | collective-permute-done | bytes 1056 | tf_op jit(solution)/shard_map/ppermute | solution.py:358
  65.9 0.4 shard_map.98
  66.3 9.3 %all_to_all.22.refs_0_.refs_5_ = f32[16,5,128]{2,1,0:T(8,128)S(1)} all-to-all(f32[16,5,128]{2,1,0:T(8,128)S(1)} %get-tuple-element.33), channel_id=1, replica_groups=mesh['lon'=32,'lat'=16] {'lat'}, dimensions={0} | all-to-all | bytes 81920 | tf_op jit(solution)/shard_map/all_to_all | solution.py:362
  75.7 0.1 shard_map.99
  75.8 16.8 %all_to_all.23.refs_6_ = f32[32,1,128]{2,1,0:T(1,128)S(1)} all-to-all(f32[32,1,128]{2,1,0:T(1,128)S(1)} %shard_map.99), channel_id=1, replica_groups=mesh['lon'=32,'lat'=16] {'lon'}, dimensions={0} | all-to-all | bytes 32768 | tf_op jit(solution)/shard_map/all_to_all | solution.py:364
  92.5 0.9 %shard_map.100 = (f32[224,128]{1,0:T(8,128)}, f32[224,128]{1,0:T(8,128)}, f32[224,128]{1,0:T(8,128)}) custom-call(s32[1]{0:T(128)} %bitcast.refs_0_, f32[128,256]{1,0:T(8,128)S(1)} %get-tuple-element.28.refs_1_, f32[128,256]{1,0:T(8,128)S(1)} %get-tuple-element.32.refs_2_, f32[128,256]{1,0:T(8,128)S(1)} %get-tuple-element.20.refs_1_.refs_4_.refs_3_, ...), custom_call_target="tpu_custom_call" | custom-call | flops 100000 | bytes 581636 | tf_op jit(solution)/shard_map/pallas_call | solution.py:25
Async XLA Ops:
  1.3 1.7 %copy-start = (f32[10,16,16,256]{3,2,1,0:T(8,128)S(1)}, f32[10,16,16,256]{3,2,1,0:T(8,128)}, u32[]{:S(2)}) copy-start(f32[10,16,16,256]{3,2,1,0:T(8,128)} %refs_0_.2) | copy-start | bytes 7864324
  3.0 24.3 %copy-start.1 = (f32[10,16,16,256]{3,2,1,0:T(8,128)S(1)}, f32[10,16,16,256]{3,2,1,0:T(8,128)}, u32[]{:S(2)}) copy-start(f32[10,16,16,256]{3,2,1,0:T(8,128)} %refs_0_.2) | copy-start | bytes 7864324
  3.0 57.5 %copy-start.2 = (f32[16,8192]{1,0:T(8,128)S(1)}, f32[16,8192]{1,0:T(8,128)}, u32[]{:S(2)}) copy-start(f32[16,8192]{1,0:T(8,128)} %refs_7_.1) | copy-start | bytes 1572868
  3.9 23.4 %collective-permute-start = (f32[192,256]{1,0:T(8,128)}, f32[192,256]{1,0:T(8,128)S(1)}, u32[]{:S(2)}, u32[]{:S(2)}) collective-permute-start(f32[192,256]{1,0:T(8,128)} %get-tuple-element.22), channel_id=1, source_target_pairs={{0,1},{1,2},{2,3},{3,4},{4,5},{5,6},{6,7},{7,8},{8,9},{9,10},{10,1... | collective-permute-start | bytes 589832 | tf_op jit(solution)/shard_map/ppermute | solution.py:332
  8.0 19.3 %collective-permute-start.1 = (f32[192,256]{1,0:T(8,128)}, f32[192,256]{1,0:T(8,128)S(1)}, u32[]{:S(2)}, u32[]{:S(2)}) collective-permute-start(f32[192,256]{1,0:T(8,128)} %get-tuple-element.23), channel_id=1, source_target_pairs={{1,0},{2,1},{3,2},{4,3},{5,4},{6,5},{7,6},{8,7},{9,8},{10,9},{11,1... | collective-permute-start | bytes 589832 | tf_op jit(solution)/shard_map/ppermute | solution.py:333
  9.3 0.9 copy-start.3
  10.2 0.7 copy-start.4
  10.9 0.7 copy-start.5
  11.6 0.7 copy-start.6
  27.8 32.7 %collective-permute-start.2 = (f32[192,256]{1,0:T(8,128)S(1)}, f32[192,256]{1,0:T(8,128)S(1)}, u32[]{:S(2)}, u32[]{:S(2)}) collective-permute-start(f32[192,256]{1,0:T(8,128)S(1)} %get-tuple-element.25), channel_id=1, source_target_pairs={{0,16},{16,32},{32,48},{48,64},{64,80},{80,96},{96,112},{112,128},... | collective-permute-start | bytes 589832 | tf_op jit(solution)/shard_map/ppermute | solution.py:348
  32.0 28.5 %collective-permute-start.3 = (f32[192,256]{1,0:T(8,128)S(1)}, f32[192,256]{1,0:T(8,128)S(1)}, u32[]{:S(2)}, u32[]{:S(2)}) collective-permute-start(f32[192,256]{1,0:T(8,128)S(1)} %get-tuple-element.26), channel_id=1, source_target_pairs={{16,0},{32,16},{48,32},{64,48},{80,64},{96,80},{112,96},{128,112},... | collective-permute-start | bytes 589832 | tf_op jit(solution)/shard_map/ppermute | solution.py:349
  61.3 2.1 %collective-permute-start.4 = (f32[2,128]{1,0:T(2,128)S(1)}, f32[2,128]{1,0:T(2,128)S(1)}, u32[]{:S(2)}, u32[]{:S(2)}) collective-permute-start(f32[2,128]{1,0:T(2,128)S(1)} %get-tuple-element.30), channel_id=1, source_target_pairs={{0,16},{16,32},{32,48},{48,64},{64,80},{80,96},{96,112},{112,128},... | collective-permute-start | bytes 3080 | tf_op jit(solution)/shard_map/ppermute | solution.py:357
  62.7 3.3 %collective-permute-start.5 = (f32[2,128]{1,0:T(2,128)S(1)}, f32[2,128]{1,0:T(2,128)S(1)}, u32[]{:S(2)}, u32[]{:S(2)}) collective-permute-start(f32[2,128]{1,0:T(2,128)S(1)} %get-tuple-element.31), channel_id=1, source_target_pairs={{16,0},{32,16},{48,32},{64,48},{80,64},{96,80},{112,96},{128,112},... | collective-permute-start | bytes 3080 | tf_op jit(solution)/shard_map/ppermute | solution.py:358

commit v3 on v2

--- a/solution.py
+++ b/solution.py
@@ -13,46 +13,32 @@
 OBS = 2048
 
 VM = pl.BlockSpec(memory_space=pltpu.VMEM)
-SM = pl.BlockSpec(memory_space=pltpu.SMEM)
+PLACES = {
+    "v": VM,
+    "s": pl.BlockSpec(memory_space=pltpu.SMEM),
+    "h": pl.BlockSpec(memory_space=pltpu.HBM),
+}
 
 
 def iota(shape, dim):
     return lax.broadcasted_iota(jnp.int32, shape, dim)
 
 
-def call(kernel, outs, ins, smem=0, scratch=(), flops=100000, limit=16, hbm=0):
+def call(kernel, outs, ins, scratch=(), flops=100000, limit=16384, places=None):
     size = sum(4 * x.size for x in ins)
     return pl.pallas_call(
         kernel,
         out_shape=[jax.ShapeDtypeStruct(s, F32) for s in outs],
-        in_specs=[SM] * smem + [pl.BlockSpec(memory_space=pltpu.HBM)] * hbm + [VM] * (len(ins) - smem - hbm),
+        in_specs=[PLACES[p] for p in places or "v" * len(ins)],
         out_specs=[VM] * len(outs),
         scratch_shapes=list(scratch),
         cost_estimate=pl.CostEstimate(flops=flops, bytes_accessed=size, transcendentals=0),
-        compiler_params=pltpu.CompilerParams(vmem_limit_bytes=limit << 20),
+        compiler_params=pltpu.CompilerParams(vmem_limit_bytes=limit << 10),
     )(*ins)
 
 
 def tri_rows(get):
     return jnp.concatenate([get(p, 8) for p in range(8)] + [get(p, 16) for p in range(8, 16)], axis=0)
-
-
-def halo_kernel(reach_ref, fac_ref, south_ref, north_ref, first, last, sems):
-    copies = [
-        pltpu.make_async_copy(fac_ref.at[0], first, sems.at[0]),
-        pltpu.make_async_copy(fac_ref.at[BLK + 1], last, sems.at[1]),
-    ]
-    for copy in copies:
-        copy.start()
-    reach = reach_ref[0, 0]
-    lane = iota((TRI, EXT), 1)
-    row = iota((TRI, EXT), 0)
-    q = jnp.where(row < 64, row & 7, row & 15)
-    inside = (lane >= HW - reach) & (lane < HW + COLS + reach)
-    copies[0].wait()
-    north_ref[...] = jnp.where(inside & (q >= HW - reach), tri_rows(lambda p, n: first[p, 0:n, :]), 0.0)
-    copies[1].wait()
-    south_ref[...] = jnp.where(inside & (q < reach), tri_rows(lambda p, n: last[p, 0:n, :]), 0.0)
 
 
 def pieces(x):
@@ -63,13 +49,33 @@
     return hi, mid, low
 
 
-def load_kernel(n_lat, lat_ref, cell_ref, value_ref, weight_ref, land_ref, diag_ref, rhs_ref, ocean_ref, send_ref,
-                wide, left, right):
-    me = lat_ref[0]
-    wide[0:HW, :] = jnp.zeros((HW, ROWS), F32)
-    wide[HW : HW + COLS, :] = land_ref[...].astype(F32)
-    wide[HW + COLS : EXT, :] = jnp.zeros((HW, ROWS), F32)
-    ocean = jnp.transpose(wide[...])
+def first_kernel(n_lat, reach_ref, fac_hbm, land_hbm, cell_hbm, value_hbm, weight_hbm, south_ref, north_ref, diag_ref,
+                 rhs_ref, ocean_ref, send_ref, first, last, wide, cell_ref, value_ref, weight_ref, left, right,
+                 sems):
+    moves = (
+        (cell_hbm, cell_ref),
+        (value_hbm, value_ref),
+        (weight_hbm, weight_ref),
+        (land_hbm, wide.at[pl.ds(HW, COLS), :]),
+        (fac_hbm.at[0], first),
+        (fac_hbm.at[BLK + 1], last),
+    )
+    copies = [pltpu.make_async_copy(src, dst, sems.at[n]) for n, (src, dst) in enumerate(moves)]
+    for copy in copies:
+        copy.start()
+    me = lax.axis_index("lat")
+    wide[0:HW, :] = jnp.zeros((HW, ROWS), jnp.int32)
+    wide[HW + COLS : EXT, :] = jnp.zeros((HW, ROWS), jnp.int32)
+    for copy in copies:
+        copy.wait()
+    edge = iota((TRI, EXT), 1)
+    row = iota((TRI, EXT), 0)
+    q = jnp.where(row < 64, row & 7, row & 15)
+    reach = reach_ref[0, 0]
+    inside = (edge >= HW - reach) & (edge < HW + COLS + reach)
+    north_ref[...] = jnp.where(inside & (q >= HW - reach), tri_rows(lambda p, n: first[p, 0:n, :]), 0.0)
+    south_ref[...] = jnp.where(inside & (q < reach), tri_rows(lambda p, n: last[p, 0:n, :]), 0.0)
+    ocean = jnp.transpose(wide[...].astype(F32))
     ocean_ref[...] = ocean
     step = 512
     for start in range(0, OBS, step):
@@ -219,9 +225,9 @@
     face_e_ref[1:2, :] = o_right[111:112]
 
 
-def image_kernel(n_lat, n_row, lat_ref, z_ref, ocean_ref, diag_ref, rhs_ref, got_ref, from_w_ref, from_e_ref,
+def image_kernel(n_lat, n_row, z_ref, ocean_ref, diag_ref, rhs_ref, got_ref, from_w_ref, from_e_ref,
                  image_ref, send_ref):
-    me = lat_ref[0]
+    me = lax.axis_index("lat")
     lane = iota((ROWS, EXT), 1)
     row = iota((ROWS, EXT), 0)
     z = z_ref[...]
@@ -276,8 +282,8 @@
         send_ref[p] = total
 
 
-def final_kernel(n_lat, lat_ref, z_ref, image_ref, rhs_ref, ocean_ref, got_ref, sums_ref, sol_ref, res_ref, pre_ref):
-    me = lat_ref[0]
+def final_kernel(n_lat, z_ref, image_ref, rhs_ref, ocean_ref, got_ref, sums_ref, sol_ref, res_ref, pre_ref):
+    me = lax.axis_index("lat")
     row = iota((ROWS, EXT), 0)
     z = z_ref[...]
     sums = jnp.sum(sums_ref[...], axis=0)
@@ -306,7 +312,6 @@
 def body(land_sea, obs_cell, obs_value, obs_weight, intersection, factors, coarse_inverse):
     n_lat, n_lon = lax.axis_size("lat"), lax.axis_size("lon")
     n_row = n_lat * 16 // 128
-    me = lax.axis_index("lat").astype(jnp.int32).reshape(1)
     ring = [(j, (j + 1) % n_lon) for j in range(n_lon)]
     back = [(b, a) for a, b in ring]
     line = [(i, i + 1) for i in range(n_lat - 1)]
@@ -321,29 +326,39 @@
         return run
 
     slab = (TRI, EXT)
-    to_s, to_n = call(
-        halo_kernel,
-        [slab, slab],
-        (intersection, factors),
-        smem=1,
-        hbm=1,
-        scratch=[pltpu.VMEM((16, 16, EXT), F32), pltpu.VMEM((16, 16, EXT), F32), pltpu.SemaphoreType.DMA((2,))],
+    to_s, to_n, diag, rhs, ocean, send = call(
+        k(first_kernel, n_lat),
+        [slab, slab, tile, tile, tile, (n_lat, n_row + 2, 128)],
+        (
+            intersection,
+            factors,
+            land_sea.T,
+            obs_cell.reshape(1, OBS),
+            obs_value.reshape(1, OBS),
+            obs_weight.reshape(1, OBS),
+        ),
+        places="shhhhh",
+        limit=61000,
+        scratch=[
+            pltpu.VMEM((16, 16, EXT), F32),
+            pltpu.VMEM((16, 16, EXT), F32),
+            pltpu.VMEM((EXT, ROWS), jnp.int32),
+            pltpu.VMEM((1, OBS), jnp.int32),
+            pltpu.VMEM((1, OBS), F32),
+            pltpu.VMEM((1, OBS), F32),
+            pltpu.VMEM((6 * ROWS, OBS), jnp.bfloat16),
+            pltpu.VMEM((EXT, OBS), jnp.bfloat16),
+            pltpu.SemaphoreType.DMA((6,)),
+        ],
     )
     from_n = lax.ppermute(to_s, "lat", line)
     from_s = lax.ppermute(to_n, "lat", up)
-    diag, rhs, ocean, send = call(
-        k(load_kernel, n_lat),
-        [tile, tile, tile, (n_lat, n_row + 2, 128)],
-        (me, obs_cell.reshape(1, OBS), obs_value.reshape(1, OBS), obs_weight.reshape(1, OBS), land_sea.T),
-        smem=1,
-        scratch=[pltpu.VMEM((EXT, ROWS), F32), pltpu.VMEM((6 * ROWS, OBS), jnp.bfloat16), pltpu.VMEM((EXT, OBS), jnp.bfloat16)],
-    )
     got = lax.all_to_all(send, "lat", 0, 0, tiled=True)
     to_e, to_w, send = call(
         k(side_kernel, n_lon, n_row),
         [slab, slab, (n_lon, n_row, 128)],
         (intersection, factors, from_n, from_s, got),
-        smem=1,
+        places="svvvv",
     )
     from_w = lax.ppermute(to_e, "lon", ring)
     from_e = lax.ppermute(to_w, "lon", back)
@@ -357,14 +372,14 @@
     z_w = lax.ppermute(face_e, "lon", ring)
     z_e = lax.ppermute(face_w, "lon", back)
     image, send = call(
-        k(image_kernel, n_lat, n_row), [tile, (n_lat, 5, 128)], (me, z, ocean, diag, rhs, got, z_w, z_e), smem=1
+        k(image_kernel, n_lat, n_row), [tile, (n_lat, 5, 128)], (z, ocean, diag, rhs, got, z_w, z_e)
     )
     edges = lax.all_to_all(send, "lat", 0, 0, tiled=True)
     (send,) = call(k(cross_kernel, n_lat, n_lon), [(n_lon, 1, 128)], (edges,))
     sums = lax.all_to_all(send, "lon", 0, 0, tiled=True)
     out = (COLS, ROWS)
     return tuple(
-        x.T for x in call(k(final_kernel, n_lat), [out, out, out], (me, z, image, rhs, ocean, edges, sums), smem=1)
+        x.T for x in call(k(final_kernel, n_lat), [out, out, out], (z, image, rhs, ocean, edges, sums))
     )
 
 

time: 94 us -> 90.6 us (0.964)
  local copies, waits for them, and re-layouts: 4.72 us -> 0.02 us
  Pallas kernels: 4.68 us -> 5.82 us
    unnamed x14 -> x10, local copies, waits for them, and re-layouts: 4.72 us -> 0.02 us
    pallas_call x7 -> x6, Pallas kernels: 4.68 us -> 5.82 us  [call(): pl.pallas_call(kernel, out_shape=[jax.ShapeDtypeStruct(s, F32) for s in o...]
  transfers between devices with their start and end apart: 6 -> 6, of which waited for: 2 -> 2; matrix products, arithmetic and copies ran while one was open for 0% -> 0% of each run, Pallas kernels for 1% -> 0%
where the time goes in v3:
time: 90.6 us; the launch traced here: 90.3 us
  blocking collectives  68.7 us (76%)
  starting transfers between devices  10.9 us (12%)
  Pallas kernels  5.82 us (6%)
  waiting for transfers between devices  3.3 us (4%)
  between operations  1.54 us (2%)
    all_to_all x1, blocking collectives, body(): coarse = lax.all_to_all(send, 'lon', 0, 0, tiled=True)  28.5 us
    all_to_all x1, blocking collectives, body(): sums = lax.all_to_all(send, 'lon', 0, 0, tiled=True)  16.8 us
    all_to_all x1, blocking collectives, body(): got = lax.all_to_all(send, 'lat', 0, 0, tiled=True)  14.1 us
    all_to_all x1, blocking collectives, body(): edges = lax.all_to_all(send, 'lat', 0, 0, tiled=True)  9.33 us
    pallas_call x6, Pallas kernels, call(): pl.pallas_call(kernel, out_shape=[jax.ShapeDtypeStruct(s, F32) for s in o...  5.82 us
    ppermute x1, starting transfers between devices, body(): from_w = lax.ppermute(to_e, 'lon', ring)  4.2 us
    ppermute x1, starting transfers between devices, body(): from_n = lax.ppermute(to_s, 'lat', line)  4.08 us
    ppermute x1, waiting for transfers between devices, body(): z_e = lax.ppermute(face_w, 'lon', back)  2.57 us
  transfers between devices with their start and end apart: 6, of which 2 were waited for; matrix products, arithmetic and copies ran while one was open for 0% of the time, Pallas kernels for 0%

profile of v3, /device:TPU:1, one launch (start us, length us, event | category | flops | bytes accessed | tf_op | source)
XLA Modules:
  0.0 90.3 jit_solution(15512146791081528140)
XLA Ops:
  0.6 0.0 copy-start
  1.4 0.0 copy-start.3
  1.4 3.1 %shard_map.94 = (f32[192,256]{1,0:T(8,128)}, f32[192,256]{1,0:T(8,128)}, f32[128,256]{1,0:T(8,128)}, f32[128,256]{1,0:T(8,128)}, f32[128,256]{1,0:T(8,128)}, /*index=5*/f32[16,4,128]{2,1,0:T(4,128)}) custom-call(s32[1,1]{1,0:T(1,128)S(6)} %copy.10.refs_0_, f32[10,16,16,256]{3,2,1,0:T(8,128)} %refs_0_.3, s32[224,128]{1,0:T(8,128)} %bitcast.7, ...), custom_call_target="tpu_custom_call" | custom-call | flops 100000 | bytes 2760708 | tf_op jit(solution)/shard_map/pallas_call | solution.py:29
  4.6 0.0 copy-start.1
  4.6 0.0 copy-start.2
  4.6 4.1 %collective-permute-start = (f32[192,256]{1,0:T(8,128)}, f32[192,256]{1,0:T(8,128)S(1)}, u32[]{:S(2)}, u32[]{:S(2)}) collective-permute-start(f32[192,256]{1,0:T(8,128)} %get-tuple-element.22), channel_id=1, source_target_pairs={{0,1},{1,2},{2,3},{3,4},{4,5},{5,6},{6,7},{7,8},{8,9},{9,10},{10,1... | collective-permute-start | bytes 589832 | tf_op jit(solution)/shard_map/ppermute | solution.py:354
  8.7 1.3 %collective-permute-start.1 = (f32[192,256]{1,0:T(8,128)}, f32[192,256]{1,0:T(8,128)S(1)}, u32[]{:S(2)}, u32[]{:S(2)}) collective-permute-start(f32[192,256]{1,0:T(8,128)} %get-tuple-element.23), channel_id=1, source_target_pairs={{1,0},{2,1},{3,2},{4,3},{5,4},{6,5},{7,6},{8,7},{9,8},{10,9},{11,1... | collective-permute-start | bytes 589832 | tf_op jit(solution)/shard_map/ppermute | solution.py:355
  10.0 14.1 %all_to_all.20.refs_4_ = f32[16,4,128]{2,1,0:T(4,128)S(1)} all-to-all(f32[16,4,128]{2,1,0:T(4,128)} %get-tuple-element.24), channel_id=1, replica_groups=mesh['lon'=32,'lat'=16] {'lat'}, dimensions={0} | all-to-all | bytes 65536 | tf_op jit(solution)/shard_map/all_to_all | solution.py:356
  24.1 0.0 collective-permute-done.refs_2_.refs_5_
  24.1 0.0 collective-permute-done.1.refs_3_.refs_6_
  24.1 0.0 copy-done
  24.1 0.5 shard_map.95
  24.6 0.0 copy-start.4
  24.6 4.2 %collective-permute-start.2 = (f32[192,256]{1,0:T(8,128)S(1)}, f32[192,256]{1,0:T(8,128)S(1)}, u32[]{:S(2)}, u32[]{:S(2)}) collective-permute-start(f32[192,256]{1,0:T(8,128)S(1)} %get-tuple-element.25), channel_id=1, source_target_pairs={{0,16},{16,32},{32,48},{48,64},{64,80},{80,96},{96,112},{112,128},... | collective-permute-start | bytes 589832 | tf_op jit(solution)/shard_map/ppermute | solution.py:363
  28.8 0.0 collective-permute-start.3
  28.8 28.5 %all_to_all.21.refs_8_ = f32[32,2,128]{2,1,0:T(2,128)S(1)} all-to-all(f32[32,2,128]{2,1,0:T(2,128)S(1)} %get-tuple-element.27), channel_id=1, replica_groups=mesh['lon'=32,'lat'=16] {'lon'}, dimensions={0} | all-to-all | bytes 65536 | tf_op jit(solution)/shard_map/all_to_all | solution.py:365
  57.3 0.0 collective-permute-done.2.refs_3_
  57.3 0.0 collective-permute-done.3.refs_4_
  57.3 0.0 copy-done.3
  57.3 0.0 copy-done.1
  57.3 0.0 copy-done.2
  57.4 0.8 shard_map.96
  58.1 1.4 %collective-permute-start.4 = (f32[2,128]{1,0:T(2,128)S(1)}, f32[2,128]{1,0:T(2,128)S(1)}, u32[]{:S(2)}, u32[]{:S(2)}) collective-permute-start(f32[2,128]{1,0:T(2,128)S(1)} %get-tuple-element.30), channel_id=1, source_target_pairs={{0,16},{16,32},{32,48},{48,64},{64,80},{80,96},{96,112},{112,128},... | collective-permute-start | bytes 3080 | tf_op jit(solution)/shard_map/ppermute | solution.py:372
  59.5 0.0 collective-permute-start.5
  59.5 0.7 collective-permute-done.4.refs_5_
  60.2 2.6 %collective-permute-done.5.refs_6_ = f32[2,128]{1,0:T(2,128)S(1)} collective-permute-done((f32[2,128]{1,0:T(2,128)S(1)}, f32[2,128]{1,0:T(2,128)S(1)}, u32[]{:S(2)}, u32[]{:S(2)}) %collective-permute-start.5) | collective-permute-done | bytes 1056 | tf_op jit(solution)/shard_map/ppermute | solution.py:373
  62.8 0.0 copy-done.4
  62.8 0.4 shard_map.97
  63.2 9.3 %all_to_all.22.refs_0_.refs_4_ = f32[16,5,128]{2,1,0:T(8,128)S(1)} all-to-all(f32[16,5,128]{2,1,0:T(8,128)S(1)} %get-tuple-element.33), channel_id=1, replica_groups=mesh['lon'=32,'lat'=16] {'lat'}, dimensions={0} | all-to-all | bytes 81920 | tf_op jit(solution)/shard_map/all_to_all | solution.py:377
  72.5 0.1 shard_map.98
  72.6 16.8 %all_to_all.23.refs_5_ = f32[32,1,128]{2,1,0:T(1,128)S(1)} all-to-all(f32[32,1,128]{2,1,0:T(1,128)S(1)} %shard_map.98), channel_id=1, replica_groups=mesh['lon'=32,'lat'=16] {'lon'}, dimensions={0} | all-to-all | bytes 32768 | tf_op jit(solution)/shard_map/all_to_all | solution.py:379
  89.3 0.9 %shard_map.99 = (f32[224,128]{1,0:T(8,128)}, f32[224,128]{1,0:T(8,128)}, f32[224,128]{1,0:T(8,128)}) custom-call(f32[128,256]{1,0:T(8,128)S(1)} %get-tuple-element.28.refs_0_, f32[128,256]{1,0:T(8,128)S(1)} %get-tuple-element.32.refs_1_, f32[128,256]{1,0:T(8,128)S(1)} %copy-done.1, f32[128,256]{1,0:T(8,128)S(1)} %copy-done.2, ...), custom_call_target="tpu_custom_call" | custom-call | flops 100000 | bytes 581632 | tf_op jit(solution)/shard_map/pallas_call | solution.py:29
Async XLA Ops:
  0.6 23.4 %copy-start = (f32[10,16,16,256]{3,2,1,0:T(8,128)S(1)}, f32[10,16,16,256]{3,2,1,0:T(8,128)}, u32[]{:S(2)}) copy-start(f32[10,16,16,256]{3,2,1,0:T(8,128)} %refs_0_.3) | copy-start | bytes 7864324
  1.4 55.9 %copy-start.3 = (f32[16,8192]{1,0:T(8,128)S(1)}, f32[16,8192]{1,0:T(8,128)}, u32[]{:S(2)}) copy-start(f32[16,8192]{1,0:T(8,128)} %refs_7_.1) | copy-start | bytes 1572868
  4.6 52.8 %copy-start.1 = (f32[128,256]{1,0:T(8,128)S(1)}, f32[128,256]{1,0:T(8,128)}, u32[]{:S(2)}) copy-start(f32[128,256]{1,0:T(8,128)} %get-tuple-element.20.refs_1_.refs_3_.refs_2_) | copy-start | bytes 393220
  4.6 52.8 %copy-start.2 = (f32[128,256]{1,0:T(8,128)S(1)}, f32[128,256]{1,0:T(8,128)}, u32[]{:S(2)}) copy-start(f32[128,256]{1,0:T(8,128)} %get-tuple-element.21.refs_2_.refs_1_.refs_3_) | copy-start | bytes 393220
  4.6 19.5 %collective-permute-start = (f32[192,256]{1,0:T(8,128)}, f32[192,256]{1,0:T(8,128)S(1)}, u32[]{:S(2)}, u32[]{:S(2)}) collective-permute-start(f32[192,256]{1,0:T(8,128)} %get-tuple-element.22), channel_id=1, source_target_pairs={{0,1},{1,2},{2,3},{3,4},{4,5},{5,6},{6,7},{7,8},{8,9},{9,10},{10,1... | collective-permute-start | bytes 589832 | tf_op jit(solution)/shard_map/ppermute | solution.py:354
  8.7 15.4 %collective-permute-start.1 = (f32[192,256]{1,0:T(8,128)}, f32[192,256]{1,0:T(8,128)S(1)}, u32[]{:S(2)}, u32[]{:S(2)}) collective-permute-start(f32[192,256]{1,0:T(8,128)} %get-tuple-element.23), channel_id=1, source_target_pairs={{1,0},{2,1},{3,2},{4,3},{5,4},{6,5},{7,6},{8,7},{9,8},{10,9},{11,1... | collective-permute-start | bytes 589832 | tf_op jit(solution)/shard_map/ppermute | solution.py:355
  24.6 38.2 %copy-start.4 = (f32[128,256]{1,0:T(8,128)S(1)}, f32[128,256]{1,0:T(8,128)}, u32[]{:S(2)}) copy-start(f32[128,256]{1,0:T(8,128)} %get-tuple-element.29.refs_2_) | copy-start | bytes 393220
  24.6 32.7 %collective-permute-start.2 = (f32[192,256]{1,0:T(8,128)S(1)}, f32[192,256]{1,0:T(8,128)S(1)}, u32[]{:S(2)}, u32[]{:S(2)}) collective-permute-start(f32[192,256]{1,0:T(8,128)S(1)} %get-tuple-element.25), channel_id=1, source_target_pairs={{0,16},{16,32},{32,48},{48,64},{64,80},{80,96},{96,112},{112,128},... | collective-permute-start | bytes 589832 | tf_op jit(solution)/shard_map/ppermute | solution.py:363
  28.8 28.5 %collective-permute-start.3 = (f32[192,256]{1,0:T(8,128)S(1)}, f32[192,256]{1,0:T(8,128)S(1)}, u32[]{:S(2)}, u32[]{:S(2)}) collective-permute-start(f32[192,256]{1,0:T(8,128)S(1)} %get-tuple-element.26), channel_id=1, source_target_pairs={{16,0},{32,16},{48,32},{64,48},{80,64},{96,80},{112,96},{128,112},... | collective-permute-start | bytes 589832 | tf_op jit(solution)/shard_map/ppermute | solution.py:364
  58.1 2.1 %collective-permute-start.4 = (f32[2,128]{1,0:T(2,128)S(1)}, f32[2,128]{1,0:T(2,128)S(1)}, u32[]{:S(2)}, u32[]{:S(2)}) collective-permute-start(f32[2,128]{1,0:T(2,128)S(1)} %get-tuple-element.30), channel_id=1, source_target_pairs={{0,16},{16,32},{32,48},{48,64},{64,80},{80,96},{96,112},{112,128},... | collective-permute-start | bytes 3080 | tf_op jit(solution)/shard_map/ppermute | solution.py:372
  59.5 3.3 %collective-permute-start.5 = (f32[2,128]{1,0:T(2,128)S(1)}, f32[2,128]{1,0:T(2,128)S(1)}, u32[]{:S(2)}, u32[]{:S(2)}) collective-permute-start(f32[2,128]{1,0:T(2,128)S(1)} %get-tuple-element.31), channel_id=1, source_target_pairs={{16,0},{32,16},{48,32},{64,48},{80,64},{96,80},{112,96},{128,112},... | collective-permute-start | bytes 3080 | tf_op jit(solution)/shard_map/ppermute | solution.py:373

commit v4 on v3

--- a/solution.py
+++ b/solution.py
@@ -49,9 +49,9 @@
     return hi, mid, low
 
 
-def first_kernel(n_lat, reach_ref, fac_hbm, land_hbm, cell_hbm, value_hbm, weight_hbm, south_ref, north_ref, diag_ref,
-                 rhs_ref, ocean_ref, send_ref, first, last, wide, cell_ref, value_ref, weight_ref, left, right,
-                 sems):
+def first_kernel(n_lat, reach_ref, fac_hbm, land_hbm, cell_hbm, value_hbm, weight_hbm, inverse_hbm, south_ref, north_ref, diag_ref,
+                 rhs_ref, ocean_ref, send_ref, extra_ref, first, last, wide, cell_ref, value_ref, weight_ref, left, right,
+                 inverse_ref, sems):
     moves = (
         (cell_hbm, cell_ref),
         (value_hbm, value_ref),
@@ -59,6 +59,7 @@
         (land_hbm, wide.at[pl.ds(HW, COLS), :]),
         (fac_hbm.at[0], first),
         (fac_hbm.at[BLK + 1], last),
+        (inverse_hbm, inverse_ref),
     )
     copies = [pltpu.make_async_copy(src, dst, sems.at[n]) for n, (src, dst) in enumerate(moves)]
     for copy in copies:
@@ -66,15 +67,8 @@
     me = lax.axis_index("lat")
     wide[0:HW, :] = jnp.zeros((HW, ROWS), jnp.int32)
     wide[HW + COLS : EXT, :] = jnp.zeros((HW, ROWS), jnp.int32)
-    for copy in copies:
+    for copy in copies[:4]:
         copy.wait()
-    edge = iota((TRI, EXT), 1)
-    row = iota((TRI, EXT), 0)
-    q = jnp.where(row < 64, row & 7, row & 15)
-    reach = reach_ref[0, 0]
-    inside = (edge >= HW - reach) & (edge < HW + COLS + reach)
-    north_ref[...] = jnp.where(inside & (q >= HW - reach), tri_rows(lambda p, n: first[p, 0:n, :]), 0.0)
-    south_ref[...] = jnp.where(inside & (q < reach), tri_rows(lambda p, n: last[p, 0:n, :]), 0.0)
     ocean = jnp.transpose(wide[...].astype(F32))
     ocean_ref[...] = ocean
     step = 512
@@ -100,8 +94,8 @@
     for s in range(4):
         band = jnp.sum(rhs[s * 32 : s * 32 + 32], axis=0, keepdims=True)
         pooled = jnp.where((sub >> 2) == s, band, pooled)
-    first = HW + (sub & 3) * 56
-    pooled = jnp.where((lane >= first) & (lane < first + 56), pooled, 0.0)
+    begin = HW + (sub & 3) * 56
+    pooled = jnp.where((lane >= begin) & (lane < begin + 56), pooled, 0.0)
     coarse = jnp.sum(pooled, axis=1, keepdims=True)
     n_row = n_lat * 16 // 128
     placed = jnp.sum(jnp.where(lane == sub + 16 * me, coarse, 0.0), axis=0, keepdims=True)
@@ -111,27 +105,60 @@
         face = jnp.where(p < me, ocean[0:1], ocean[ROWS - 1 : ROWS])
         send_ref[p, n_row : n_row + 1, :] = face[:, 0:128]
         send_ref[p, n_row + 1 : n_row + 2, :] = face[:, 128:256]
-
-
-def side_kernel(n_lon, n_row, reach_ref, fac_ref, from_n_ref, from_s_ref, got_ref, to_e_ref, to_w_ref, send_ref):
+    for copy in copies[4:6]:
+        copy.wait()
+    edge = iota((TRI, EXT), 1)
+    row = iota((TRI, EXT), 0)
+    q = jnp.where(row < 64, row & 7, row & 15)
+    reach = reach_ref[0, 0]
+    inside = (edge >= HW - reach) & (edge < HW + COLS + reach)
+    north_ref[...] = jnp.where(inside & (q >= HW - reach), tri_rows(lambda p, n: first[p, 0:n, :]), 0.0)
+    south_ref[...] = jnp.where(inside & (q < reach), tri_rows(lambda p, n: last[p, 0:n, :]), 0.0)
+    side_lane = iota((16, EXT), 1)
+    for half, face, edge in ((0, 16, 0), (1, 239, 15)):
+        load = jnp.zeros((16, EXT), F32)
+        mask = jnp.zeros((16, EXT), F32)
+        for k in range(BLK):
+            spots = (side_lane == k * 16 + edge) | (side_lane == 160 + k)
+            if k == 0:
+                spots = spots | (side_lane == 128 + edge) | (side_lane == 168)
+            if k == BLK - 1:
+                spots = spots | (side_lane == 144 + edge) | (side_lane == 169)
+            load = jnp.where(spots, rhs[k * 16 : k * 16 + 16, face : face + 1], load)
+            mask = jnp.where(spots, ocean[k * 16 : k * 16 + 16, face : face + 1], mask)
+        extra_ref[half, 0:16, :] = load
+        extra_ref[half, 16:32, :] = mask
+    copies[6].wait()
+    for half in range(2):
+        for m in range(inverse_ref.shape[1] // EXT):
+            for t in range(4):
+                at_row, source = 32 + 4 * m + t, 4 * t + 3 * half
+                extra_ref[half, at_row : at_row + 1, :] = inverse_ref[source : source + 1, m * EXT : (m + 1) * EXT]
+
+
+def side_kernel(n_lon, n_row, reach_ref, fac_ref, from_n_ref, from_s_ref, extra_ref, got_ref, to_e_ref,
+                to_w_ref, send_ref):
     reach = reach_ref[0, 0]
     lane = iota((TRI, 128), 1)
-    east = jnp.zeros((TRI, 128), F32)
-    west = jnp.zeros((TRI, 128), F32)
-    for k in range(BLK):
-        own = (lane >= k * 16) & (lane < k * 16 + 16)
-        hi = tri_rows(lambda p, n: fac_ref[k + 1, p, 0:n, 128:256])
-        lo = tri_rows(lambda p, n: fac_ref[k + 1, p, 0:n, 0:128])
-        east = jnp.where(own & (lane - k * 16 < reach), pltpu.roll(hi, (k * 16 - 112) % 128, 1), east)
-        west = jnp.where(own & (lane - k * 16 >= HW - reach), pltpu.roll(lo, k * 16, 1) if k else lo, west)
-    to_e_ref[:, 0:128] = east
-    to_w_ref[:, 0:128] = west
-    north, south = from_n_ref[:, 128:256], from_s_ref[:, 128:256]
-    to_e_ref[:, 128:256] = jnp.where(
-        lane < 16, pltpu.roll(north, 16, 1), jnp.where(lane < 32, pltpu.roll(south, 32, 1), 0.0)
-    )
-    north, south = from_n_ref[:, 0:128], from_s_ref[:, 0:128]
-    to_w_ref[:, 128:256] = jnp.where(lane < 16, north, jnp.where(lane < 32, pltpu.roll(south, 16, 1), 0.0))
+    for ref, half, face, start in ((to_e_ref, 1, 111, 112), (to_w_ref, 0, 16, 0)):
+        lanes = slice(half * 128, half * 128 + 128)
+        bulk = jnp.zeros((TRI, 128), F32)
+        rest = jnp.zeros((TRI, 128), F32)
+        for k in range(BLK):
+            block = tri_rows(lambda p, n: fac_ref[k + 1, p, 0:n, lanes])
+            at = lane - k * 16
+            own = (at >= 0) & (at < jnp.minimum(reach, 16)) if half else (at >= HW - reach) & (at < 16)
+            shift = (k * 16 - start) % 128
+            bulk = jnp.where(own, pltpu.roll(block, shift, 1) if shift else block, bulk)
+            rest = jnp.where(lane == 32 + k, pltpu.roll(block, (32 + k - face) % 128, 1), rest)
+        north, south = from_n_ref[:, lanes], from_s_ref[:, lanes]
+        rest = jnp.where(lane < 16, pltpu.roll(north, 16, 1) if half else north, rest)
+        rest = jnp.where((lane >= 16) & (lane < 32), pltpu.roll(south, 32 if half else 16, 1), rest)
+        rest = jnp.where(lane == 40, pltpu.roll(north, (40 - face) % 128, 1), rest)
+        rest = jnp.where(lane == 41, pltpu.roll(south, (41 - face) % 128, 1), rest)
+        ref[0:TRI, 0:128] = bulk
+        ref[0:TRI, 128:256] = rest
+        ref[TRI:, :] = extra_ref[half]
     total = jnp.sum(got_ref[:, 0:n_row, :], axis=0)
     for p in range(n_lon):
         send_ref[p] = total
@@ -162,8 +189,9 @@
     return get
 
 
-def solve_kernel(n_lon, n_row, fac_ref, rhs_ref, ocean_ref, from_w_ref, from_e_ref, from_n_ref, from_s_ref,
-                 inverse_ref, coarse_ref, z_ref, face_w_ref, face_e_ref, acc):
+def solve_kernel(n_lat, n_lon, n_row, fac_ref, rhs_ref, ocean_ref, diag_ref, to_w_ref, to_e_ref, from_w_ref, from_e_ref,
+                 from_n_ref, from_s_ref, inverse_ref, got_ref, coarse_ref, z_ref, image_ref, send_ref, acc, z_pad, o_pad):
+    me = lax.axis_index("lat")
     lane = iota((16, 128), 1)
     wide_lane = iota((16, EXT), 1)
     u_w = jnp.zeros((16, 128), F32)
@@ -182,10 +210,15 @@
             lane < 16, pltpu.roll(top, (-at) % 128, 1), jnp.where(lane < 32, pltpu.roll(end, (16 - at) % 128, 1), 0.0)
         )
 
+    ring_w, ring_e = from_w_ref[TRI : TRI + 16, :], from_e_ref[TRI : TRI + 16, :]
     u_w = jnp.concatenate([u_w, corners(top[:, 0:128], end[:, 0:128], 16)], axis=1)
     u_e = jnp.concatenate([u_e, corners(top[:, 128:256], end[:, 128:256], 96)], axis=1)
+    u_w = jnp.where(wide_lane >= 160, ring_w, u_w)
+    u_e = jnp.where(wide_lane >= 160, ring_e, u_e)
     g_w = apply_block(u_w, tri_get(from_w_ref))
     g_e = apply_block(u_e, tri_get(from_e_ref))
+    h_w = apply_block(ring_w, tri_get(to_w_ref))
+    h_e = apply_block(ring_e, tri_get(to_e_ref))
     in_w = (lane >= 16) & (lane < 32)
     in_e = (lane >= 96) & (lane < 112)
     for k in range(BLK):
@@ -202,43 +235,47 @@
         acc[rows, 128:256] += jnp.where(in_e, add_e, 0.0)
     for rows, ref in ((slice(0, 16), from_n_ref), (slice(ROWS - 16, ROWS), from_s_ref)):
         acc[rows, :] += apply_block(rhs_ref[rows, :], tri_get(ref))
-    dot = jnp.zeros((16, 128), F32)
-    for j in range(n_lon):
-        for r in range(n_row):
-            at = (j * n_row + r) * 128
-            dot = dot + inverse_ref[:, at : at + 128] * coarse_ref[j, r : r + 1, :]
+    dot = jnp.zeros((16, EXT), F32)
+    dot_w = jnp.zeros((4, EXT), F32)
+    dot_e = jnp.zeros((4, EXT), F32)
+    for m in range(n_lon * n_row // 2):
+        part = [coarse_ref[n // n_row, n % n_row : n % n_row + 1, :] for n in (2 * m, 2 * m + 1)]
+        part = jnp.concatenate(part, axis=1)
+        dot = dot + inverse_ref[:, m * EXT : (m + 1) * EXT] * part
+        at_row = TRI + 32 + 4 * m
+        dot_w = dot_w + from_w_ref[at_row : at_row + 4, :] * part
+        dot_e = dot_e + from_e_ref[at_row : at_row + 4, :] * part
     answer = jnp.sum(dot, axis=1, keepdims=True)
+    answer_w = jnp.sum(dot_w, axis=1, keepdims=True)
+    answer_e = jnp.sum(dot_e, axis=1, keepdims=True)
     sub = iota((16, EXT), 0)
     first = HW + (sub & 3) * 56
     spread = jnp.where((wide_lane >= first) & (wide_lane < first + 56), answer, 0.0)
-    for s in range(4):
-        rows = slice(s * 32, s * 32 + 32)
+    for k in range(BLK):
+        rows = slice(k * 16, k * 16 + 16)
+        s = k // 2
         band = jnp.sum(jnp.where((sub >> 2) == s, spread, 0.0), axis=0, keepdims=True)
-        z_ref[rows, :] = ocean_ref[rows, :] * (acc[rows, :] + band)
-    z_left = jnp.transpose(z_ref[:, 0:128])
-    z_right = jnp.transpose(z_ref[:, 128:256])
-    o_left = jnp.transpose(ocean_ref[:, 0:128])
-    o_right = jnp.transpose(ocean_ref[:, 128:256])
-    face_w_ref[0:1, :] = z_left[16:17]
-    face_w_ref[1:2, :] = o_left[16:17]
-    face_e_ref[0:1, :] = z_right[111:112]
-    face_e_ref[1:2, :] = o_right[111:112]
-
-
-def image_kernel(n_lat, n_row, z_ref, ocean_ref, diag_ref, rhs_ref, got_ref, from_w_ref, from_e_ref,
-                 image_ref, send_ref):
-    me = lax.axis_index("lat")
-    lane = iota((ROWS, EXT), 1)
+        ocean = ocean_ref[rows, :]
+        z = ocean * (acc[rows, :] + band)
+        z_ref[rows, :] = z
+
+        def edge(g, h, ref, at, answer):
+            ring = h[:, k * 16 + at : k * 16 + at + 1] + g[:, 160 + k : 161 + k]
+            if k == 0:
+                ring = ring + (h[:, 128 + at : 129 + at] + g[:, 168:169])
+            if k == BLK - 1:
+                ring = ring + (h[:, 144 + at : 145 + at] + g[:, 169:170])
+            mask = ref[TRI + 16 : TRI + 32, 160 + k : 161 + k]
+            return mask, mask * (ring + answer[s : s + 1])
+
+        o_w, z_w = edge(g_w, h_w, from_w_ref, 15, answer_w)
+        o_e, z_e = edge(g_e, h_e, from_e_ref, 0, answer_e)
+        z_pad[rows, :] = jnp.where(wide_lane == 15, z_w, jnp.where(wide_lane == 240, z_e, z))
+        o_pad[rows, :] = jnp.where(wide_lane == 15, o_w, jnp.where(wide_lane == 240, o_e, ocean))
+
     row = iota((ROWS, EXT), 0)
     z = z_ref[...]
     ocean = ocean_ref[...]
-
-    def column(ref, n):
-        col = jnp.transpose(jnp.broadcast_to(ref[n : n + 1, :], (128, 128)))
-        return jnp.concatenate([col, col], axis=1)
-
-    def padded(x, n):
-        return jnp.where(lane == 15, column(from_w_ref, n), jnp.where(lane == 240, column(from_e_ref, n), x))
 
     def sides(x):
         return pltpu.roll(x, 1, 1) + pltpu.roll(x, EXT - 1, 1)
@@ -255,8 +292,8 @@
             row == ROWS - 1, south, pltpu.roll(x, ROWS - 1, 0)
         )
 
-    total = sides(padded(ocean, 1)) + rows(ocean, o_north, o_south)
-    beside = sides(padded(z, 0)) + rows(z, 0.0, 0.0)
+    total = sides(o_pad[...]) + rows(ocean, o_north, o_south)
+    beside = sides(z_pad[...]) + rows(z, 0.0, 0.0)
     image = ocean * ((diag_ref[...] + DAMPING) * z + (total * z - beside)) + (1.0 - ocean) * z
     image_ref[...] = image
     affinity = jnp.sum(jnp.sum(rhs_ref[...] * z, axis=0, keepdims=True), axis=1, keepdims=True)
@@ -326,9 +363,10 @@
         return run
 
     slab = (TRI, EXT)
-    to_s, to_n, diag, rhs, ocean, send = call(
+    more = 32 + 4 * coarse_inverse.shape[1] // EXT
+    to_s, to_n, diag, rhs, ocean, send, extra = call(
         k(first_kernel, n_lat),
-        [slab, slab, tile, tile, tile, (n_lat, n_row + 2, 128)],
+        [slab, slab, tile, tile, tile, (n_lat, n_row + 2, 128), (2, more, EXT)],
         (
             intersection,
             factors,
@@ -336,8 +374,9 @@
             obs_cell.reshape(1, OBS),
             obs_value.reshape(1, OBS),
             obs_weight.reshape(1, OBS),
+            coarse_inverse,
         ),
-        places="shhhhh",
+        places="shhhhhh",
         limit=61000,
         scratch=[
             pltpu.VMEM((16, 16, EXT), F32),
@@ -348,31 +387,28 @@
             pltpu.VMEM((1, OBS), F32),
             pltpu.VMEM((6 * ROWS, OBS), jnp.bfloat16),
             pltpu.VMEM((EXT, OBS), jnp.bfloat16),
-            pltpu.SemaphoreType.DMA((6,)),
+            pltpu.VMEM(coarse_inverse.shape, F32),
+            pltpu.SemaphoreType.DMA((7,)),
         ],
     )
     from_n = lax.ppermute(to_s, "lat", line)
     from_s = lax.ppermute(to_n, "lat", up)
     got = lax.all_to_all(send, "lat", 0, 0, tiled=True)
+    message = (TRI + more, EXT)
     to_e, to_w, send = call(
         k(side_kernel, n_lon, n_row),
-        [slab, slab, (n_lon, n_row, 128)],
-        (intersection, factors, from_n, from_s, got),
-        places="svvvv",
+        [message, message, (n_lon, n_row, 128)],
+        (intersection, factors, from_n, from_s, extra, got),
+        places="svvvvv",
     )
     from_w = lax.ppermute(to_e, "lon", ring)
     from_e = lax.ppermute(to_w, "lon", back)
     coarse = lax.all_to_all(send, "lon", 0, 0, tiled=True)
-    z, face_w, face_e = call(
-        k(solve_kernel, n_lon, n_row),
-        [tile, (2, 128), (2, 128)],
-        (factors, rhs, ocean, from_w, from_e, from_n, from_s, coarse_inverse, coarse),
-        scratch=[pltpu.VMEM(tile, F32)],
-    )
-    z_w = lax.ppermute(face_e, "lon", ring)
-    z_e = lax.ppermute(face_w, "lon", back)
-    image, send = call(
-        k(image_kernel, n_lat, n_row), [tile, (n_lat, 5, 128)], (z, ocean, diag, rhs, got, z_w, z_e)
+    z, image, send = call(
+        k(solve_kernel, n_lat, n_lon, n_row),
+        [tile, tile, (n_lat, 5, 128)],
+        (factors, rhs, ocean, diag, to_w, to_e, from_w, from_e, from_n, from_s, coarse_inverse, got, coarse),
+        scratch=[pltpu.VMEM(tile, F32), pltpu.VMEM(tile, F32), pltpu.VMEM(tile, F32)],
     )
     edges = lax.all_to_all(send, "lat", 0, 0, tiled=True)
     (send,) = call(k(cross_kernel, n_lat, n_lon), [(n_lon, 1, 128)], (edges,))

time: 90.6 us -> 86.4 us (0.954)
  waiting for transfers between devices: 3.3 us -> 0.01 us
  blocking collectives: 68.7 us -> 66.8 us
  Pallas kernels: 5.82 us -> 7.16 us
  starting transfers between devices: 10.9 us -> 9.59 us
  local copies, waits for them, and re-layouts: 0.02 us -> 0.99 us
    ppermute x2 -> x0, waiting for transfers between devices: 3.29 us -> none  [the longest x1 2.57 us: body(): z_e = lax.ppermute(face_w, 'lon', back)]
    ppermute x1, starting transfers between devices: 0.01 us -> 2.68 us  [body(): from_e = lax.ppermute(to_w, 'lon', back)]
    ppermute x1, starting transfers between devices: 4.2 us -> 1.55 us  [body(): from_w = lax.ppermute(to_e, 'lon', ring)]
    all_to_all x1, blocking collectives: 28.5 us -> 26.3 us  [body(): coarse = lax.all_to_all(send, 'lon', 0, 0, tiled=True)]
    ppermute x2 -> x0, starting transfers between devices: 1.36 us -> none  [the longest x1 1.35 us: body(): z_w = lax.ppermute(face_e, 'lon', ring)]
    pallas_call x6 -> x5, Pallas kernels: 5.82 us -> 7.16 us  [call(): pl.pallas_call(kernel, out_shape=[jax.ShapeDtypeStruct(s, F32) for s in o...]
    unnamed x10 -> x12, local copies, waits for them, and re-layouts: 0.02 us -> 0.99 us
  transfers between devices with their start and end apart: 6 -> 4, of which waited for: 2 -> 0; matrix products, arithmetic and copies ran while one was open for 0% -> 0% of each run, Pallas kernels for 0% -> 0%
where the time goes in v4:
time: 86.4 us; the launch traced here: 86.1 us
  blocking collectives  66.8 us (77%)
  starting transfers between devices  9.59 us (11%)
  Pallas kernels  7.16 us (8%)
  between operations  1.54 us (2%)
  local copies, waits for them, and re-layouts  0.99 us (1%)
    all_to_all x1, blocking collectives, body(): coarse = lax.all_to_all(send, 'lon', 0, 0, tiled=True)  26.3 us
    all_to_all x1, blocking collectives, body(): sums = lax.all_to_all(send, 'lon', 0, 0, tiled=True)  17.1 us
    all_to_all x1, blocking collectives, body(): got = lax.all_to_all(send, 'lat', 0, 0, tiled=True)  14.1 us
    all_to_all x1, blocking collectives, body(): edges = lax.all_to_all(send, 'lat', 0, 0, tiled=True)  9.3 us
    pallas_call x5, Pallas kernels, call(): pl.pallas_call(kernel, out_shape=[jax.ShapeDtypeStruct(s, F32) for s in o...  7.16 us
    ppermute x1, starting transfers between devices, body(): from_n = lax.ppermute(to_s, 'lat', line)  4.08 us
    ppermute x1, starting transfers between devices, body(): from_e = lax.ppermute(to_w, 'lon', back)  2.68 us
  transfers between devices with their start and end apart: 4, of which 0 were waited for; matrix products, arithmetic and copies ran while one was open for 0% of the time, Pallas kernels for 0%

profile of v4, /device:TPU:1, one launch (start us, length us, event | category | flops | bytes accessed | tf_op | source)
XLA Modules:
  0.0 86.1 jit_solution(3498823518545393915)
XLA Ops:
  0.6 0.0 copy-start
  1.4 0.0 copy-start.1
  1.4 3.5 %shard_map.94 = (f32[192,256]{1,0:T(8,128)}, f32[192,256]{1,0:T(8,128)}, f32[128,256]{1,0:T(8,128)}, f32[128,256]{1,0:T(8,128)}, f32[128,256]{1,0:T(8,128)}, /*i...) custom-call(s32[1,1]{1,0:T(1,128)S(6)} %copy.10.refs_0_, f32[10,16,16,256]{3,2,1,0:T(8,128)} %refs_0_.3, s32[224,128]{1,0:T(8,128)} %bitcast.7, ...), custom_call_target="tpu_custom_call" | custom-call | flops 100000 | bytes 3284996 | tf_op jit(solution)/shard_map/pallas_call | solution.py:29
  4.9 0.0 copy-start.2
  4.9 0.0 copy-start.3
  4.9 4.1 %collective-permute-start = (f32[192,256]{1,0:T(8,128)}, f32[192,256]{1,0:T(8,128)S(1)}, u32[]{:S(2)}, u32[]{:S(2)}) collective-permute-start(f32[192,256]{1,0:T(8,128)} %get-tuple-element.22), channel_id=1, source_target_pairs={{0,1},{1,2},{2,3},{3,4},{4,5},{5,6},{6,7},{7,8},{8,9},{9,10},{10,1... | collective-permute-start | bytes 589832 | tf_op jit(solution)/shard_map/ppermute | solution.py:394
  9.0 1.3 %collective-permute-start.1 = (f32[192,256]{1,0:T(8,128)}, f32[192,256]{1,0:T(8,128)S(1)}, u32[]{:S(2)}, u32[]{:S(2)}) collective-permute-start(f32[192,256]{1,0:T(8,128)} %get-tuple-element.23), channel_id=1, source_target_pairs={{1,0},{2,1},{3,2},{4,3},{5,4},{6,5},{7,6},{8,7},{9,8},{10,9},{11,1... | collective-permute-start | bytes 589832 | tf_op jit(solution)/shard_map/ppermute | solution.py:395
  10.3 14.1 %all_to_all.20.refs_5_.refs_11_ = f32[16,4,128]{2,1,0:T(4,128)S(1)} all-to-all(f32[16,4,128]{2,1,0:T(4,128)} %get-tuple-element.25), channel_id=1, replica_groups=mesh['lon'=32,'lat'=16] {'lat'}, dimensions={0} | all-to-all | bytes 65536 | tf_op jit(solution)/shard_map/all_to_all | solution.py:396
  24.4 0.0 collective-permute-done.refs_2_.refs_8_
  24.4 0.0 collective-permute-done.1.refs_3_.refs_9_
  24.4 0.0 copy-done
  24.4 0.0 copy-start.4
  24.4 1.0 %copy-done.4 = f32[2,160,256]{2,1,0:T(8,128)S(1)} copy-done((f32[2,160,256]{2,1,0:T(8,128)S(1)}, f32[2,160,256]{2,1,0:T(8,128)}, u32[]{:S(2)}) %copy-start.4) | copy-done | bytes 327704
  25.4 0.0 copy-start.5
  25.4 1.1 %shard_map.95 = (f32[352,256]{1,0:T(8,128)S(1)}, f32[352,256]{1,0:T(8,128)S(1)}, f32[32,2,128]{2,1,0:T(2,128)S(1)}) custom-call(s32[1,1]{1,0:T(1,128)S(6)} %copy.10.refs_0_, f32[10,16,16,256]{3,2,1,0:T(8,128)S(1)} %copy-done, f32[192,256]{1,0:T(8,128)S(1)} %collective-permute-done.refs_2_.refs_8_, f32[192,256]{1,0:T(8,128)S(1)} %collective-permute-done.1.refs_3_.refs_9_, ...), custom_call_target="tpu_custom_call" | custom-call | flops 100000 | bytes 3375108 | tf_op jit(solution)/shard_map/pallas_call | solution.py:29
  26.5 2.7 %collective-permute-start.3 = (f32[352,256]{1,0:T(8,128)S(1)}, f32[352,256]{1,0:T(8,128)S(1)}, u32[]{:S(2)}, u32[]{:S(2)}) collective-permute-start(f32[352,256]{1,0:T(8,128)S(1)} %get-tuple-element.26.refs_4_), channel_id=1, source_target_pairs={{16,0},{32,16},{48,32},{64,48},{80,64},{96,80},{112,96},{128,112},... | collective-permute-start | bytes 1081352 | tf_op jit(solution)/shard_map/ppermute | solution.py:405
  29.2 1.5 %collective-permute-start.2 = (f32[352,256]{1,0:T(8,128)S(1)}, f32[352,256]{1,0:T(8,128)S(1)}, u32[]{:S(2)}, u32[]{:S(2)}) collective-permute-start(f32[352,256]{1,0:T(8,128)S(1)} %get-tuple-element.27.refs_5_), channel_id=1, source_target_pairs={{0,16},{16,32},{32,48},{48,64},{64,80},{80,96},{96,112},{112,128},... | collective-permute-start | bytes 1081352 | tf_op jit(solution)/shard_map/ppermute | solution.py:404
  30.7 26.3 %all_to_all.21.refs_12_ = f32[32,2,128]{2,1,0:T(2,128)S(1)} all-to-all(f32[32,2,128]{2,1,0:T(2,128)S(1)} %get-tuple-element.28), channel_id=1, replica_groups=mesh['lon'=32,'lat'=16] {'lon'}, dimensions={0} | all-to-all | bytes 65536 | tf_op jit(solution)/shard_map/all_to_all | solution.py:406
  57.0 0.0 collective-permute-done.3.refs_7_
  57.0 0.0 collective-permute-done.2.refs_6_
  57.0 0.0 copy-done.1
  57.0 0.0 copy-done.2
  57.0 0.0 copy-done.3
  57.0 0.0 copy-done.5
  57.1 1.6 %shard_map.96 = (f32[128,256]{1,0:T(8,128)S(1)}, f32[128,256]{1,0:T(8,128)S(1)}, f32[16,5,128]{2,1,0:T(8,128)S(1)}) custom-call(f32[10,16,16,256]{3,2,1,0:T(8,128)S(1)} %copy-done, f32[128,256]{1,0:T(8,128)S(1)} %copy-done.2, f32[128,256]{1,0:T(8,128)S(1)} %copy-done.3, f32[128,256]{1,0:T(8,128)S(1)} %copy-done.5, f32[352,256]{1,0:T(8,128)S(1)} %get-tuple-element.26.refs_4_, ...), custom_call_target="tpu_custom_call" | custom-call | flops 100000 | bytes 5439488 | tf_op jit(solution)/shard_map/pallas_call | solution.py:29
  58.6 9.3 %all_to_all.22.refs_0_.refs_4_ = f32[16,5,128]{2,1,0:T(8,128)S(1)} all-to-all(f32[16,5,128]{2,1,0:T(8,128)S(1)} %get-tuple-element.31), channel_id=1, replica_groups=mesh['lon'=32,'lat'=16] {'lat'}, dimensions={0} | all-to-all | bytes 81920 | tf_op jit(solution)/shard_map/all_to_all | solution.py:413
  67.9 0.1 shard_map.97
  68.0 17.1 %all_to_all.23.refs_5_ = f32[32,1,128]{2,1,0:T(1,128)S(1)} all-to-all(f32[32,1,128]{2,1,0:T(1,128)S(1)} %shard_map.97), channel_id=1, replica_groups=mesh['lon'=32,'lat'=16] {'lon'}, dimensions={0} | all-to-all | bytes 32768 | tf_op jit(solution)/shard_map/all_to_all | solution.py:415
  85.1 0.9 %shard_map.98 = (f32[224,128]{1,0:T(8,128)}, f32[224,128]{1,0:T(8,128)}, f32[224,128]{1,0:T(8,128)}) custom-call(f32[128,256]{1,0:T(8,128)S(1)} %get-tuple-element.29.refs_0_, f32[128,256]{1,0:T(8,128)S(1)} %get-tuple-element.30.refs_1_, f32[128,256]{1,0:T(8,128)S(1)} %copy-done.2, f32[128,256]{1,0:T(8,128)S(1)} %copy-done.3, ...), custom_call_target="tpu_custom_call" | custom-call | flops 100000 | bytes 581632 | tf_op jit(solution)/shard_map/pallas_call | solution.py:29
Async XLA Ops:
  0.6 23.8 %copy-start = (f32[10,16,16,256]{3,2,1,0:T(8,128)S(1)}, f32[10,16,16,256]{3,2,1,0:T(8,128)}, u32[]{:S(2)}) copy-start(f32[10,16,16,256]{3,2,1,0:T(8,128)} %refs_0_.3) | copy-start | bytes 7864324
  1.4 55.6 %copy-start.1 = (f32[16,8192]{1,0:T(8,128)S(1)}, f32[16,8192]{1,0:T(8,128)}, u32[]{:S(2)}) copy-start(f32[16,8192]{1,0:T(8,128)} %refs_10_.1) | copy-start | bytes 1572868
  4.9 52.1 %copy-start.2 = (f32[128,256]{1,0:T(8,128)S(1)}, f32[128,256]{1,0:T(8,128)}, u32[]{:S(2)}) copy-start(f32[128,256]{1,0:T(8,128)} %get-tuple-element.19.refs_1_.refs_2_) | copy-start | bytes 393220
  4.9 52.1 %copy-start.3 = (f32[128,256]{1,0:T(8,128)S(1)}, f32[128,256]{1,0:T(8,128)}, u32[]{:S(2)}) copy-start(f32[128,256]{1,0:T(8,128)} %get-tuple-element.20.refs_2_.refs_3_) | copy-start | bytes 393220
  4.9 19.5 %collective-permute-start = (f32[192,256]{1,0:T(8,128)}, f32[192,256]{1,0:T(8,128)S(1)}, u32[]{:S(2)}, u32[]{:S(2)}) collective-permute-start(f32[192,256]{1,0:T(8,128)} %get-tuple-element.22), channel_id=1, source_target_pairs={{0,1},{1,2},{2,3},{3,4},{4,5},{5,6},{6,7},{7,8},{8,9},{9,10},{10,1... | collective-permute-start | bytes 589832 | tf_op jit(solution)/shard_map/ppermute | solution.py:394
  9.0 15.4 %collective-permute-start.1 = (f32[192,256]{1,0:T(8,128)}, f32[192,256]{1,0:T(8,128)S(1)}, u32[]{:S(2)}, u32[]{:S(2)}) collective-permute-start(f32[192,256]{1,0:T(8,128)} %get-tuple-element.23), channel_id=1, source_target_pairs={{1,0},{2,1},{3,2},{4,3},{5,4},{6,5},{7,6},{8,7},{9,8},{10,9},{11,1... | collective-permute-start | bytes 589832 | tf_op jit(solution)/shard_map/ppermute | solution.py:395
  24.4 1.0 %copy-start.4 = (f32[2,160,256]{2,1,0:T(8,128)S(1)}, f32[2,160,256]{2,1,0:T(8,128)}, u32[]{:S(2)}) copy-start(f32[2,160,256]{2,1,0:T(8,128)} %get-tuple-element.24.refs_4_) | copy-start | bytes 983044
  25.4 31.7 %copy-start.5 = (f32[128,256]{1,0:T(8,128)S(1)}, f32[128,256]{1,0:T(8,128)}, u32[]{:S(2)}) copy-start(f32[128,256]{1,0:T(8,128)} %get-tuple-element.21.refs_3_) | copy-start | bytes 393220
  26.5 30.5 %collective-permute-start.3 = (f32[352,256]{1,0:T(8,128)S(1)}, f32[352,256]{1,0:T(8,128)S(1)}, u32[]{:S(2)}, u32[]{:S(2)}) collective-permute-start(f32[352,256]{1,0:T(8,128)S(1)} %get-tuple-element.26.refs_4_), channel_id=1, source_target_pairs={{16,0},{32,16},{48,32},{64,48},{80,64},{96,80},{112,96},{128,112},... | collective-permute-start | bytes 1081352 | tf_op jit(solution)/shard_map/ppermute | solution.py:405
  29.2 27.9 %collective-permute-start.2 = (f32[352,256]{1,0:T(8,128)S(1)}, f32[352,256]{1,0:T(8,128)S(1)}, u32[]{:S(2)}, u32[]{:S(2)}) collective-permute-start(f32[352,256]{1,0:T(8,128)S(1)} %get-tuple-element.27.refs_5_), channel_id=1, source_target_pairs={{0,16},{16,32},{32,48},{48,64},{64,80},{80,96},{96,112},{112,128},... | collective-permute-start | bytes 1081352 | tf_op jit(solution)/shard_map/ppermute | solution.py:404

commit v5 on v4

--- a/solution.py
+++ b/solution.py
@@ -369,15 +369,20 @@
         [slab, slab, tile, tile, tile, (n_lat, n_row + 2, 128), (2, more, EXT)],
         (
             intersection,
-            factors,
-            land_sea.T,
-            obs_cell.reshape(1, OBS),
-            obs_value.reshape(1, OBS),
-            obs_weight.reshape(1, OBS),
-            coarse_inverse,
+            *(
+                pltpu.with_memory_space_constraint(x, pltpu.HBM)
+                for x in (
+                    factors,
+                    land_sea.T,
+                    obs_cell.reshape(1, OBS),
+                    obs_value.reshape(1, OBS),
+                    obs_weight.reshape(1, OBS),
+                    coarse_inverse,
+                )
+            ),
         ),
         places="shhhhhh",
-        limit=61000,
+        limit=16384,
         scratch=[
             pltpu.VMEM((16, 16, EXT), F32),
             pltpu.VMEM((16, 16, EXT), F32),

time: 86.4 us -> 84 us (0.972)
  Pallas kernels: 7.16 us -> 6.13 us
  local copies, waits for them, and re-layouts: 0.99 us -> 0.01 us
    pallas_call x5, Pallas kernels: 7.16 us -> 6.13 us  [call(): pl.pallas_call(kernel, out_shape=[jax.ShapeDtypeStruct(s, F32) for s in o...]
    unnamed x12 -> x4, local copies, waits for them, and re-layouts: 0.99 us -> 0.01 us
where the time goes in v5:
time: 84 us; the launch traced here: 83.7 us
  blocking collectives  66.6 us (79%)
  starting transfers between devices  9.46 us (11%)
  Pallas kernels  6.13 us (7%)
  between operations  1.49 us (2%)
    all_to_all x1, blocking collectives, body(): coarse = lax.all_to_all(send, 'lon', 0, 0, tiled=True)  26.3 us
    all_to_all x1, blocking collectives, body(): sums = lax.all_to_all(send, 'lon', 0, 0, tiled=True)  17.1 us
    all_to_all x1, blocking collectives, body(): got = lax.all_to_all(send, 'lat', 0, 0, tiled=True)  13.9 us
    all_to_all x1, blocking collectives, body(): edges = lax.all_to_all(send, 'lat', 0, 0, tiled=True)  9.3 us
    pallas_call x5, Pallas kernels, call(): pl.pallas_call(kernel, out_shape=[jax.ShapeDtypeStruct(s, F32) for s in o...  6.13 us
    ppermute x1, starting transfers between devices, body(): from_n = lax.ppermute(to_s, 'lat', line)  3.95 us
    ppermute x1, starting transfers between devices, body(): from_e = lax.ppermute(to_w, 'lon', back)  2.68 us
  transfers between devices with their start and end apart: 4, of which 0 were waited for; matrix products, arithmetic and copies ran while one was open for 0% of the time, Pallas kernels for 0%

profile of v5, /device:TPU:1, one launch (start us, length us, event | category | flops | bytes accessed | tf_op | source)
XLA Modules:
  0.0 83.7 jit_solution(16067903037925490827)
XLA Ops:
  0.6 0.0 copy-start
  1.4 0.0 copy-start.1
  1.4 2.5 %shard_map.94 = (f32[192,256]{1,0:T(8,128)S(1)}, f32[192,256]{1,0:T(8,128)S(1)}, f32[128,256]{1,0:T(8,128)S(1)}, f32[128,256]{1,0:T(8,128)S(1)}, f32[128,256]{1,...) custom-call(s32[1,1]{1,0:T(1,128)S(6)} %copy.10.refs_0_, f32[10,16,16,256]{3,2,1,0:T(8,128)} %refs_0_.3, ...), custom_call_target="tpu_custom_call" | custom-call | flops 100000 | bytes 3284996 | tf_op jit(solution)/shard_map/pallas_call | solution.py:29
  3.9 3.9 %collective-permute-start = (f32[192,256]{1,0:T(8,128)S(1)}, f32[192,256]{1,0:T(8,128)S(1)}, u32[]{:S(2)}, u32[]{:S(2)}) collective-permute-start(f32[192,256]{1,0:T(8,128)S(1)} %get-tuple-element.22), channel_id=1, source_target_pairs={{0,1},{1,2},{2,3},{3,4},{4,5},{5,6},{6,7},{7,8},{8,9},{9,10},{10,1... | collective-permute-start | bytes 589832 | tf_op jit(solution)/shard_map/ppermute | solution.py:399
  7.9 1.3 %collective-permute-start.1 = (f32[192,256]{1,0:T(8,128)S(1)}, f32[192,256]{1,0:T(8,128)S(1)}, u32[]{:S(2)}, u32[]{:S(2)}) collective-permute-start(f32[192,256]{1,0:T(8,128)S(1)} %get-tuple-element.23), channel_id=1, source_target_pairs={{1,0},{2,1},{3,2},{4,3},{5,4},{6,5},{7,6},{8,7},{9,8},{10,9},{11,1... | collective-permute-start | bytes 589832 | tf_op jit(solution)/shard_map/ppermute | solution.py:400
  9.2 13.9 %all_to_all.20.refs_5_.refs_11_ = f32[16,4,128]{2,1,0:T(4,128)S(1)} all-to-all(f32[16,4,128]{2,1,0:T(4,128)S(1)} %get-tuple-element.25), channel_id=1, replica_groups=mesh['lon'=32,'lat'=16] {'lat'}, dimensions={0} | all-to-all | bytes 65536 | tf_op jit(solution)/shard_map/all_to_all | solution.py:401
  23.1 0.0 collective-permute-done.refs_2_.refs_8_
  23.1 0.0 collective-permute-done.1.refs_3_.refs_9_
  23.1 0.0 copy-done
  23.1 1.1 %shard_map.95 = (f32[352,256]{1,0:T(8,128)S(1)}, f32[352,256]{1,0:T(8,128)S(1)}, f32[32,2,128]{2,1,0:T(2,128)S(1)}) custom-call(s32[1,1]{1,0:T(1,128)S(6)} %copy.10.refs_0_, f32[10,16,16,256]{3,2,1,0:T(8,128)S(1)} %copy-done, f32[192,256]{1,0:T(8,128)S(1)} %collective-permute-done.refs_2_.refs_8_, f32[192,256]{1,0:T(8,128)S(1)} %collective-permute-done.1.refs_3_.refs_9_, ...), custom_call_target="tpu_custom_call" | custom-call | flops 100000 | bytes 3375108 | tf_op jit(solution)/shard_map/pallas_call | solution.py:29
  24.2 2.7 %collective-permute-start.3 = (f32[352,256]{1,0:T(8,128)S(1)}, f32[352,256]{1,0:T(8,128)S(1)}, u32[]{:S(2)}, u32[]{:S(2)}) collective-permute-start(f32[352,256]{1,0:T(8,128)S(1)} %get-tuple-element.26.refs_4_), channel_id=1, source_target_pairs={{16,0},{32,16},{48,32},{64,48},{80,64},{96,80},{112,96},{128,112},... | collective-permute-start | bytes 1081352 | tf_op jit(solution)/shard_map/ppermute | solution.py:410
  26.8 1.5 %collective-permute-start.2 = (f32[352,256]{1,0:T(8,128)S(1)}, f32[352,256]{1,0:T(8,128)S(1)}, u32[]{:S(2)}, u32[]{:S(2)}) collective-permute-start(f32[352,256]{1,0:T(8,128)S(1)} %get-tuple-element.27.refs_5_), channel_id=1, source_target_pairs={{0,16},{16,32},{32,48},{48,64},{64,80},{80,96},{96,112},{112,128},... | collective-permute-start | bytes 1081352 | tf_op jit(solution)/shard_map/ppermute | solution.py:409
  28.4 26.3 %all_to_all.21.refs_12_ = f32[32,2,128]{2,1,0:T(2,128)S(1)} all-to-all(f32[32,2,128]{2,1,0:T(2,128)S(1)} %get-tuple-element.28), channel_id=1, replica_groups=mesh['lon'=32,'lat'=16] {'lon'}, dimensions={0} | all-to-all | bytes 65536 | tf_op jit(solution)/shard_map/all_to_all | solution.py:411
  54.7 0.0 collective-permute-done.3.refs_7_
  54.7 0.0 collective-permute-done.2.refs_6_
  54.7 0.0 copy-done.1
  54.7 1.5 %shard_map.96 = (f32[128,256]{1,0:T(8,128)S(1)}, f32[128,256]{1,0:T(8,128)S(1)}, f32[16,5,128]{2,1,0:T(8,128)S(1)}) custom-call(f32[10,16,16,256]{3,2,1,0:T(8,128)S(1)} %copy-done, f32[128,256]{1,0:T(8,128)S(1)} %get-tuple-element.19.refs_1_.refs_2_, f32[128,256]{1,0:T(8,128)S(1)} %get-tuple-element.20.refs_2_.refs_3_, ...), custom_call_target="tpu_custom_call" | custom-call | flops 100000 | bytes 5439488 | tf_op jit(solution)/shard_map/pallas_call | solution.py:29
  56.2 9.3 %all_to_all.22.refs_0_.refs_4_ = f32[16,5,128]{2,1,0:T(8,128)S(1)} all-to-all(f32[16,5,128]{2,1,0:T(8,128)S(1)} %get-tuple-element.31), channel_id=1, replica_groups=mesh['lon'=32,'lat'=16] {'lat'}, dimensions={0} | all-to-all | bytes 81920 | tf_op jit(solution)/shard_map/all_to_all | solution.py:418
  65.5 0.1 shard_map.97
  65.6 17.1 %all_to_all.23.refs_5_ = f32[32,1,128]{2,1,0:T(1,128)S(1)} all-to-all(f32[32,1,128]{2,1,0:T(1,128)S(1)} %shard_map.97), channel_id=1, replica_groups=mesh['lon'=32,'lat'=16] {'lon'}, dimensions={0} | all-to-all | bytes 32768 | tf_op jit(solution)/shard_map/all_to_all | solution.py:420
  82.7 0.9 %shard_map.98 = (f32[224,128]{1,0:T(8,128)}, f32[224,128]{1,0:T(8,128)}, f32[224,128]{1,0:T(8,128)}) custom-call(f32[128,256]{1,0:T(8,128)S(1)} %get-tuple-element.29.refs_0_, f32[128,256]{1,0:T(8,128)S(1)} %get-tuple-element.30.refs_1_, f32[128,256]{1,0:T(8,128)S(1)} %get-tuple-element.19.refs_1_.refs_2_, f32[128,256]{1,0:T(8,128)S(1)} %get-tuple-element.20.refs_2_.refs_3_, ...), custom_call_target="tpu_custom_call" | custom-call | flops 100000 | bytes 581632 | tf_op jit(solution)/shard_map/pallas_call | solution.py:29
Async XLA Ops:
  0.6 22.4 %copy-start = (f32[10,16,16,256]{3,2,1,0:T(8,128)S(1)}, f32[10,16,16,256]{3,2,1,0:T(8,128)}, u32[]{:S(2)}) copy-start(f32[10,16,16,256]{3,2,1,0:T(8,128)} %refs_0_.3) | copy-start | bytes 7864324
  1.4 53.3 %copy-start.1 = (f32[16,8192]{1,0:T(8,128)S(1)}, f32[16,8192]{1,0:T(8,128)}, u32[]{:S(2)}) copy-start(f32[16,8192]{1,0:T(8,128)} %refs_10_.1) | copy-start | bytes 1572868
  3.9 19.1 %collective-permute-start = (f32[192,256]{1,0:T(8,128)S(1)}, f32[192,256]{1,0:T(8,128)S(1)}, u32[]{:S(2)}, u32[]{:S(2)}) collective-permute-start(f32[192,256]{1,0:T(8,128)S(1)} %get-tuple-element.22), channel_id=1, source_target_pairs={{0,1},{1,2},{2,3},{3,4},{4,5},{5,6},{6,7},{7,8},{8,9},{9,10},{10,1... | collective-permute-start | bytes 589832 | tf_op jit(solution)/shard_map/ppermute | solution.py:399
  7.9 15.2 %collective-permute-start.1 = (f32[192,256]{1,0:T(8,128)S(1)}, f32[192,256]{1,0:T(8,128)S(1)}, u32[]{:S(2)}, u32[]{:S(2)}) collective-permute-start(f32[192,256]{1,0:T(8,128)S(1)} %get-tuple-element.23), channel_id=1, source_target_pairs={{1,0},{2,1},{3,2},{4,3},{5,4},{6,5},{7,6},{8,7},{9,8},{10,9},{11,1... | collective-permute-start | bytes 589832 | tf_op jit(solution)/shard_map/ppermute | solution.py:400
  24.2 30.5 %collective-permute-start.3 = (f32[352,256]{1,0:T(8,128)S(1)}, f32[352,256]{1,0:T(8,128)S(1)}, u32[]{:S(2)}, u32[]{:S(2)}) collective-permute-start(f32[352,256]{1,0:T(8,128)S(1)} %get-tuple-element.26.refs_4_), channel_id=1, source_target_pairs={{16,0},{32,16},{48,32},{64,48},{80,64},{96,80},{112,96},{128,112},... | collective-permute-start | bytes 1081352 | tf_op jit(solution)/shard_map/ppermute | solution.py:410
  26.8 27.9 %collective-permute-start.2 = (f32[352,256]{1,0:T(8,128)S(1)}, f32[352,256]{1,0:T(8,128)S(1)}, u32[]{:S(2)}, u32[]{:S(2)}) collective-permute-start(f32[352,256]{1,0:T(8,128)S(1)} %get-tuple-element.27.refs_5_), channel_id=1, source_target_pairs={{0,16},{16,32},{32,48},{48,64},{64,80},{80,96},{96,112},{112,128},... | collective-permute-start | bytes 1081352 | tf_op jit(solution)/shard_map/ppermute | solution.py:409

commit v6 on v5

--- a/solution.py
+++ b/solution.py
@@ -11,6 +11,7 @@
 BLK = 8
 TRI = 192
 OBS = 2048
+RING = ([170] + [144 + 16 * k for k in range(1, 7)] + [171], [255, 170, 171] + [127 + 16 * k for k in range(3, 8)])
 
 VM = pl.BlockSpec(memory_space=pltpu.VMEM)
 PLACES = {
@@ -97,14 +98,12 @@
     begin = HW + (sub & 3) * 56
     pooled = jnp.where((lane >= begin) & (lane < begin + 56), pooled, 0.0)
     coarse = jnp.sum(pooled, axis=1, keepdims=True)
-    n_row = n_lat * 16 // 128
-    placed = jnp.sum(jnp.where(lane == sub + 16 * me, coarse, 0.0), axis=0, keepdims=True)
+    spare = jnp.sum(jnp.where(lane == sub, coarse, 0.0), axis=0, keepdims=True)
+    edge_lane = iota((1, EXT), 1)
     for p in range(n_lat):
-        for r in range(n_row):
-            send_ref[p, r : r + 1, :] = placed[:, r * 128 : (r + 1) * 128]
-        face = jnp.where(p < me, ocean[0:1], ocean[ROWS - 1 : ROWS])
-        send_ref[p, n_row : n_row + 1, :] = face[:, 0:128]
-        send_ref[p, n_row + 1 : n_row + 2, :] = face[:, 128:256]
+        face = jnp.where(edge_lane < HW, spare, jnp.where(p < me, ocean[0:1], ocean[ROWS - 1 : ROWS]))
+        send_ref[p, 0:1, :] = face[:, 0:128]
+        send_ref[p, 1:2, :] = face[:, 128:256]
     for copy in copies[4:6]:
         copy.wait()
     edge = iota((TRI, EXT), 1)
@@ -119,7 +118,7 @@
         load = jnp.zeros((16, EXT), F32)
         mask = jnp.zeros((16, EXT), F32)
         for k in range(BLK):
-            spots = (side_lane == k * 16 + edge) | (side_lane == 160 + k)
+            spots = (side_lane == k * 16 + edge) | (side_lane == RING[half][k])
             if k == 0:
                 spots = spots | (side_lane == 128 + edge) | (side_lane == 168)
             if k == BLK - 1:
@@ -149,8 +148,12 @@
             at = lane - k * 16
             own = (at >= 0) & (at < jnp.minimum(reach, 16)) if half else (at >= HW - reach) & (at < 16)
             shift = (k * 16 - start) % 128
-            bulk = jnp.where(own, pltpu.roll(block, shift, 1) if shift else block, bulk)
-            rest = jnp.where(lane == 32 + k, pltpu.roll(block, (32 + k - face) % 128, 1), rest)
+            moved = pltpu.roll(block, shift, 1) if shift else block
+            bulk = jnp.where(own, moved, bulk)
+            ring = RING[half][k] - 128
+            if (face + shift) % 128 != ring:
+                moved = pltpu.roll(block, (ring - face) % 128, 1)
+            rest = jnp.where(lane == ring, moved, rest)
         north, south = from_n_ref[:, lanes], from_s_ref[:, lanes]
         rest = jnp.where(lane < 16, pltpu.roll(north, 16, 1) if half else north, rest)
         rest = jnp.where((lane >= 16) & (lane < 32), pltpu.roll(south, 32 if half else 16, 1), rest)
@@ -159,9 +162,15 @@
         ref[0:TRI, 0:128] = bulk
         ref[0:TRI, 128:256] = rest
         ref[TRI:, :] = extra_ref[half]
-    total = jnp.sum(got_ref[:, 0:n_row, :], axis=0)
+    small = iota((1, 128), 1)
+    total = [jnp.zeros((1, 128), F32) for _ in range(n_row)]
+    for p in range(n_row * 8):
+        at = p * 16 % 128
+        part = pltpu.roll(got_ref[p, 0:1, :], at, 1) if at else got_ref[p, 0:1, :]
+        total[p // 8] = jnp.where((small >= at) & (small < at + 16), part, total[p // 8])
     for p in range(n_lon):
-        send_ref[p] = total
+        for r in range(n_row):
+            send_ref[p, r : r + 1, :] = total[r]
 
 
 def apply_block(u, get):
@@ -217,8 +226,12 @@
     u_e = jnp.where(wide_lane >= 160, ring_e, u_e)
     g_w = apply_block(u_w, tri_get(from_w_ref))
     g_e = apply_block(u_e, tri_get(from_e_ref))
-    h_w = apply_block(ring_w, tri_get(to_w_ref))
-    h_e = apply_block(ring_e, tri_get(to_e_ref))
+    own_w, own_e = tri_get(to_w_ref), tri_get(to_e_ref)
+
+    def own_get(p, n):
+        return jnp.where((wide_lane[0:n] & 15) == 0, own_e(p, n), own_w(p, n))
+
+    h = apply_block(jnp.where((wide_lane & 15) == 0, ring_e, ring_w), own_get)
     in_w = (lane >= 16) & (lane < 32)
     in_e = (lane >= 96) & (lane < 112)
     for k in range(BLK):
@@ -259,17 +272,17 @@
         z = ocean * (acc[rows, :] + band)
         z_ref[rows, :] = z
 
-        def edge(g, h, ref, at, answer):
-            ring = h[:, k * 16 + at : k * 16 + at + 1] + g[:, 160 + k : 161 + k]
+        def edge(g, ref, at, spot, answer):
+            ring = h[:, k * 16 + at : k * 16 + at + 1] + g[:, spot : spot + 1]
             if k == 0:
                 ring = ring + (h[:, 128 + at : 129 + at] + g[:, 168:169])
             if k == BLK - 1:
                 ring = ring + (h[:, 144 + at : 145 + at] + g[:, 169:170])
-            mask = ref[TRI + 16 : TRI + 32, 160 + k : 161 + k]
+            mask = ref[TRI + 16 : TRI + 32, spot : spot + 1]
             return mask, mask * (ring + answer[s : s + 1])
 
-        o_w, z_w = edge(g_w, h_w, from_w_ref, 15, answer_w)
-        o_e, z_e = edge(g_e, h_e, from_e_ref, 0, answer_e)
+        o_w, z_w = edge(g_w, from_w_ref, 15, RING[1][k], answer_w)
+        o_e, z_e = edge(g_e, from_e_ref, 0, RING[0][k], answer_e)
         z_pad[rows, :] = jnp.where(wide_lane == 15, z_w, jnp.where(wide_lane == 240, z_e, z))
         o_pad[rows, :] = jnp.where(wide_lane == 15, o_w, jnp.where(wide_lane == 240, o_e, ocean))
 
@@ -281,8 +294,8 @@
         return pltpu.roll(x, 1, 1) + pltpu.roll(x, EXT - 1, 1)
 
     def line(index, inside):
-        face = jnp.concatenate([got_ref[index, n_row : n_row + 1, :], got_ref[index, n_row + 1 : n_row + 2, :]], axis=1)
-        return jnp.where(inside, face, 0.0)
+        face = jnp.concatenate([got_ref[index, 0:1, :], got_ref[index, 1:2, :]], axis=1)
+        return jnp.where(inside & (iota((1, EXT), 1) >= HW), face, 0.0)
 
     o_north = line(jnp.maximum(me - 1, 0), me > 0)
     o_south = line(jnp.minimum(me + 1, n_lat - 1), me < n_lat - 1)
@@ -301,11 +314,10 @@
     small = iota((1, 128), 1)
     scalars = jnp.where(small == 0, affinity, jnp.where(small == 1, energy, 0.0))
     for p in range(n_lat):
-        send_ref[p, 0:1, :] = z[0:1, 0:128]
+        send_ref[p, 0:1, :] = jnp.where(small < 2, scalars, z[0:1, 0:128])
         send_ref[p, 1:2, :] = z[0:1, 128:256]
         send_ref[p, 2:3, :] = z[ROWS - 1 : ROWS, 0:128]
         send_ref[p, 3:4, :] = z[ROWS - 1 : ROWS, 128:256]
-        send_ref[p, 4:5, :] = scalars
 
 
 def cross_kernel(n_lat, n_lon, got_ref, send_ref):
@@ -314,7 +326,7 @@
         cross = cross + got_ref[i, 2:4, :] * got_ref[i + 1, 0:2, :]
     cross = jnp.sum(jnp.sum(cross, axis=0, keepdims=True), axis=1, keepdims=True)
     small = iota((1, 128), 1)
-    total = jnp.sum(got_ref[:, 4:5, :], axis=0) - jnp.where(small == 1, 2.0 * cross, 0.0)
+    total = jnp.where(small < 2, jnp.sum(got_ref[:, 0:1, :], axis=0), 0.0) - jnp.where(small == 1, 2.0 * cross, 0.0)
     for p in range(n_lon):
         send_ref[p] = total
 
@@ -366,7 +378,7 @@
     more = 32 + 4 * coarse_inverse.shape[1] // EXT
     to_s, to_n, diag, rhs, ocean, send, extra = call(
         k(first_kernel, n_lat),
-        [slab, slab, tile, tile, tile, (n_lat, n_row + 2, 128), (2, more, EXT)],
+        [slab, slab, tile, tile, tile, (n_lat, 2, 128), (2, more, EXT)],
         (
             intersection,
             *(
@@ -411,7 +423,7 @@
     coarse = lax.all_to_all(send, "lon", 0, 0, tiled=True)
     z, image, send = call(
         k(solve_kernel, n_lat, n_lon, n_row),
-        [tile, tile, (n_lat, 5, 128)],
+        [tile, tile, (n_lat, 4, 128)],
         (factors, rhs, ocean, diag, to_w, to_e, from_w, from_e, from_n, from_s, coarse_inverse, got, coarse),
         scratch=[pltpu.VMEM(tile, F32), pltpu.VMEM(tile, F32), pltpu.VMEM(tile, F32)],
     )

time: 84 us -> 83.2 us (level)
  no operation moved by 1% of the time
where the time goes in v6:
time: 83.2 us; the launch traced here: 83 us
  blocking collectives  66.5 us (80%)
  starting transfers between devices  9.46 us (11%)
  Pallas kernels  5.52 us (7%)
  between operations  1.49 us (2%)
    all_to_all x1, blocking collectives, body(): coarse = lax.all_to_all(send, 'lon', 0, 0, tiled=True)  26.3 us
    all_to_all x1, blocking collectives, body(): sums = lax.all_to_all(send, 'lon', 0, 0, tiled=True)  17.1 us
    all_to_all x1, blocking collectives, body(): got = lax.all_to_all(send, 'lat', 0, 0, tiled=True)  13.9 us
    all_to_all x1, blocking collectives, body(): edges = lax.all_to_all(send, 'lat', 0, 0, tiled=True)  9.18 us
    pallas_call x5, Pallas kernels, call(): pl.pallas_call(kernel, out_shape=[jax.ShapeDtypeStruct(s, F32) for s in o...  5.52 us
    ppermute x1, starting transfers between devices, body(): from_n = lax.ppermute(to_s, 'lat', line)  3.95 us
    ppermute x1, starting transfers between devices, body(): from_e = lax.ppermute(to_w, 'lon', back)  2.68 us
  transfers between devices with their start and end apart: 4, of which 0 were waited for; matrix products, arithmetic and copies ran while one was open for 0% of the time, Pallas kernels for 0%

profile of v6, /device:TPU:1, one launch (start us, length us, event | category | flops | bytes accessed | tf_op | source)
XLA Modules:
  0.0 83.0 jit_solution(16829810328446612478)
XLA Ops:
  0.6 0.0 copy-start
  1.4 0.0 copy-start.1
  1.4 2.5 %shard_map.94 = (f32[192,256]{1,0:T(8,128)S(1)}, f32[192,256]{1,0:T(8,128)S(1)}, f32[128,256]{1,0:T(8,128)S(1)}, f32[128,256]{1,0:T(8,128)S(1)}, f32[128,256]{1,...) custom-call(s32[1,1]{1,0:T(1,128)S(6)} %copy.10.refs_0_, f32[10,16,16,256]{3,2,1,0:T(8,128)} %refs_0_.3, ...), custom_call_target="tpu_custom_call" | custom-call | flops 100000 | bytes 3284996 | tf_op jit(solution)/shard_map/pallas_call | solution.py:30
  3.9 3.9 %collective-permute-start = (f32[192,256]{1,0:T(8,128)S(1)}, f32[192,256]{1,0:T(8,128)S(1)}, u32[]{:S(2)}, u32[]{:S(2)}) collective-permute-start(f32[192,256]{1,0:T(8,128)S(1)} %get-tuple-element.22), channel_id=1, source_target_pairs={{0,1},{1,2},{2,3},{3,4},{4,5},{5,6},{6,7},{7,8},{8,9},{9,10},{10,1... | collective-permute-start | bytes 589832 | tf_op jit(solution)/shard_map/ppermute | solution.py:411
  7.9 1.3 %collective-permute-start.1 = (f32[192,256]{1,0:T(8,128)S(1)}, f32[192,256]{1,0:T(8,128)S(1)}, u32[]{:S(2)}, u32[]{:S(2)}) collective-permute-start(f32[192,256]{1,0:T(8,128)S(1)} %get-tuple-element.23), channel_id=1, source_target_pairs={{1,0},{2,1},{3,2},{4,3},{5,4},{6,5},{7,6},{8,7},{9,8},{10,9},{11,1... | collective-permute-start | bytes 589832 | tf_op jit(solution)/shard_map/ppermute | solution.py:412
  9.2 13.9 %all_to_all.20.refs_5_.refs_11_ = f32[16,2,128]{2,1,0:T(2,128)S(1)} all-to-all(f32[16,2,128]{2,1,0:T(2,128)S(1)} %get-tuple-element.25), channel_id=1, replica_groups=mesh['lon'=32,'lat'=16] {'lat'}, dimensions={0} | all-to-all | bytes 32768 | tf_op jit(solution)/shard_map/all_to_all | solution.py:413
  23.0 0.0 collective-permute-done.refs_2_.refs_8_
  23.0 0.0 collective-permute-done.1.refs_3_.refs_9_
  23.0 0.0 copy-done
  23.1 0.8 shard_map.95
  23.8 2.7 %collective-permute-start.3 = (f32[352,256]{1,0:T(8,128)S(1)}, f32[352,256]{1,0:T(8,128)S(1)}, u32[]{:S(2)}, u32[]{:S(2)}) collective-permute-start(f32[352,256]{1,0:T(8,128)S(1)} %get-tuple-element.26.refs_4_), channel_id=1, source_target_pairs={{16,0},{32,16},{48,32},{64,48},{80,64},{96,80},{112,96},{128,112},... | collective-permute-start | bytes 1081352 | tf_op jit(solution)/shard_map/ppermute | solution.py:422
  26.5 1.5 %collective-permute-start.2 = (f32[352,256]{1,0:T(8,128)S(1)}, f32[352,256]{1,0:T(8,128)S(1)}, u32[]{:S(2)}, u32[]{:S(2)}) collective-permute-start(f32[352,256]{1,0:T(8,128)S(1)} %get-tuple-element.27.refs_5_), channel_id=1, source_target_pairs={{0,16},{16,32},{32,48},{48,64},{64,80},{80,96},{96,112},{112,128},... | collective-permute-start | bytes 1081352 | tf_op jit(solution)/shard_map/ppermute | solution.py:421
  28.1 26.3 %all_to_all.21.refs_12_ = f32[32,2,128]{2,1,0:T(2,128)S(1)} all-to-all(f32[32,2,128]{2,1,0:T(2,128)S(1)} %get-tuple-element.28), channel_id=1, replica_groups=mesh['lon'=32,'lat'=16] {'lon'}, dimensions={0} | all-to-all | bytes 65536 | tf_op jit(solution)/shard_map/all_to_all | solution.py:423
  54.4 0.0 collective-permute-done.3.refs_7_
  54.4 0.0 collective-permute-done.2.refs_6_
  54.4 0.0 copy-done.1
  54.4 1.2 %shard_map.96 = (f32[128,256]{1,0:T(8,128)S(1)}, f32[128,256]{1,0:T(8,128)S(1)}, f32[16,4,128]{2,1,0:T(4,128)S(1)}) custom-call(f32[10,16,16,256]{3,2,1,0:T(8,128)S(1)} %copy-done, f32[128,256]{1,0:T(8,128)S(1)} %get-tuple-element.19.refs_1_.refs_2_, f32[128,256]{1,0:T(8,128)S(1)} %get-tuple-element.20.refs_2_.refs_3_, ...), custom_call_target="tpu_custom_call" | custom-call | flops 100000 | bytes 5423104 | tf_op jit(solution)/shard_map/pallas_call | solution.py:30
  55.6 9.2 %all_to_all.22.refs_0_.refs_4_ = f32[16,4,128]{2,1,0:T(4,128)S(1)} all-to-all(f32[16,4,128]{2,1,0:T(4,128)S(1)} %get-tuple-element.31), channel_id=1, replica_groups=mesh['lon'=32,'lat'=16] {'lat'}, dimensions={0} | all-to-all | bytes 65536 | tf_op jit(solution)/shard_map/all_to_all | solution.py:430
  64.8 0.1 shard_map.97
  64.9 17.1 %all_to_all.23.refs_5_ = f32[32,1,128]{2,1,0:T(1,128)S(1)} all-to-all(f32[32,1,128]{2,1,0:T(1,128)S(1)} %shard_map.97), channel_id=1, replica_groups=mesh['lon'=32,'lat'=16] {'lon'}, dimensions={0} | all-to-all | bytes 32768 | tf_op jit(solution)/shard_map/all_to_all | solution.py:432
  82.0 0.9 %shard_map.98 = (f32[224,128]{1,0:T(8,128)}, f32[224,128]{1,0:T(8,128)}, f32[224,128]{1,0:T(8,128)}) custom-call(f32[128,256]{1,0:T(8,128)S(1)} %get-tuple-element.29.refs_0_, f32[128,256]{1,0:T(8,128)S(1)} %get-tuple-element.30.refs_1_, f32[128,256]{1,0:T(8,128)S(1)} %get-tuple-element.19.refs_1_.refs_2_, f32[128,256]{1,0:T(8,128)S(1)} %get-tuple-element.20.refs_2_.refs_3_, ...), custom_call_target="tpu_custom_call" | custom-call | flops 100000 | bytes 573440 | tf_op jit(solution)/shard_map/pallas_call | solution.py:30
Async XLA Ops:
  0.6 22.4 %copy-start = (f32[10,16,16,256]{3,2,1,0:T(8,128)S(1)}, f32[10,16,16,256]{3,2,1,0:T(8,128)}, u32[]{:S(2)}) copy-start(f32[10,16,16,256]{3,2,1,0:T(8,128)} %refs_0_.3) | copy-start | bytes 7864324
  1.4 52.9 %copy-start.1 = (f32[16,8192]{1,0:T(8,128)S(1)}, f32[16,8192]{1,0:T(8,128)}, u32[]{:S(2)}) copy-start(f32[16,8192]{1,0:T(8,128)} %refs_10_.1) | copy-start | bytes 1572868
  3.9 19.1 %collective-permute-start = (f32[192,256]{1,0:T(8,128)S(1)}, f32[192,256]{1,0:T(8,128)S(1)}, u32[]{:S(2)}, u32[]{:S(2)}) collective-permute-start(f32[192,256]{1,0:T(8,128)S(1)} %get-tuple-element.22), channel_id=1, source_target_pairs={{0,1},{1,2},{2,3},{3,4},{4,5},{5,6},{6,7},{7,8},{8,9},{9,10},{10,1... | collective-permute-start | bytes 589832 | tf_op jit(solution)/shard_map/ppermute | solution.py:411
  7.9 15.2 %collective-permute-start.1 = (f32[192,256]{1,0:T(8,128)S(1)}, f32[192,256]{1,0:T(8,128)S(1)}, u32[]{:S(2)}, u32[]{:S(2)}) collective-permute-start(f32[192,256]{1,0:T(8,128)S(1)} %get-tuple-element.23), channel_id=1, source_target_pairs={{1,0},{2,1},{3,2},{4,3},{5,4},{6,5},{7,6},{8,7},{9,8},{10,9},{11,1... | collective-permute-start | bytes 589832 | tf_op jit(solution)/shard_map/ppermute | solution.py:412
  23.8 30.5 %collective-permute-start.3 = (f32[352,256]{1,0:T(8,128)S(1)}, f32[352,256]{1,0:T(8,128)S(1)}, u32[]{:S(2)}, u32[]{:S(2)}) collective-permute-start(f32[352,256]{1,0:T(8,128)S(1)} %get-tuple-element.26.refs_4_), channel_id=1, source_target_pairs={{16,0},{32,16},{48,32},{64,48},{80,64},{96,80},{112,96},{128,112},... | collective-permute-start | bytes 1081352 | tf_op jit(solution)/shard_map/ppermute | solution.py:422
  26.5 27.9 %collective-permute-start.2 = (f32[352,256]{1,0:T(8,128)S(1)}, f32[352,256]{1,0:T(8,128)S(1)}, u32[]{:S(2)}, u32[]{:S(2)}) collective-permute-start(f32[352,256]{1,0:T(8,128)S(1)} %get-tuple-element.27.refs_5_), channel_id=1, source_target_pairs={{0,16},{16,32},{32,48},{48,64},{64,80},{80,96},{96,112},{112,128},... | collective-permute-start | bytes 1081352 | tf_op jit(solution)/shard_map/ppermute | solution.py:421

commit v7 on v6

--- a/solution.py
+++ b/solution.py
@@ -25,13 +25,13 @@
     return lax.broadcasted_iota(jnp.int32, shape, dim)
 
 
-def call(kernel, outs, ins, scratch=(), flops=100000, limit=16384, places=None):
+def call(kernel, outs, ins, scratch=(), flops=100000, limit=16384, places=None, out=VM):
     size = sum(4 * x.size for x in ins)
     return pl.pallas_call(
         kernel,
         out_shape=[jax.ShapeDtypeStruct(s, F32) for s in outs],
         in_specs=[PLACES[p] for p in places or "v" * len(ins)],
-        out_specs=[VM] * len(outs),
+        out_specs=[out] * len(outs),
         scratch_shapes=list(scratch),
         cost_estimate=pl.CostEstimate(flops=flops, bytes_accessed=size, transcendentals=0),
         compiler_params=pltpu.CompilerParams(vmem_limit_bytes=limit << 10),
@@ -331,10 +331,18 @@
         send_ref[p] = total
 
 
-def final_kernel(n_lat, z_ref, image_ref, rhs_ref, ocean_ref, got_ref, sums_ref, sol_ref, res_ref, pre_ref):
+def final_kernel(n_lat, z_ref, image_ref, rhs_ref, ocean_ref, got_ref, sums_ref, sol_hbm, res_hbm, pre_hbm, sol_ref, res_ref,
+                 pre_ref, sems):
+    def store(n, ref, hbm, x):
+        ref[...] = jnp.transpose(x)[HW : HW + COLS, :]
+        copy = pltpu.make_async_copy(ref, hbm, sems.at[n])
+        copy.start()
+        return copy
+
     me = lax.axis_index("lat")
     row = iota((ROWS, EXT), 0)
     z = z_ref[...]
+    copies = [store(0, pre_ref, pre_hbm, z)]
     sums = jnp.sum(sums_ref[...], axis=0)
     small = iota((1, 128), 1)
     affinity = jnp.sum(jnp.where(small == 0, sums, 0.0), axis=1, keepdims=True)
@@ -350,12 +358,10 @@
     edge = jnp.where(row == 0, z_north, jnp.where(row == ROWS - 1, z_south, 0.0))
     image = image_ref[...] - ocean_ref[...] * edge
 
-    def store(ref, x):
-        ref[...] = jnp.transpose(x)[HW : HW + COLS, :]
-
-    store(pre_ref, z)
-    store(sol_ref, alpha * z)
-    store(res_ref, rhs_ref[...] - alpha * image)
+    copies.append(store(1, sol_ref, sol_hbm, alpha * z))
+    copies.append(store(2, res_ref, res_hbm, rhs_ref[...] - alpha * image))
+    for copy in copies:
+        copy.wait()
 
 
 def body(land_sea, obs_cell, obs_value, obs_weight, intersection, factors, coarse_inverse):
@@ -431,9 +437,14 @@
     (send,) = call(k(cross_kernel, n_lat, n_lon), [(n_lon, 1, 128)], (edges,))
     sums = lax.all_to_all(send, "lon", 0, 0, tiled=True)
     out = (COLS, ROWS)
-    return tuple(
-        x.T for x in call(k(final_kernel, n_lat), [out, out, out], (z, image, rhs, ocean, edges, sums))
-    )
+    outs = call(
+        k(final_kernel, n_lat),
+        [out, out, out],
+        (z, image, rhs, ocean, edges, sums),
+        scratch=[pltpu.VMEM(out, F32)] * 3 + [pltpu.SemaphoreType.DMA((3,))],
+        out=PLACES["h"],
+    )
+    return tuple(x.T for x in outs)
 
 
 def solution(mesh):

time: 83.2 us -> 83.2 us (level)
  no operation moved by 1% of the time
where the time goes in v7:
time: 83.2 us; the launch traced here: 82.9 us
  blocking collectives  66.5 us (80%)
  starting transfers between devices  9.46 us (11%)
  Pallas kernels  5.51 us (7%)
  between operations  1.49 us (2%)
    all_to_all x1, blocking collectives, body(): coarse = lax.all_to_all(send, 'lon', 0, 0, tiled=True)  26.3 us
    all_to_all x1, blocking collectives, body(): sums = lax.all_to_all(send, 'lon', 0, 0, tiled=True)  17.1 us
    all_to_all x1, blocking collectives, body(): got = lax.all_to_all(send, 'lat', 0, 0, tiled=True)  13.9 us
    all_to_all x1, blocking collectives, body(): edges = lax.all_to_all(send, 'lat', 0, 0, tiled=True)  9.18 us
    pallas_call x5, Pallas kernels, call(): pl.pallas_call(kernel, out_shape=[jax.ShapeDtypeStruct(s, F32) for s in o...  5.51 us
    ppermute x1, starting transfers between devices, body(): from_n = lax.ppermute(to_s, 'lat', line)  3.95 us
    ppermute x1, starting transfers between devices, body(): from_e = lax.ppermute(to_w, 'lon', back)  2.68 us
  transfers between devices with their start and end apart: 4, of which 0 were waited for; matrix products, arithmetic and copies ran while one was open for 0% of the time, Pallas kernels for 0%

profile of v7, /device:TPU:1, one launch (start us, length us, event | category | flops | bytes accessed | tf_op | source)
XLA Modules:
  0.0 82.9 jit_solution(439914517263418786)
XLA Ops:
  0.6 0.0 copy-start
  1.4 0.0 copy-start.1
  1.4 2.5 %shard_map.94 = (f32[192,256]{1,0:T(8,128)S(1)}, f32[192,256]{1,0:T(8,128)S(1)}, f32[128,256]{1,0:T(8,128)S(1)}, f32[128,256]{1,0:T(8,128)S(1)}, f32[128,256]{1,...) custom-call(s32[1,1]{1,0:T(1,128)S(6)} %copy.10.refs_0_, f32[10,16,16,256]{3,2,1,0:T(8,128)} %refs_0_.3, ...), custom_call_target="tpu_custom_call" | custom-call | flops 100000 | bytes 3284996 | tf_op jit(solution)/shard_map/pallas_call | solution.py:30
  3.9 3.9 %collective-permute-start = (f32[192,256]{1,0:T(8,128)S(1)}, f32[192,256]{1,0:T(8,128)S(1)}, u32[]{:S(2)}, u32[]{:S(2)}) collective-permute-start(f32[192,256]{1,0:T(8,128)S(1)} %get-tuple-element.22), channel_id=1, source_target_pairs={{0,1},{1,2},{2,3},{3,4},{4,5},{5,6},{6,7},{7,8},{8,9},{9,10},{10,1... | collective-permute-start | bytes 589832 | tf_op jit(solution)/shard_map/ppermute | solution.py:417
  7.9 1.3 %collective-permute-start.1 = (f32[192,256]{1,0:T(8,128)S(1)}, f32[192,256]{1,0:T(8,128)S(1)}, u32[]{:S(2)}, u32[]{:S(2)}) collective-permute-start(f32[192,256]{1,0:T(8,128)S(1)} %get-tuple-element.23), channel_id=1, source_target_pairs={{1,0},{2,1},{3,2},{4,3},{5,4},{6,5},{7,6},{8,7},{9,8},{10,9},{11,1... | collective-permute-start | bytes 589832 | tf_op jit(solution)/shard_map/ppermute | solution.py:418
  9.2 13.9 %all_to_all.20.refs_5_.refs_11_ = f32[16,2,128]{2,1,0:T(2,128)S(1)} all-to-all(f32[16,2,128]{2,1,0:T(2,128)S(1)} %get-tuple-element.25), channel_id=1, replica_groups=mesh['lon'=32,'lat'=16] {'lat'}, dimensions={0} | all-to-all | bytes 32768 | tf_op jit(solution)/shard_map/all_to_all | solution.py:419
  23.0 0.0 collective-permute-done.refs_2_.refs_8_
  23.0 0.0 collective-permute-done.1.refs_3_.refs_9_
  23.0 0.0 copy-done
  23.1 0.8 shard_map.95
  23.8 2.7 %collective-permute-start.3 = (f32[352,256]{1,0:T(8,128)S(1)}, f32[352,256]{1,0:T(8,128)S(1)}, u32[]{:S(2)}, u32[]{:S(2)}) collective-permute-start(f32[352,256]{1,0:T(8,128)S(1)} %get-tuple-element.26.refs_4_), channel_id=1, source_target_pairs={{16,0},{32,16},{48,32},{64,48},{80,64},{96,80},{112,96},{128,112},... | collective-permute-start | bytes 1081352 | tf_op jit(solution)/shard_map/ppermute | solution.py:428
  26.5 1.5 %collective-permute-start.2 = (f32[352,256]{1,0:T(8,128)S(1)}, f32[352,256]{1,0:T(8,128)S(1)}, u32[]{:S(2)}, u32[]{:S(2)}) collective-permute-start(f32[352,256]{1,0:T(8,128)S(1)} %get-tuple-element.27.refs_5_), channel_id=1, source_target_pairs={{0,16},{16,32},{32,48},{48,64},{64,80},{80,96},{96,112},{112,128},... | collective-permute-start | bytes 1081352 | tf_op jit(solution)/shard_map/ppermute | solution.py:427
  28.1 26.3 %all_to_all.21.refs_12_ = f32[32,2,128]{2,1,0:T(2,128)S(1)} all-to-all(f32[32,2,128]{2,1,0:T(2,128)S(1)} %get-tuple-element.28), channel_id=1, replica_groups=mesh['lon'=32,'lat'=16] {'lon'}, dimensions={0} | all-to-all | bytes 65536 | tf_op jit(solution)/shard_map/all_to_all | solution.py:429
  54.4 0.0 collective-permute-done.3.refs_7_
  54.4 0.0 collective-permute-done.2.refs_6_
  54.4 0.0 copy-done.1
  54.4 1.2 %shard_map.96 = (f32[128,256]{1,0:T(8,128)S(1)}, f32[128,256]{1,0:T(8,128)S(1)}, f32[16,4,128]{2,1,0:T(4,128)S(1)}) custom-call(f32[10,16,16,256]{3,2,1,0:T(8,128)S(1)} %copy-done, f32[128,256]{1,0:T(8,128)S(1)} %get-tuple-element.19.refs_1_.refs_2_, f32[128,256]{1,0:T(8,128)S(1)} %get-tuple-element.20.refs_2_.refs_3_, ...), custom_call_target="tpu_custom_call" | custom-call | flops 100000 | bytes 5423104 | tf_op jit(solution)/shard_map/pallas_call | solution.py:30
  55.6 9.2 %all_to_all.22.refs_0_.refs_4_ = f32[16,4,128]{2,1,0:T(4,128)S(1)} all-to-all(f32[16,4,128]{2,1,0:T(4,128)S(1)} %get-tuple-element.31), channel_id=1, replica_groups=mesh['lon'=32,'lat'=16] {'lat'}, dimensions={0} | all-to-all | bytes 65536 | tf_op jit(solution)/shard_map/all_to_all | solution.py:436
  64.8 0.1 shard_map.97
  64.9 17.1 %all_to_all.23.refs_5_ = f32[32,1,128]{2,1,0:T(1,128)S(1)} all-to-all(f32[32,1,128]{2,1,0:T(1,128)S(1)} %shard_map.97), channel_id=1, replica_groups=mesh['lon'=32,'lat'=16] {'lon'}, dimensions={0} | all-to-all | bytes 32768 | tf_op jit(solution)/shard_map/all_to_all | solution.py:438
  82.0 0.9 %shard_map.98 = (f32[224,128]{1,0:T(8,128)}, f32[224,128]{1,0:T(8,128)}, f32[224,128]{1,0:T(8,128)}) custom-call(f32[128,256]{1,0:T(8,128)S(1)} %get-tuple-element.29.refs_0_, f32[128,256]{1,0:T(8,128)S(1)} %get-tuple-element.30.refs_1_, f32[128,256]{1,0:T(8,128)S(1)} %get-tuple-element.19.refs_1_.refs_2_, f32[128,256]{1,0:T(8,128)S(1)} %get-tuple-element.20.refs_2_.refs_3_, ...), custom_call_target="tpu_custom_call" | custom-call | flops 100000 | bytes 573440 | tf_op jit(solution)/shard_map/pallas_call | solution.py:30
Async XLA Ops:
  0.6 22.4 %copy-start = (f32[10,16,16,256]{3,2,1,0:T(8,128)S(1)}, f32[10,16,16,256]{3,2,1,0:T(8,128)}, u32[]{:S(2)}) copy-start(f32[10,16,16,256]{3,2,1,0:T(8,128)} %refs_0_.3) | copy-start | bytes 7864324
  1.4 52.9 %copy-start.1 = (f32[16,8192]{1,0:T(8,128)S(1)}, f32[16,8192]{1,0:T(8,128)}, u32[]{:S(2)}) copy-start(f32[16,8192]{1,0:T(8,128)} %refs_10_.1) | copy-start | bytes 1572868
  3.9 19.1 %collective-permute-start = (f32[192,256]{1,0:T(8,128)S(1)}, f32[192,256]{1,0:T(8,128)S(1)}, u32[]{:S(2)}, u32[]{:S(2)}) collective-permute-start(f32[192,256]{1,0:T(8,128)S(1)} %get-tuple-element.22), channel_id=1, source_target_pairs={{0,1},{1,2},{2,3},{3,4},{4,5},{5,6},{6,7},{7,8},{8,9},{9,10},{10,1... | collective-permute-start | bytes 589832 | tf_op jit(solution)/shard_map/ppermute | solution.py:417
  7.9 15.2 %collective-permute-start.1 = (f32[192,256]{1,0:T(8,128)S(1)}, f32[192,256]{1,0:T(8,128)S(1)}, u32[]{:S(2)}, u32[]{:S(2)}) collective-permute-start(f32[192,256]{1,0:T(8,128)S(1)} %get-tuple-element.23), channel_id=1, source_target_pairs={{1,0},{2,1},{3,2},{4,3},{5,4},{6,5},{7,6},{8,7},{9,8},{10,9},{11,1... | collective-permute-start | bytes 589832 | tf_op jit(solution)/shard_map/ppermute | solution.py:418
  23.8 30.5 %collective-permute-start.3 = (f32[352,256]{1,0:T(8,128)S(1)}, f32[352,256]{1,0:T(8,128)S(1)}, u32[]{:S(2)}, u32[]{:S(2)}) collective-permute-start(f32[352,256]{1,0:T(8,128)S(1)} %get-tuple-element.26.refs_4_), channel_id=1, source_target_pairs={{16,0},{32,16},{48,32},{64,48},{80,64},{96,80},{112,96},{128,112},... | collective-permute-start | bytes 1081352 | tf_op jit(solution)/shard_map/ppermute | solution.py:428
  26.5 27.9 %collective-permute-start.2 = (f32[352,256]{1,0:T(8,128)S(1)}, f32[352,256]{1,0:T(8,128)S(1)}, u32[]{:S(2)}, u32[]{:S(2)}) collective-permute-start(f32[352,256]{1,0:T(8,128)S(1)} %get-tuple-element.27.refs_5_), channel_id=1, source_target_pairs={{0,16},{16,32},{32,48},{48,64},{64,80},{80,96},{96,112},{112,128},... | collective-permute-start | bytes 1081352 | tf_op jit(solution)/shard_map/ppermute | solution.py:427
